TPU v7x, 1024 devices: a whole 4x8x16 slice. The times are simulated.
1024 devices in a mesh: gx: 64 (over z, y_hi, core), gy: 16 (over x, y_lo).
Axes of the slice: x: 4, y: 8 (y_hi: 2, y_lo: 4; y = y_hi * 4 + y_lo), z: 16, core: 2. Of those that a mesh axis runs over, the one named last changes fastest.
Arguments:
- orbitals: bfloat16 [351232, 512], P(('gx', 'gy')), may hold values from -24 to 24
- potential: float32 [351232], P(('gx', 'gy')), may hold values from 0.5 to 2
- cell_stiffness: bfloat16 [512, 512], replicated, may hold values from -1 to 2.5, as said below
Outputs:
- filtered: bfloat16 [351232, 512], P(('gx', 'gy'))
- projected_ham: float32 [512, 512], P('gx', 'gy')
- correlation: float32 [512, 512], P('gx', 'gy')
Inputs may be any that keep to these rules, and one draw needn't show every extreme that they name: `cell_stiffness`: symmetric.
All inputs are finite; a program needn't handle non-finite values.
Results may differ from a plain program's by a relative error of at most 0.005.
Values may be sent and summed in bfloat16 or wider, within the bound.
No kernel may reach another device: no remote copies, remote signals or barrier semaphores. Data moves between devices by JAX's collectives and lax.ppermute only.
A program may use at most 32 MiB of HBM per device.

v0:
```python
import math

import jax
import jax.numpy as jnp
from jax import lax
from jax.sharding import PartitionSpec as P

DEG = 7


SPECTRUM_CENTER = 2.0
SPECTRUM_HALF = 2.0


def passed_along(value, axis, by):
    length = lax.axis_size(axis)
    pairs = [(i, i + by) for i in range(length) if 0 <= i + by < length]
    return lax.ppermute(value, axis, pairs)


def split_axis(values, which, degree):
    length = values.shape[which]
    cell_count = (length - 1) // degree
    leading = lax.slice_in_dim(values, 0, degree * cell_count, axis=which)
    leading = leading.reshape(
        values.shape[:which] + (cell_count, degree) + values.shape[which + 1 :]
    )
    trailing = lax.slice_in_dim(values, degree, length, stride=degree, axis=which)
    trailing = jnp.expand_dims(trailing, which + 1)
    joined = jnp.concatenate([leading, trailing], axis=which + 1)
    return jnp.swapaxes(joined, which, which + 1)


def join_axis(values, which, degree):
    values = jnp.swapaxes(values, which, which + 1)
    cell_count = values.shape[which]
    new_shape = values.shape[:which] + (cell_count * degree,) + values.shape[which + 2 :]
    leading = lax.slice_in_dim(values, 0, degree, axis=which + 1).reshape(new_shape)
    trailing = lax.slice_in_dim(values, degree, degree + 1, axis=which + 1)
    filler = jnp.zeros(
        trailing.shape[: which + 1] + (degree - 1,) + trailing.shape[which + 2 :], values.dtype
    )
    trailing = jnp.concatenate([filler, trailing], axis=which + 1).reshape(new_shape)
    widths_lead = [(0, 0)] * len(new_shape)
    widths_lead[which] = (0, 1)
    widths_trail = [(0, 0)] * len(new_shape)
    widths_trail[which] = (1, 0)
    return jnp.pad(leading, widths_lead) + jnp.pad(trailing, widths_trail)


def cell_image(node_slab, stiffness, degree):
    side = degree + 1
    cells = split_axis(node_slab, 1, degree)
    cells = split_axis(cells, 3, degree)
    cells = jnp.transpose(cells, (0, 1, 3, 2, 4, 5))
    cell_shape = cells.shape
    product = jnp.dot(stiffness, cells.reshape(side**3, -1), preferred_element_type=jnp.float32)
    product = jnp.transpose(product.reshape(cell_shape), (0, 1, 3, 2, 4, 5))
    product = join_axis(product, 3, degree)
    return join_axis(product, 1, degree)


def gram(left, right):
    return lax.dot_general(
        left, right, (((0,), (0,)), ((), ())), preferred_element_type=jnp.float32
    )


def image_of(field, potential_local, stiffness):
    plane_z = field.shape[2]
    upper_plane = passed_along(field[0:1], "gx", -1)
    extended = jnp.concatenate([field, upper_plane], axis=0)
    beside = passed_along(extended[:, 0:1], "gy", -1)
    extended = jnp.concatenate([extended, beside], axis=1)
    extended = jnp.pad(extended, ((0, 0), (0, 0), (0, 1), (0, 0)))
    contrib = cell_image(extended, stiffness, DEG)[:, :, :plane_z]
    from_lower_y = passed_along(contrib[:, DEG:], "gy", 1)
    contrib = jnp.concatenate([contrib[:, 0:1] + from_lower_y, contrib[:, 1:DEG]], axis=1)
    from_lower_x = passed_along(contrib[DEG:], "gx", 1)
    owned = jnp.concatenate([contrib[0:1] + from_lower_x, contrib[1:DEG]], axis=0)
    return owned + potential_local[..., None] * field.astype(jnp.float32)


def per_device(orbitals, potential, cell_stiffness):
    node_count = orbitals.shape[0]
    orbital_count = orbitals.shape[1]
    plane_z = node_count // (DEG * DEG)
    devices_x = lax.axis_size("gx")
    devices_y = lax.axis_size("gy")
    norm_scale = 1.0 / math.sqrt(node_count * devices_x * devices_y)
    field = orbitals.reshape(DEG, DEG, plane_z, orbital_count)
    potential_local = potential.reshape(DEG, DEG, plane_z)
    first_image = image_of(field, potential_local, cell_stiffness)
    lifted = ((first_image - SPECTRUM_CENTER * field.astype(jnp.float32)) / SPECTRUM_HALF).astype(
        jnp.bfloat16
    )
    second_image = image_of(lifted, potential_local, cell_stiffness)
    filtered = (
        2.0 * (second_image - SPECTRUM_CENTER * lifted.astype(jnp.float32)) / SPECTRUM_HALF
        - field.astype(jnp.float32)
    ).astype(jnp.bfloat16)
    image_rounded = second_image.astype(jnp.bfloat16)
    flat_filtered = filtered.reshape(node_count, orbital_count)
    ham_term = (
        gram(
            lifted.reshape(node_count, orbital_count),
            image_rounded.reshape(node_count, orbital_count),
        )
        * norm_scale
    )
    correlation_term = gram(flat_filtered, flat_filtered) * norm_scale
    block_rows = orbital_count // devices_x
    block_cols = orbital_count // devices_y
    ham_total, correlation_total = lax.psum((ham_term, correlation_term), ("gx", "gy"))
    row_start = lax.axis_index("gx") * block_rows
    col_start = lax.axis_index("gy") * block_cols
    projected_ham = lax.dynamic_slice(ham_total, (row_start, col_start), (block_rows, block_cols))
    correlation = lax.dynamic_slice(
        correlation_total, (row_start, col_start), (block_rows, block_cols)
    )
    return (flat_filtered, projected_ham, correlation)


def solution(mesh):
    placed = (P(("gx", "gy"), None), P(("gx", "gy")), P())
    return jax.shard_map(
        per_device,
        mesh=mesh,
        in_specs=placed,
        out_specs=(P(("gx", "gy"), None), P("gx", "gy"), P("gx", "gy")),
        check_vma=False,
    )
```

profile of v0, /device:TPU:1, one launch (start us, length us, event | category | flops | bytes accessed | tf_op | source)
XLA Modules:
  0.0 600.9 jit_solution(1293503230800011790)
XLA Ops:
  7.2 0.9 slice-done
  8.2 16.0 %collective-permute-start = (bf16[1,7,7,512]{3,2,1,0:T(8,128)(2,1)S(1)}, bf16[1,7,7,512]{3,2,1,0:T(8,128)(2,1)S(1)}, u32[]{:S(2)}, u32[]{:S(2)}) collective-permute-start(bf16[1,7,7,512]{3,2,1,0:T(8,128)(2,1)S(1)} %slice.112), channel_id=1, source_target_pairs={{16,0},{32,16},{48,32},{64,48},{80,64},{96,80},{112,96},{128,112},... | collective-permute-start | bytes 150536 | tf_op jit(solution)/shard_map/ppermute | solution.py:18
  24.2 1.1 reshape.81
  25.4 1.3 collective-permute-start.1
  26.7 5.6 collective-permute-done.1
  32.7 0.3 pad_maximum_fusion
  33.0 0.4 fusion.26
  33.6 0.3 slice_bitcast_fusion.1
  33.9 0.3 add_bitcast_fusion.1
  34.4 1.3 collective-permute-start.2
  35.9 1.8 collective-permute-done.2
  37.7 1.9 collective-permute-start.3
  39.8 1.8 collective-permute-done.3
  41.6 0.3 fusion.8
  41.9 2.1 collective-permute-start.4
  44.0 7.9 %collective-permute-done.4 = bf16[1,7,7,512]{3,2,1,0:T(8,128)(2,1)S(1)} collective-permute-done((bf16[1,7,7,512]{3,2,1,0:T(8,128)(2,1)S(1)}, bf16[1,7,7,512]{3,2,1,0:T(8,128)(2,1)S(1)}, u32[]{:S(2)}, u32[]{:S(2)}) %collective-permute-start.4) | collective-permute-done | bytes 50208 | tf_op jit(solution)/shard_map/ppermute | solution.py:18
  51.8 1.3 collective-permute-start.5
  53.1 5.4 collective-permute-done.5
  59.0 0.3 pad_maximum_fusion.1
  59.3 0.4 fusion.27
  60.2 0.3 add_bitcast_fusion
  60.6 3.4 collective-permute-start.6
  64.2 1.8 collective-permute-done.6
  66.0 5.2 collective-permute-start.7
  71.4 1.7 collective-permute-done.7
  73.2 0.9 copy-done.1
  74.1 0.3 fusion.17
  74.5 1.7 convolution_multiply_fusion.1
  76.2 1.5 convolution_multiply_fusion
  77.7 513.7 %all-reduce.17.cloned.1.call-done = (f32[512,512]{1,0:T(8,128)}, f32[512,512]{1,0:T(8,128)}) async-done(((f32[512,512]{1,0:T(8,128)}, f32[512,512]{1,0:T(8,128)}), (f32[512,512]{1,0:T(8,128)}, f32[512,512]{1,0:T(8,128)})) %all-reduce.17.cloned.1.call-update) | async-done | bytes 2097168 | tf_op jit(solution)/shard_map/psum | solution.py:114
  591.4 1.3 dynamic_slice.7
  592.7 1.3 dynamic_slice.6
  (53 shorter events, 2.8 us)
Async XLA Ops:
  7.2 25.9 %copy-start = (bf16[512,512]{1,0:T(8,128)(2,1)S(1)}, bf16[512,512]{1,0:T(8,128)(2,1)}, u32[]{:S(2)}) copy-start(bf16[512,512]{1,0:T(8,128)(2,1)} %param.5) | copy-start | bytes 1572868
  7.2 1.0 slice-start
  7.2 584.2 %all-reduce.17.cloned.1.call-start = ((), (), s32[]{:S(2)}) async-start(), calls=%async_computation | async-start | bytes 4194304 | tf_op jit(solution)/shard_map/psum | solution.py:114
  8.2 17.2 %collective-permute-start = (bf16[1,7,7,512]{3,2,1,0:T(8,128)(2,1)S(1)}, bf16[1,7,7,512]{3,2,1,0:T(8,128)(2,1)S(1)}, u32[]{:S(2)}, u32[]{:S(2)}) collective-permute-start(bf16[1,7,7,512]{3,2,1,0:T(8,128)(2,1)S(1)} %slice.112), channel_id=1, source_target_pairs={{16,0},{32,16},{48,32},{64,48},{80,64},{96,80},{112,96},{128,112},... | collective-permute-start | bytes 150536 | tf_op jit(solution)/shard_map/ppermute | solution.py:18
  25.4 6.9 %collective-permute-start.1 = (bf16[8,1,7,512]{3,2,1,0:T(8,128)(2,1)S(1)}, bf16[8,1,7,512]{3,2,1,0:T(8,128)(2,1)S(1)}, u32[]{:S(2)}, u32[]{:S(2)}) collective-permute-start(bf16[8,1,7,512]{3,2,1,0:T(8,128)(2,1)S(1)} %slice.144), channel_id=1, source_target_pairs={{1,0},{2,1},{3,2},{4,3},{5,4},{6,5},{7,6},{8,7},{9,8},{10,9},{11,1... | collective-permute-start | bytes 172040 | tf_op jit(solution)/shard_map/ppermute | solution.py:18
  34.4 3.2 collective-permute-start.2
  37.7 2.0 copy-start.3
  37.7 3.9 collective-permute-start.3
  41.9 9.9 %collective-permute-start.4 = (bf16[1,7,7,512]{3,2,1,0:T(8,128)(2,1)S(1)}, bf16[1,7,7,512]{3,2,1,0:T(8,128)(2,1)S(1)}, u32[]{:S(2)}, u32[]{:S(2)}) collective-permute-start(bf16[1,7,7,512]{3,2,1,0:T(8,128)(2,1)S(1)} %slice.153), channel_id=1, source_target_pairs={{16,0},{32,16},{48,32},{64,48},{80,64},{96,80},{112,96},{128,112},... | collective-permute-start | bytes 150536 | tf_op jit(solution)/shard_map/ppermute | solution.py:18
  51.8 6.7 %collective-permute-start.5 = (bf16[8,1,7,512]{3,2,1,0:T(8,128)(2,1)S(1)}, bf16[8,1,7,512]{3,2,1,0:T(8,128)(2,1)S(1)}, u32[]{:S(2)}, u32[]{:S(2)}) collective-permute-start(bf16[8,1,7,512]{3,2,1,0:T(8,128)(2,1)S(1)} %pad_maximum_fusion.4), channel_id=1, source_target_pairs={{1,0},{2,1},{3,2},{4,3},{5,4},{6,5},{7,6},{8,7},{9,8},{10,9},{11,1... | collective-permute-start | bytes 172040 | tf_op jit(solution)/shard_map/ppermute | solution.py:18
  60.6 5.3 collective-permute-start.6
  66.0 7.0 %collective-permute-start.7 = (f32[1,7,7,512]{3,2,1,0:T(8,128)S(1)}, f32[1,7,7,512]{3,2,1,0:T(8,128)S(1)}, u32[]{:S(2)}, u32[]{:S(2)}) collective-permute-start(f32[1,7,7,512]{3,2,1,0:T(8,128)S(1)} %pad_maximum_fusion.2), channel_id=1, source_target_pairs={{0,16},{16,32},{32,48},{48,64},{64,80},{80,96},{96,112},{112,128},... | collective-permute-start | bytes 301064 | tf_op jit(solution)/shard_map/ppermute | solution.py:18
  73.1 1.0 copy-start.1
  74.4 1.7 copy-start.2
Sparse Core Ops, SparseCore 0:
  77.8 513.5 all-reduce.16
where the time goes:
time: 601 us
  waiting for transfers between devices  540 us (90%)
  starting transfers between devices  32.5 us (5%)
  between operations  14.5 us (2%)
  local copies, waits for them, and re-layouts  7.62 us (1%)
    psum x1, waiting for transfers between devices, per_device(): lax.psum((ham_term, correlation_term), ('gx', 'gy'))  514 us
    ppermute x8, starting transfers between devices, passed_along(): return lax.ppermute(value, axis, pairs)  32.5 us
    ppermute x8, waiting for transfers between devices, passed_along(): return lax.ppermute(value, axis, pairs)  25.9 us
  transfers between devices with their start and end apart: 9, of which 8 were waited for; matrix products, arithmetic and copies ran while one was open for 0% of the time, Pallas kernels for 0%

commit v1 on v0

v1 whole, which is shorter than its diff:
```python
import math

import numpy as np

import jax
import jax.numpy as jnp
from jax import lax
from jax.experimental import pallas as pl
from jax.experimental.pallas import tpu as pltpu
from jax.sharding import Mesh, PartitionSpec as P

DEG = 7
SIDE = DEG + 1
FACE = DEG * DEG
RIM = FACE + DEG
OWN = FACE * DEG
CELL = OWN + 2 * FACE + DEG
VMEM_LIMIT = 24 * 2**20
SPECTRUM_CENTER = 2.0
SPECTRUM_HALF = 2.0
F32 = jnp.float32
BF16 = jnp.bfloat16


def node_lists():
    def at(a, b):
        return [(a * SIDE + b) * SIDE + c for c in range(DEG)]

    own = [n for a in range(DEG) for b in range(DEG) for n in at(a, b)]
    face_x = [n for b in range(DEG) for n in at(DEG, b)]
    face_y = [n for a in range(DEG) for n in at(a, DEG)]
    return own, face_x, face_y, at(DEG, DEG)


def dot(left, right):
    return jnp.dot(left, right, preferred_element_type=F32)


def gram(left, right):
    return lax.dot_general(left, right, (((0,), (0,)), ((), ())), preferred_element_type=F32)


def one_hot(column, width):
    return (column == lax.broadcasted_iota(jnp.int32, (column.shape[0], width), 1)).astype(F32).astype(BF16)


def call(kernel, *shapes, scratch=(), results=()):
    def run(*args):
        vmem = pl.BlockSpec(memory_space=pltpu.VMEM)
        return pl.pallas_call(
            kernel,
            out_shape=[
                jax.ShapeDtypeStruct(*shape) if i in results else pltpu.VMEM(*shape) for i, shape in enumerate(shapes)
            ],
            in_specs=[vmem] * len(args),
            out_specs=[vmem] * len(shapes),
            scratch_shapes=list(scratch),
            compiler_params=pltpu.CompilerParams(vmem_limit_bytes=VMEM_LIMIT),
            name=kernel.__name__,
        )(*[pltpu.with_memory_space_constraint(arg, pltpu.VMEM) for arg in args])

    return run


def take_face_y(source, packed):
    for i in range(DEG):
        packed[i * DEG : (i + 1) * DEG, :] = source[i * FACE : i * FACE + DEG, :]


def prepare_body(field, stiffness, rows, columns, order_out, face_y, partial, wide, packed):
    left = one_hot(rows[...], SIDE**3)
    right = one_hot(columns[...], SIDE**3)
    mixed = dot(left, stiffness[...]).astype(BF16)
    order_out[...] = lax.dot_general(mixed, right, (((1,), (1,)), ((), ())), preferred_element_type=F32).astype(BF16)
    wide[...] = field[...].astype(F32)
    take_face_y(wide, packed)
    face_y[...] = packed[...].astype(BF16)
    partial[...] = dot(order_out[:, :OWN], field[...])


def add_face_body(ordered, partial, face_x, total):
    total[...] = partial[...] + dot(ordered[:, OWN : OWN + FACE], face_x[...])


def close_body(ordered, partial, rim, own, away_x, face_y):
    total = partial[...] + dot(ordered[:, OWN + FACE :], rim[...])
    own[...] = total[:OWN]
    away_x[...] = total[OWN : OWN + RIM]
    face_y[...] = total[OWN + RIM :]


def lift_body(own, from_x, from_y, field, potential, lifted, face_x, face_y, image, packed):
    field32 = field[...].astype(F32)
    image[...] = own[...]
    image[:FACE, :] += from_x[:FACE, :]
    for i in range(DEG):
        image[i * FACE : i * FACE + DEG, :] += from_y[i * DEG : (i + 1) * DEG, :]
    first_image = image[...] + potential[...] * field32
    image[...] = (first_image - SPECTRUM_CENTER * field32) / SPECTRUM_HALF
    lifted[...] = image[...].astype(BF16)
    face_x[...] = image[:FACE, :].astype(BF16)
    take_face_y(image, packed)
    face_y[...] = packed[...].astype(BF16)


def multiply_body(ordered, lifted, partial):
    partial[...] = dot(ordered[:, :OWN], lifted[...])


def solution(mesh):
    length_x, length_y = mesh.shape["gx"], mesh.shape["gy"]
    length_z = length_x // 4
    split_mesh = Mesh(mesh.devices.reshape(length_z, 2, 2, length_y), ("z", "half", "core", "gy"))
    gx = ("z", "half", "core")
    every = gx + ("gy",)

    def passed_x(value, by):
        return lax.ppermute(value, gx, [(i, i + by) for i in range(length_x) if 0 <= i + by < length_x])

    def passed_y(value, by):
        return lax.ppermute(value, "gy", [(i, i + by) for i in range(length_y) if 0 <= i + by < length_y])

    def per_device(orbitals, potential, cell_stiffness):
        node_count, orbital_count = orbitals.shape
        norm_scale = 1.0 / math.sqrt(node_count * length_x * length_y)
        block_rows = orbital_count // length_x
        block_cols = orbital_count // length_y
        half = orbital_count // 2
        quarter = orbital_count // 4
        own, face_x, face_y, edge = node_lists()
        row_order = jnp.asarray(np.array(own + face_x + edge + face_y, np.int32)[:, None])
        column_order = jnp.asarray(np.array(own + face_x + face_y + edge, np.int32)[:, None])
        orbital_order = jnp.asarray(
            np.arange(orbital_count, dtype=np.int32)
            .reshape(length_z, 2, 2, block_rows)
            .transpose(2, 1, 0, 3)
            .reshape(-1, 1)
        )
        weight = potential[:, None]
        face = (FACE, orbital_count)
        cell = (CELL, orbital_count)
        nodes = (OWN, orbital_count)
        rim = (RIM, orbital_count)

        def closed(ordered, partial, above_x, own_face_y):
            total = call(add_face_body, (cell, F32))(ordered, partial, above_x)[0]
            above_y = passed_y(jnp.concatenate([own_face_y, above_x[:DEG]], axis=0), -1)
            return above_y, *call(close_body, (nodes, F32), (rim, F32), (face, F32))(ordered, total, above_y)

        def shared(away_x, away_y):
            from_x = passed_x(away_x, 1)
            from_y = passed_y(away_y + jnp.pad(from_x[FACE:], ((0, FACE - DEG), (0, 0))), 1)
            return from_x, from_y

        above_x = passed_x(orbitals[:FACE], -1)
        ordered, own_face_y, partial = call(
            prepare_body,
            ((CELL, CELL), BF16),
            (face, BF16),
            (cell, F32),
            scratch=(pltpu.VMEM(nodes, F32), pltpu.VMEM(face, F32)),
        )(orbitals, cell_stiffness, row_order, column_order)
        _, own_image, away_x, away_y = closed(ordered, partial, above_x, own_face_y)
        from_x, from_y = shared(away_x, away_y)
        lifted, lifted_face_x, lifted_face_y = call(
            lift_body,
            (nodes, BF16),
            (face, BF16),
            (face, BF16),
            scratch=(pltpu.VMEM(nodes, F32), pltpu.VMEM(face, F32)),
        )(own_image, from_x, from_y, orbitals, weight)

        above_x = passed_x(lifted_face_x, -1)
        partial = call(multiply_body, (cell, F32))(ordered, lifted)[0]
        above_y, own_image, away_x, away_y = closed(ordered, partial, above_x, lifted_face_y)
        from_x, from_y = shared(away_x, away_y)

        gram_shape = (2, orbital_count, half)
        padded = -(-CELL // 128) * 128

        def ham_body(own_image, away_x, away_y, lifted, above_x, above_y, potential, order, out, images, values):
            values[CELL:, :] = jnp.zeros((padded - CELL, orbital_count), F32)
            images[CELL:, :] = jnp.zeros((padded - CELL, orbital_count), F32)
            values[:OWN, :] = lifted[...].astype(F32)
            values[OWN : OWN + FACE, :] = above_x[...].astype(F32)
            values[OWN + FACE : CELL, :] = above_y[...].astype(F32)
            images[:OWN, :] = own_image[...] + potential[...] * values[:OWN, :]
            images[OWN : OWN + FACE, :] = away_x[:FACE, :]
            images[OWN + FACE : OWN + 2 * FACE, :] = away_y[...]
            images[OWN + 2 * FACE : CELL, :] = away_x[FACE:, :]
            shuffle = one_hot(order[...], orbital_count)
            shuffled = lax.dot_general(
                values[...].astype(BF16), shuffle, (((1,), (1,)), ((), ())), preferred_element_type=F32
            ).astype(BF16)
            product = (gram(images[...].astype(BF16), shuffled) * norm_scale).astype(BF16)
            out[0] = product[:, :half]
            out[1] = product[:, half:]

        ham_term = call(
            ham_body,
            (gram_shape, BF16),
            scratch=(pltpu.VMEM((padded, orbital_count), F32), pltpu.VMEM((padded, orbital_count), F32)),
        )(own_image, away_x, away_y, lifted, above_x, above_y, weight, orbital_order)[0]

        rows = -(-OWN // 128) * 128

        def filter_body(own_image, from_x, from_y, lifted, field, potential, order, ham, filtered, out, image):
            lifted32 = lifted[...].astype(F32)
            image[OWN:, :] = jnp.zeros((rows - OWN, orbital_count), F32)
            image[:OWN, :] = own_image[...]
            image[:FACE, :] += from_x[:FACE, :]
            for i in range(DEG):
                image[i * FACE : i * FACE + DEG, :] += from_y[i * DEG : (i + 1) * DEG, :]
            second_image = image[:OWN, :] + potential[...] * lifted32
            image[:OWN, :] = (
                2.0 * (second_image - SPECTRUM_CENTER * lifted32) / SPECTRUM_HALF - field[...].astype(F32)
            )
            values = image[...].astype(BF16)
            filtered[...] = image[:OWN, :].astype(BF16)
            shuffle = one_hot(order[...], orbital_count)
            shuffled = lax.dot_general(
                values, shuffle, (((1,), (1,)), ((), ())), preferred_element_type=F32
            ).astype(BF16)
            product = (gram(values, shuffled) * norm_scale).astype(BF16)
            for side in range(2):
                out[side, 0] = ham[side]
                out[side, 1] = product[:, side * half : (side + 1) * half]

        filtered, terms = call(
            filter_body,
            (nodes, BF16),
            ((2, 2, orbital_count, half), BF16),
            scratch=(pltpu.VMEM((rows, orbital_count), F32),),
            results=(0,),
        )(own_image, from_x, from_y, lifted, orbitals, weight, orbital_order, ham_term)

        def pair_body(terms, out):
            for which in range(2):
                total = (terms[0, which].astype(F32) + terms[1, which].astype(F32)).astype(BF16)
                for side in range(2):
                    part = total[:, side * quarter : (side + 1) * quarter]
                    for j in range(length_y):
                        out[side, j, which * block_cols : (which + 1) * block_cols] = part[
                            j * block_cols : (j + 1) * block_cols
                        ]

        def plane_body(terms, out):
            total = terms[0].astype(F32)
            for source in range(1, 2 * length_y):
                total += terms[source].astype(F32)
            out[...] = total.T

        def line_body(terms, ham, correlation):
            total = terms[0]
            for source in range(1, length_z):
                total += terms[source]
            ham[...] = total[:, :block_cols]
            correlation[...] = total[:, block_cols:]

        terms = lax.all_to_all(terms, "core", 0, 0, tiled=True)
        terms = call(pair_body, ((2, length_y, 2 * block_cols, quarter), BF16))(terms)[0]
        terms = terms.reshape(2 * length_y, 2 * block_cols, quarter)
        terms = lax.all_to_all(terms, ("half", "gy"), 0, 0, tiled=True)
        terms = call(plane_body, ((quarter, 2 * block_cols), F32))(terms)[0]
        terms = terms.reshape(length_z, block_rows, 2 * block_cols)
        terms = lax.all_to_all(terms, "z", 0, 0, tiled=True)
        block = (block_rows, block_cols)
        projected_ham, correlation = call(line_body, (block, F32), (block, F32), results=(0, 1))(terms)
        return filtered, projected_ham, correlation

    return jax.shard_map(
        per_device,
        mesh=split_mesh,
        in_specs=(P(every, None), P(every), P()),
        out_specs=(P(every, None), P(gx, "gy"), P(gx, "gy")),
        check_vma=False,
    )
```

time: 601 us -> 137 us (0.23)
  waiting for transfers between devices: 540 us -> 22.5 us
  blocking collectives: 0 us -> 68.2 us
  between operations: 14.5 us -> 0.85 us
  Pallas kernels: 0 us -> 6.08 us
    psum x1 -> x0, waiting for transfers between devices: 514 us -> none  [per_device(): lax.psum((ham_term, correlation_term), ('gx', 'gy'))]
    all_to_all x0 -> x3, blocking collectives: none -> 68.2 us  [the longest x1 32.6 us: per_device(): terms = lax.all_to_all(terms, 'z', 0, 0, tiled=True)]
    pallas_call x0 -> x12, Pallas kernels: none -> 6.08 us  [run(): pl.pallas_call(kernel, out_shape=[jax.ShapeDtypeStruct(*shape) if i in re...]
  transfers between devices with their start and end apart: 9 -> 8, of which waited for: 8 -> 7; matrix products, arithmetic and copies ran while one was open for 0% -> 0% of each run, Pallas kernels for 0% -> 2%
where the time goes in v1:
time: 137 us; the launch traced here: 136 us
  blocking collectives  68.2 us (50%)
  starting transfers between devices  31.8 us (23%)
  waiting for transfers between devices  22.5 us (16%)
  Pallas kernels  6.08 us (4%)
  local copies, waits for them, and re-layouts  5.54 us (4%)
    all_to_all x1, blocking collectives, per_device(): terms = lax.all_to_all(terms, 'z', 0, 0, tiled=True)  32.6 us
    all_to_all x1, blocking collectives, per_device(): terms = lax.all_to_all(terms, ('half', 'gy'), 0, 0, tiled=True)  31.5 us
    ppermute x4, starting transfers between devices, passed_x(): lax.ppermute(value, gx, [(i, i + by) for i in range(length_x) if 0 <= i +...  23.1 us
    ppermute x4, waiting for transfers between devices, passed_x(): lax.ppermute(value, gx, [(i, i + by) for i in range(length_x) if 0 <= i +...  12.6 us
    ppermute x4, waiting for transfers between devices, passed_y(): lax.ppermute(value, 'gy', [(i, i + by) for i in range(length_y) if 0 <= i...  9.91 us
    ppermute x4, starting transfers between devices, passed_y(): lax.ppermute(value, 'gy', [(i, i + by) for i in range(length_y) if 0 <= i...  8.74 us
    pallas_call x12, Pallas kernels, run(): pl.pallas_call(kernel, out_shape=[jax.ShapeDtypeStruct(*shape) if i in re...  6.08 us
    all_to_all x1, blocking collectives, per_device(): terms = lax.all_to_all(terms, 'core', 0, 0, tiled=True)  4.2 us
  transfers between devices with their start and end apart: 8, of which 7 were waited for; matrix products, arithmetic and copies ran while one was open for 0% of the time, Pallas kernels for 2%

profile of v1, /device:TPU:1, one launch (start us, length us, event | category | flops | bytes accessed | tf_op | source)
XLA Modules:
  0.0 135.8 jit_solution(14939367922471068343)
XLA Ops:
  0.6 0.8 slice.15
  1.5 16.0 %collective-permute-start = (bf16[49,512]{1,0:T(8,128)(2,1)S(1)}, bf16[49,512]{1,0:T(8,128)(2,1)S(1)}, u32[]{:S(2)}, u32[]{:S(2)}) collective-permute-start(bf16[49,512]{1,0:T(8,128)(2,1)S(1)} %slice.15), channel_id=1, source_target_pairs={{16,0},{32,16},{48,32},{64,48},{80,64},{96,80},{112,96},{128,112},... | collective-permute-start | bytes 150536 | tf_op jit(solution)/shard_map/ppermute | solution.py:118
  17.5 1.0 copy-done
  18.5 1.0 copy-done.3
  19.5 0.9 copy-done.4
  20.4 0.9 copy-done.5
  21.4 1.0 prepare_body.1
  22.4 1.3 collective-permute-start.1
  23.7 0.3 add_face_body.2.partial
  24.0 3.9 %collective-permute-done.1.rim = bf16[56,512]{1,0:T(8,128)(2,1)S(1)} collective-permute-done((bf16[56,512]{1,0:T(8,128)(2,1)S(1)}, bf16[56,512]{1,0:T(8,128)(2,1)S(1)}, u32[]{:S(2)}, u32[]{:S(2)}) %collective-permute-start.1) | collective-permute-done | bytes 57376 | tf_op jit(solution)/shard_map/ppermute | solution.py:121
  28.2 1.9 %collective-permute-start.2 = (f32[56,512]{1,0:T(8,128)S(1)}, f32[56,512]{1,0:T(8,128)S(1)}, u32[]{:S(2)}, u32[]{:S(2)}) collective-permute-start(f32[56,512]{1,0:T(8,128)S(1)} %get-tuple-element.23), channel_id=1, source_target_pairs={{0,16},{16,32},{32,48},{48,64},{64,80},{80,96},{96,112},{112,128},... | collective-permute-start | bytes 344072 | tf_op jit(solution)/shard_map/ppermute | solution.py:118
  30.2 1.8 %collective-permute-done.2.from_x = f32[56,512]{1,0:T(8,128)S(1)} collective-permute-done((f32[56,512]{1,0:T(8,128)S(1)}, f32[56,512]{1,0:T(8,128)S(1)}, u32[]{:S(2)}, u32[]{:S(2)}) %collective-permute-start.2) | collective-permute-done | bytes 114720 | tf_op jit(solution)/shard_map/ppermute | solution.py:118
  32.0 2.6 %collective-permute-start.3 = (f32[49,512]{1,0:T(8,128)S(1)}, f32[49,512]{1,0:T(8,128)S(1)}, u32[]{:S(2)}, u32[]{:S(2)}) collective-permute-start(f32[49,512]{1,0:T(8,128)S(1)} %pad_add_fusion.1), channel_id=1, source_target_pairs={{0,1},{1,2},{2,3},{3,4},{4,5},{5,6},{6,7},{7,8},{8,9},{9,10},{10,1... | collective-permute-start | bytes 301064 | tf_op jit(solution)/shard_map/ppermute | solution.py:121
  34.7 1.8 %collective-permute-done.3.from_y = f32[49,512]{1,0:T(8,128)S(1)} collective-permute-done((f32[49,512]{1,0:T(8,128)S(1)}, f32[49,512]{1,0:T(8,128)S(1)}, u32[]{:S(2)}, u32[]{:S(2)}) %collective-permute-start.3) | collective-permute-done | bytes 100384 | tf_op jit(solution)/shard_map/ppermute | solution.py:121
  36.7 1.9 %collective-permute-start.4 = (bf16[49,512]{1,0:T(8,128)(2,1)S(1)}, bf16[49,512]{1,0:T(8,128)(2,1)S(1)}, u32[]{:S(2)}, u32[]{:S(2)}) collective-permute-start(bf16[49,512]{1,0:T(8,128)(2,1)S(1)} %get-tuple-element.26), channel_id=1, source_target_pairs={{16,0},{32,16},{48,32},{64,48},{80,64},{96,80},{112,96},{128,112},... | collective-permute-start | bytes 150536 | tf_op jit(solution)/shard_map/ppermute | solution.py:118
  38.7 9.1 %collective-permute-done.4.face_x.above_x = bf16[49,512]{1,0:T(8,128)(2,1)S(1)} collective-permute-done((bf16[49,512]{1,0:T(8,128)(2,1)S(1)}, bf16[49,512]{1,0:T(8,128)(2,1)S(1)}, u32[]{:S(2)}, u32[]{:S(2)}) %collective-permute-start.4) | collective-permute-done | bytes 50208 | tf_op jit(solution)/shard_map/ppermute | solution.py:118
  47.7 1.3 collective-permute-start.5
  49.0 0.4 multiply_body.1.partial
  49.4 0.3 add_face_body.3.partial
  49.8 3.5 %collective-permute-done.5.rim.above_y = bf16[56,512]{1,0:T(8,128)(2,1)S(1)} collective-permute-done((bf16[56,512]{1,0:T(8,128)(2,1)S(1)}, bf16[56,512]{1,0:T(8,128)(2,1)S(1)}, u32[]{:S(2)}, u32[]{:S(2)}) %collective-permute-start.5) | collective-permute-done | bytes 57376 | tf_op jit(solution)/shard_map/ppermute | solution.py:121
  53.6 3.2 %collective-permute-start.6 = (f32[56,512]{1,0:T(8,128)S(1)}, f32[56,512]{1,0:T(8,128)S(1)}, u32[]{:S(2)}, u32[]{:S(2)}) collective-permute-start(f32[56,512]{1,0:T(8,128)S(1)} %get-tuple-element.29.away_x), channel_id=1, source_target_pairs={{0,16},{16,32},{32,48},{48,64},{64,80},{80,96},{96,112},{112,128},... | collective-permute-start | bytes 344072 | tf_op jit(solution)/shard_map/ppermute | solution.py:118
  56.8 1.8 %collective-permute-done.6.from_x = f32[56,512]{1,0:T(8,128)S(1)} collective-permute-done((f32[56,512]{1,0:T(8,128)S(1)}, f32[56,512]{1,0:T(8,128)S(1)}, u32[]{:S(2)}, u32[]{:S(2)}) %collective-permute-start.6) | collective-permute-done | bytes 114720 | tf_op jit(solution)/shard_map/ppermute | solution.py:118
  58.6 3.6 %collective-permute-start.7 = (f32[49,512]{1,0:T(8,128)S(1)}, f32[49,512]{1,0:T(8,128)S(1)}, u32[]{:S(2)}, u32[]{:S(2)}) collective-permute-start(f32[49,512]{1,0:T(8,128)S(1)} %pad_add_fusion), channel_id=1, source_target_pairs={{0,1},{1,2},{2,3},{3,4},{4,5},{5,6},{6,7},{7,8},{8,9},{9,10},{10,1... | collective-permute-start | bytes 301064 | tf_op jit(solution)/shard_map/ppermute | solution.py:121
  62.2 1.0 ham_body.1.ham
  63.2 0.8 collective-permute-done.7.from_y
  63.9 1.2 filter_body.1
  65.2 4.2 %all_to_all.15.terms = bf16[2,2,512,256]{3,2,1,0:T(8,128)(2,1)S(1)} all-to-all(bf16[2,2,512,256]{3,2,1,0:T(8,128)(2,1)S(1)} %get-tuple-element.32), channel_id=1, replica_groups=mesh['z'=16,'half'=2,'core'=2,'gy'=16] {'core'}, dimensions={0} | all-to-all | bytes 2097152 | tf_op jit(solution)/shard_map/all_to_all | solution.py:260
  69.5 31.5 %all_to_all.16.terms = bf16[32,64,128]{2,1,0:T(8,128)(2,1)S(1)} all-to-all(bf16[32,64,128]{2,1,0:T(8,128)(2,1)S(1)} %bitcast.2), channel_id=1, replica_groups=mesh['z'=16,'half'=2,'core'=2,'gy'=16] {'half','gy'}, dimensions={0} | all-to-all | bytes 1048576 | tf_op jit(solution)/shard_map/all_to_all | solution.py:263
  101.2 32.6 %all_to_all.17 = f32[16,1,512]{2,1,0:T(1,128)S(1)} all-to-all(f32[16,1,512]{2,1,0:T(1,128)S(1)} %reshape.14), channel_id=1, replica_groups=mesh['z'=16,'half'=2,'core'=2,'gy'=16] {'z'}, dimensions={0} | all-to-all | bytes 65536 | tf_op jit(solution)/shard_map/all_to_all | solution.py:266
  133.8 0.5 broadcast.4
  134.3 0.7 reduce
  135.1 0.7 line_body.1
  (27 shorter events, 1.6 us)
Async XLA Ops:
  1.5 20.9 %collective-permute-start = (bf16[49,512]{1,0:T(8,128)(2,1)S(1)}, bf16[49,512]{1,0:T(8,128)(2,1)S(1)}, u32[]{:S(2)}, u32[]{:S(2)}) collective-permute-start(bf16[49,512]{1,0:T(8,128)(2,1)S(1)} %slice.15), channel_id=1, source_target_pairs={{16,0},{32,16},{48,32},{64,48},{80,64},{96,80},{112,96},{128,112},... | collective-permute-start | bytes 150536 | tf_op jit(solution)/shard_map/ppermute | solution.py:118
  17.5 1.0 copy-start
  18.5 1.0 copy-start.3
  19.5 0.9 copy-start.4
  20.4 0.9 copy-start.5
  22.4 5.5 %collective-permute-start.1 = (bf16[56,512]{1,0:T(8,128)(2,1)S(1)}, bf16[56,512]{1,0:T(8,128)(2,1)S(1)}, u32[]{:S(2)}, u32[]{:S(2)}) collective-permute-start(bf16[56,512]{1,0:T(8,128)(2,1)S(1)} %pad_maximum_fusion), channel_id=1, source_target_pairs={{1,0},{2,1},{3,2},{4,3},{5,4},{6,5},{7,6},{8,7},{9,8},{10,9},{11,1... | collective-permute-start | bytes 172040 | tf_op jit(solution)/shard_map/ppermute | solution.py:121
  28.2 3.7 %collective-permute-start.2 = (f32[56,512]{1,0:T(8,128)S(1)}, f32[56,512]{1,0:T(8,128)S(1)}, u32[]{:S(2)}, u32[]{:S(2)}) collective-permute-start(f32[56,512]{1,0:T(8,128)S(1)} %get-tuple-element.23), channel_id=1, source_target_pairs={{0,16},{16,32},{32,48},{48,64},{64,80},{80,96},{96,112},{112,128},... | collective-permute-start | bytes 344072 | tf_op jit(solution)/shard_map/ppermute | solution.py:118
  31.9 2.6 %copy-start.6 = (f32[343]{0:T(512)S(1)}, f32[343]{0:T(512)}, u32[]{:S(2)}) copy-start(f32[343]{0:T(512)} %param.7) | copy-start | bytes 4120
  32.0 4.5 %collective-permute-start.3 = (f32[49,512]{1,0:T(8,128)S(1)}, f32[49,512]{1,0:T(8,128)S(1)}, u32[]{:S(2)}, u32[]{:S(2)}) collective-permute-start(f32[49,512]{1,0:T(8,128)S(1)} %pad_add_fusion.1), channel_id=1, source_target_pairs={{0,1},{1,2},{2,3},{3,4},{4,5},{5,6},{6,7},{7,8},{8,9},{9,10},{10,1... | collective-permute-start | bytes 301064 | tf_op jit(solution)/shard_map/ppermute | solution.py:121
  36.7 11.0 %collective-permute-start.4 = (bf16[49,512]{1,0:T(8,128)(2,1)S(1)}, bf16[49,512]{1,0:T(8,128)(2,1)S(1)}, u32[]{:S(2)}, u32[]{:S(2)}) collective-permute-start(bf16[49,512]{1,0:T(8,128)(2,1)S(1)} %get-tuple-element.26), channel_id=1, source_target_pairs={{16,0},{32,16},{48,32},{64,48},{80,64},{96,80},{112,96},{128,112},... | collective-permute-start | bytes 150536 | tf_op jit(solution)/shard_map/ppermute | solution.py:118
  47.7 5.5 %collective-permute-start.5 = (bf16[56,512]{1,0:T(8,128)(2,1)S(1)}, bf16[56,512]{1,0:T(8,128)(2,1)S(1)}, u32[]{:S(2)}, u32[]{:S(2)}) collective-permute-start(bf16[56,512]{1,0:T(8,128)(2,1)S(1)} %pad_maximum_fusion.1), channel_id=1, source_target_pairs={{1,0},{2,1},{3,2},{4,3},{5,4},{6,5},{7,6},{8,7},{9,8},{10,9},{11,1... | collective-permute-start | bytes 172040 | tf_op jit(solution)/shard_map/ppermute | solution.py:121
  53.6 8.6 %copy-start.2 = (s32[512,1]{1,0:T(8,128)S(1)}, s32[512,1]{1,0:T(8,128)}, u32[]{:S(2)}) copy-start(s32[512,1]{1,0:T(8,128)} %constant.11.clone.order) | copy-start | bytes 6148
  53.6 5.0 %collective-permute-start.6 = (f32[56,512]{1,0:T(8,128)S(1)}, f32[56,512]{1,0:T(8,128)S(1)}, u32[]{:S(2)}, u32[]{:S(2)}) collective-permute-start(f32[56,512]{1,0:T(8,128)S(1)} %get-tuple-element.29.away_x), channel_id=1, source_target_pairs={{0,16},{16,32},{32,48},{48,64},{64,80},{80,96},{96,112},{112,128},... | collective-permute-start | bytes 344072 | tf_op jit(solution)/shard_map/ppermute | solution.py:118
  58.6 5.4 %collective-permute-start.7 = (f32[49,512]{1,0:T(8,128)S(1)}, f32[49,512]{1,0:T(8,128)S(1)}, u32[]{:S(2)}, u32[]{:S(2)}) collective-permute-start(f32[49,512]{1,0:T(8,128)S(1)} %pad_add_fusion), channel_id=1, source_target_pairs={{0,1},{1,2},{2,3},{3,4},{4,5},{5,6},{6,7},{7,8},{8,9},{9,10},{10,1... | collective-permute-start | bytes 301064 | tf_op jit(solution)/shard_map/ppermute | solution.py:121
  62.2 1.8 %copy-start.1 = (bf16[343,512]{1,0:T(8,128)(2,1)S(1)}, bf16[343,512]{1,0:T(8,128)(2,1)}, u32[]{:S(2)}) copy-start(bf16[343,512]{1,0:T(8,128)(2,1)} %field.5) | copy-start | bytes 1053700

commit v2 on v1

v2 whole, which is shorter than its diff:
```python
import math

import jax
import jax.numpy as jnp
from jax import lax
from jax.experimental import pallas as pl
from jax.experimental.pallas import tpu as pltpu
from jax.sharding import Mesh, PartitionSpec as P

DEG = 7
SIDE = DEG + 1
FACE = DEG * DEG
RIM = FACE + DEG
OWN = FACE * DEG
CELL = OWN + RIM + FACE
SPECTRUM_CENTER = 2.0
SPECTRUM_HALF = 2.0
VMEM_LIMIT = 24 * 2**20
F32 = jnp.float32
BF16 = jnp.bfloat16


def dot(left, right):
    return jnp.dot(left, right, preferred_element_type=F32)


def dot_rows(left, right):
    return lax.dot_general(left, right, (((0,), (0,)), ((), ())), preferred_element_type=F32)


def dot_columns(left, right):
    return lax.dot_general(left, right, (((1,), (1,)), ((), ())), preferred_element_type=F32)


def one_hot(column, width):
    return (column == lax.broadcasted_iota(jnp.int32, (column.shape[0], width), 1)).astype(F32).astype(BF16)


def node_order():
    place = lax.broadcasted_iota(jnp.int32, (CELL, 1), 0)

    def seventh(n):
        return lax.shift_right_logical(n * 9363, 16)

    column = seventh(place)
    plane = seventh(column)
    own = plane * SIDE * SIDE + (column - plane * DEG) * SIDE + (place - column * DEG)
    rim = place - OWN
    rim = DEG * SIDE * SIDE + seventh(rim) * SIDE + (rim - seventh(rim) * DEG)
    face = place - OWN - RIM
    face = seventh(face) * SIDE * SIDE + DEG * SIDE + (face - seventh(face) * DEG)
    return jnp.where(place < OWN, own, jnp.where(place < OWN + RIM, rim, face))


def call(kernel, *shapes, scratch=(), results=(), raw=(), scalar=()):
    def run(*args):
        vmem = pl.BlockSpec(memory_space=pltpu.VMEM)
        places = [
            pl.BlockSpec(memory_space=pl.ANY)
            if i in raw
            else pl.BlockSpec(memory_space=pltpu.SMEM)
            if i in scalar
            else vmem
            for i in range(len(args))
        ]
        return pl.pallas_call(
            kernel,
            out_shape=[
                jax.ShapeDtypeStruct(*shape) if i in results else pltpu.VMEM(*shape) for i, shape in enumerate(shapes)
            ],
            in_specs=places,
            out_specs=[vmem] * len(shapes),
            scratch_shapes=list(scratch),
            compiler_params=pltpu.CompilerParams(vmem_limit_bytes=VMEM_LIMIT),
            name=kernel.__name__,
        )(
            *[
                arg
                if i in scalar
                else pltpu.with_memory_space_constraint(arg, pltpu.HBM if i in raw else pltpu.VMEM)
                for i, arg in enumerate(args)
            ]
        )

    return run


def pack_upward(partial, wide, message, stage):
    rim = partial[OWN : OWN + RIM, :]
    high = rim.astype(BF16).astype(F32)
    stage[:RIM, :] = high
    stage[RIM : 2 * RIM, :] = rim - high
    for i in range(DEG):
        stage[2 * RIM + i * DEG : 2 * RIM + (i + 1) * DEG, :] = wide[i * FACE : i * FACE + DEG, :]
    message[...] = stage[...].astype(BF16)


def prepare(field_in, stiffness_in, field, ordered, own_columns, partial, message, stiffness, wide, stage, sems):
    copies = [
        pltpu.make_async_copy(stiffness_in, stiffness, sems.at[0]),
        pltpu.make_async_copy(field_in, field, sems.at[1]),
    ]
    for copy in copies:
        copy.start()
    order = one_hot(node_order(), SIDE**3)
    copies[0].wait()
    ordered[...] = dot_columns(dot(order, stiffness[...]).astype(BF16), order)
    own_columns[...] = ordered[:, :OWN].astype(BF16)
    copies[1].wait()
    partial[...] = dot(own_columns[...], field[...])
    wide[...] = field[...].astype(F32)
    pack_upward(partial, wide, message, stage)


def split_matrix(ordered, own_x, rim_x, face_x, own_y, side_y, face_y, edge_y):
    to_x, to_y = OWN, OWN + FACE
    own_x[...] = ordered[:OWN, to_x:to_y].astype(BF16)
    rim_x[...] = ordered[OWN : OWN + RIM, to_x:to_y].astype(BF16)
    face_x[...] = ordered[OWN + RIM :, to_x:to_y].astype(BF16)
    own_y[...] = ordered[:OWN, to_y:].astype(BF16)
    side_y[...] = ordered[OWN : OWN + FACE, to_y:].astype(BF16)
    face_y[...] = ordered[OWN + RIM :, to_y:].astype(BF16)
    edge_y[...] = ordered[OWN + FACE : OWN + RIM, to_y:].astype(BF16)


def cross(inside, rim_x, face_x, partial, field, above_x, message, upward, downward, rim, wide, face, stage):
    wide[...] = message[...].astype(F32)
    rim[...] = wide[:RIM, :] + wide[RIM : 2 * RIM, :] + inside[0] * dot(rim_x[...], field[:FACE, :])
    upward[...] = partial[OWN + RIM :, :] + dot(face_x[...], above_x[...])
    upward[:DEG, :] += rim[FACE:, :]
    face[...] = above_x[...].astype(F32)
    stage[:DEG, :] = face[:DEG, :]
    own = field[...].astype(F32)
    for i in range(DEG):
        stage[DEG + i * DEG : DEG + (i + 1) * DEG, :] = own[i * FACE : i * FACE + DEG, :]
    stage[RIM:, :] = wide[2 * RIM :, :]
    downward[...] = stage[...].astype(BF16)


def gather_row(inside, own_x, face_y, edge_y, partial, field, above_x, rim, downward, own, corner, face):
    own[...] = partial[:OWN, :] + dot(own_x[...], above_x[...])
    own[:FACE, :] += rim[:FACE, :]
    face[...] = inside[1] * dot(face_y[...], downward[:RIM, :])
    for i in range(DEG):
        own[i * FACE : i * FACE + DEG, :] += face[i * DEG : (i + 1) * DEG, :]
    wide = downward[...].astype(F32)
    corner[:DEG, :] = field[...].astype(F32)[:DEG]
    corner[DEG:, :] = wide[RIM:]
    own[:DEG, :] += inside[0] * inside[1] * dot(edge_y[...], corner[...].astype(BF16))


def close(inside, own_y, side_y, own, from_y, above_y, image, far):
    wide = above_y[...].astype(F32)
    far[:DEG, :] = wide[DEG : 2 * DEG]
    far[DEG:, :] = wide[RIM:]
    image[:OWN, :] = own[...] + dot(own_y[...], above_y[:RIM, :])
    image[:FACE, :] += inside[0] * dot(side_y[...], far[...].astype(BF16))
    for i in range(DEG):
        image[i * FACE : i * FACE + DEG, :] += from_y[i * DEG : (i + 1) * DEG, :]


def lift(
    inside, own_y, side_y, own, from_y, above_y, field, potential, own_columns,
    lifted, partial, lowest, message, image, far, stage,
):
    close(inside, own_y, side_y, own, from_y, above_y, image, far)
    field32 = field[...].astype(F32)
    first_image = image[...] + potential[...] * field32
    image[...] = (first_image - SPECTRUM_CENTER * field32) / SPECTRUM_HALF
    lifted[...] = image[...].astype(BF16)
    lowest[...] = image[:FACE, :].astype(BF16)
    partial[...] = dot(own_columns[...], lifted[...])
    pack_upward(partial, image, message, stage)


def solution(mesh):
    length_x, length_y = mesh.shape["gx"], mesh.shape["gy"]
    length_z = length_x // 4
    split_mesh = Mesh(mesh.devices.reshape(length_z, 2, 2, length_y), ("z", "half", "core", "gy"))
    gx = ("z", "half", "core")
    every = gx + ("gy",)

    def passed_x(value, by):
        return lax.ppermute(value, gx, [(i, i + by) for i in range(length_x) if 0 <= i + by < length_x])

    def passed_y(value, by):
        return lax.ppermute(value, "gy", [(i, i + by) for i in range(length_y) if 0 <= i + by < length_y])

    def per_device(orbitals, potential, cell_stiffness):
        node_count, orbital_count = orbitals.shape
        norm_scale = 1.0 / math.sqrt(node_count * length_x * length_y)
        block_rows = orbital_count // length_x
        block_cols = orbital_count // length_y
        half = orbital_count // 2
        quarter = orbital_count // 4
        padded = -(-OWN // 128) * 128

        def by_orbital(rows):
            return (rows, orbital_count)

        def staged(*rows):
            return tuple(pltpu.VMEM(by_orbital(n), F32) for n in rows)

        weight = potential[:, None]
        inside = jnp.stack([lax.axis_index(gx), lax.axis_index("gy")])
        inside = (inside > 0).astype(F32)
        message_rows = 2 * RIM + FACE
        raw_rows = RIM + FACE

        above_x = passed_x(orbitals[:FACE], -1)
        field, ordered, own_columns, partial, message = call(
            prepare,
            (by_orbital(OWN), BF16),
            ((CELL, CELL), F32),
            ((CELL, OWN), BF16),
            (by_orbital(CELL), F32),
            (by_orbital(message_rows), BF16),
            scratch=(
                pltpu.VMEM((SIDE**3, SIDE**3), BF16),
                *staged(OWN, message_rows),
                pltpu.SemaphoreType.DMA((2,)),
            ),
            raw=(0, 1),
        )(orbitals, cell_stiffness)
        message = passed_x(message, 1)
        own_x, rim_x, face_x, own_y, side_y, face_y, edge_y = call(
            split_matrix,
            ((OWN, FACE), BF16),
            ((RIM, FACE), BF16),
            ((FACE, FACE), BF16),
            ((OWN, RIM), BF16),
            ((FACE, RIM), BF16),
            ((FACE, RIM), BF16),
            ((DEG, RIM), BF16),
        )(ordered)

        def row_part(partial, values, above_x, message):
            upward, downward, rim = call(
                cross,
                (by_orbital(FACE), F32),
                (by_orbital(raw_rows), BF16),
                (by_orbital(RIM), F32),
                scratch=staged(message_rows, FACE, raw_rows),
                scalar=(0,),
            )(inside, rim_x, face_x, partial, values, above_x, message)
            from_y = passed_y(upward, 1)
            above_y = passed_y(downward, -1)
            own = call(gather_row, (by_orbital(OWN), F32), scratch=staged(RIM, FACE), scalar=(0,))(
                inside, own_x, face_y, edge_y, partial, values, above_x, rim, downward
            )[0]
            return own, from_y, above_y

        own, from_y, above_y = row_part(partial, field, above_x, message)
        lifted, partial, lowest, message = call(
            lift,
            (by_orbital(OWN), BF16),
            (by_orbital(CELL), F32),
            (by_orbital(FACE), BF16),
            (by_orbital(message_rows), BF16),
            scratch=staged(OWN, RIM, message_rows),
            scalar=(0,),
        )(inside, own_y, side_y, own, from_y, above_y, field, weight, own_columns)
        above_x = passed_x(lowest, -1)
        message = passed_x(message, 1)
        own, from_y, above_y = row_part(partial, lifted, above_x, message)

        def filter_and_gram(
            inside, own_y, side_y, own, from_y, above_y, field, lifted, potential,
            filtered, out, image, far, rows,
        ):
            close(inside, own_y, side_y, own, from_y, above_y, image, far)
            image[OWN:, :] = jnp.zeros((padded - OWN, orbital_count), F32)
            rows[OWN:, :] = jnp.zeros((padded - OWN, orbital_count), F32)
            rows[:OWN, :] = lifted[...].astype(F32)
            lifted32 = rows[:OWN, :]
            image[:OWN, :] += potential[...] * lifted32
            place = lax.broadcasted_iota(jnp.int32, (orbital_count, 1), 0)
            low = lax.bitwise_and(place, quarter - 1)
            line = lax.shift_right_logical(low, block_rows.bit_length() - 1)
            side = lax.shift_right_logical(place, quarter.bit_length() - 1)
            order = (
                line * (4 * block_rows)
                + lax.bitwise_and(side, 1) * (2 * block_rows)
                + lax.shift_right_logical(side, 1) * block_rows
                + lax.bitwise_and(low, block_rows - 1)
            )
            shuffle = one_hot(order, orbital_count)

            def gram(which, left, right):
                shuffled = dot_columns(right, shuffle).astype(BF16)
                product = (dot_rows(left, shuffled) * norm_scale).astype(BF16)
                out[0, which] = product[:, :half]
                out[1, which] = product[:, half:]

            gram(0, image[...].astype(BF16), rows[...].astype(BF16))
            image[:OWN, :] = (
                2.0 * (image[:OWN, :] - SPECTRUM_CENTER * lifted32) / SPECTRUM_HALF - field[...].astype(F32)
            )
            filtered[...] = image[:OWN, :].astype(BF16)
            values = image[...].astype(BF16)
            gram(1, values, values)

        filtered, terms = call(
            filter_and_gram,
            (by_orbital(OWN), BF16),
            ((2, 2, orbital_count, half), BF16),
            scratch=staged(padded, RIM, padded),
            results=(0,),
            scalar=(0,),
        )(inside, own_y, side_y, own, from_y, above_y, field, lifted, weight)

        def pair_sum(terms, out):
            for which in range(2):
                total = (terms[0, which].astype(F32) + terms[1, which].astype(F32)).astype(BF16)
                for side in range(2):
                    part = total[:, side * quarter : (side + 1) * quarter]
                    for j in range(length_y):
                        out[side, j, which * block_cols : (which + 1) * block_cols] = part[
                            j * block_cols : (j + 1) * block_cols
                        ]

        wide = 2 * block_cols
        fold = max(1, 128 // wide)
        short = block_rows // fold

        def plane_sum(terms, out):
            total = terms[0].astype(F32)
            for source in range(1, 2 * length_y):
                total += terms[source].astype(F32)
            total = total.T.reshape(length_z, block_rows, wide)
            for part in range(fold):
                out[:, :, part * wide : (part + 1) * wide] = total[:, part * short : (part + 1) * short, :]

        def line_sum(terms, ham, correlation):
            total = terms[0]
            for source in range(1, length_z):
                total += terms[source]
            for part in range(fold):
                block = total[:, part * wide : (part + 1) * wide]
                ham[part * short : (part + 1) * short, :] = block[:, :block_cols]
                correlation[part * short : (part + 1) * short, :] = block[:, block_cols:]

        terms = lax.all_to_all(terms, "core", 0, 0, tiled=True)
        terms = call(pair_sum, ((2, length_y, wide, quarter), BF16))(terms)[0]
        terms = terms.reshape(2 * length_y, wide, quarter)
        terms = lax.all_to_all(terms, ("half", "gy"), 0, 0, tiled=True)
        terms = call(plane_sum, ((length_z, short, fold * wide), F32))(terms)[0]
        terms = lax.all_to_all(terms, "z", 0, 0, tiled=True)
        block = (block_rows, block_cols)
        projected_ham, correlation = call(line_sum, (block, F32), (block, F32), results=(0, 1))(terms)
        return filtered, projected_ham, correlation

    return jax.shard_map(
        per_device,
        mesh=split_mesh,
        in_specs=(P(every, None), P(every), P()),
        out_specs=(P(every, None), P(gx, "gy"), P(gx, "gy")),
        check_vma=False,
    )
```

time: 137 us -> 128 us (0.934)
  waiting for transfers between devices: 22.5 us -> 11.5 us
  local copies, waits for them, and re-layouts: 5.54 us -> 0.93 us
  Pallas kernels: 6.08 us -> 10.2 us
  blocking collectives: 68.2 us -> 70.7 us
    ppermute x4, waiting for transfers between devices: 9.91 us -> 2.45 us  [passed_y(): lax.ppermute(value, 'gy', [(i, i + by) for i in range(length_y) if 0 <= i...]
    unnamed x16 -> x2, local copies, waits for them, and re-layouts: 4.09 us -> 0.01 us
    pallas_call x12 -> x11, Pallas kernels: 6.08 us -> 10.2 us  [run(): pl.pallas_call(kernel, out_shape=[jax.ShapeDtypeStruct(*shape) if i in re...]
    ppermute x4, waiting for transfers between devices: 12.6 us -> 9.07 us  [passed_x(): lax.ppermute(value, gx, [(i, i + by) for i in range(length_x) if 0 <= i +...]
    all_to_all x1, blocking collectives: 31.5 us -> 33.9 us  [per_device(): terms = lax.all_to_all(terms, ('half', 'gy'), 0, 0, tiled=True)]
    ppermute x4, starting transfers between devices: 8.74 us -> 10.6 us  [passed_y(): lax.ppermute(value, 'gy', [(i, i + by) for i in range(length_y) if 0 <= i...]
    ppermute x4, starting transfers between devices: 23.1 us -> 21.6 us  [passed_x(): lax.ppermute(value, gx, [(i, i + by) for i in range(length_x) if 0 <= i +...]
  transfers between devices with their start and end apart: 8 -> 8, of which waited for: 7 -> 5; matrix products, arithmetic and copies ran while one was open for 0% -> 1% of each run, Pallas kernels for 2% -> 1%
where the time goes in v2:
time: 128 us; the launch traced here: 126 us
  blocking collectives  70.7 us (55%)
  starting transfers between devices  32.2 us (25%)
  waiting for transfers between devices  11.5 us (9%)
  Pallas kernels  10.2 us (8%)
    all_to_all x1, blocking collectives, per_device(): terms = lax.all_to_all(terms, ('half', 'gy'), 0, 0, tiled=True)  33.9 us
    all_to_all x1, blocking collectives, per_device(): terms = lax.all_to_all(terms, 'z', 0, 0, tiled=True)  32.6 us
    ppermute x4, starting transfers between devices, passed_x(): lax.ppermute(value, gx, [(i, i + by) for i in range(length_x) if 0 <= i +...  21.6 us
    ppermute x4, starting transfers between devices, passed_y(): lax.ppermute(value, 'gy', [(i, i + by) for i in range(length_y) if 0 <= i...  10.6 us
    pallas_call x11, Pallas kernels, run(): pl.pallas_call(kernel, out_shape=[jax.ShapeDtypeStruct(*shape) if i in re...  10.2 us
    ppermute x4, waiting for transfers between devices, passed_x(): lax.ppermute(value, gx, [(i, i + by) for i in range(length_x) if 0 <= i +...  9.07 us
    all_to_all x1, blocking collectives, per_device(): terms = lax.all_to_all(terms, 'core', 0, 0, tiled=True)  4.21 us
  transfers between devices with their start and end apart: 8, of which 5 were waited for; matrix products, arithmetic and copies ran while one was open for 1% of the time, Pallas kernels for 1%

profile of v2, /device:TPU:1, one launch (start us, length us, event | category | flops | bytes accessed | tf_op | source)
XLA Modules:
  0.0 126.4 jit_solution(2121344661890107523)
XLA Ops:
  0.6 2.1 %prepare.1 = (bf16[343,512]{1,0:T(8,128)(2,1)S(1)}, f32[448,448]{1,0:T(8,128)S(1)}, bf16[448,343]{1,0:T(8,128)(2,1)S(1)}, f32[448,512]{1,0:T(8,128)S(1)}, bf16[161,512]{1,0:T(8,128)(2,1)S(1)}) custom-call(bf16[343,512]{1,0:T(8,128)(2,1)} %field_in.1, bf16[512,512]{1,0:T(8,128)(2,1)} %stiffness_in.1), custom_call_target="tpu_custom_call" | custom-call | tf_op jit(solution)/shard_map/prepare/pallas_call | solution.py:66
  2.8 8.8 %collective-permute-start.1 = (bf16[161,512]{1,0:T(8,128)(2,1)S(1)}, bf16[161,512]{1,0:T(8,128)(2,1)S(1)}, u32[]{:S(2)}, u32[]{:S(2)}) collective-permute-start(bf16[161,512]{1,0:T(8,128)(2,1)S(1)} %get-tuple-element.39), channel_id=1, source_target_pairs={{0,16},{16,32},{32,48},{48,64},{64,80},{80,96},{96,112},{112,128},... | collective-permute-start | bytes 494600 | tf_op jit(solution)/shard_map/ppermute | solution.py:184
  11.6 0.8 slice.3
  12.4 8.5 %collective-permute-start = (bf16[49,512]{1,0:T(8,128)(2,1)S(1)}, bf16[49,512]{1,0:T(8,128)(2,1)S(1)}, u32[]{:S(2)}, u32[]{:S(2)}) collective-permute-start(bf16[49,512]{1,0:T(8,128)(2,1)S(1)} %slice.3), channel_id=1, source_target_pairs={{16,0},{32,16},{48,32},{64,48},{80,64},{96,80},{112,96},{128,112},... | collective-permute-start | bytes 150536 | tf_op jit(solution)/shard_map/ppermute | solution.py:184
  20.9 0.1 compare_convert_fusion.inside
  21.0 0.2 split_matrix.1
  21.2 0.6 collective-permute-done.above_x
  21.8 0.0 collective-permute-done.1.message
  21.8 0.7 cross.2
  22.6 0.0 copy-start
  22.6 1.3 %collective-permute-start.3 = (bf16[105,512]{1,0:T(8,128)(2,1)S(1)}, bf16[105,512]{1,0:T(8,128)(2,1)S(1)}, u32[]{:S(2)}, u32[]{:S(2)}) collective-permute-start(bf16[105,512]{1,0:T(8,128)(2,1)S(1)} %get-tuple-element.41.downward), channel_id=1, source_target_pairs={{1,0},{2,1},{3,2},{4,3},{5,4},{6,5},{7,6},{8,7},{9,8},{10,9},{11,1... | collective-permute-start | bytes 322568 | tf_op jit(solution)/shard_map/ppermute | solution.py:187
  23.9 4.0 %collective-permute-start.2 = (f32[49,512]{1,0:T(8,128)S(1)}, f32[49,512]{1,0:T(8,128)S(1)}, u32[]{:S(2)}, u32[]{:S(2)}) collective-permute-start(f32[49,512]{1,0:T(8,128)S(1)} %get-tuple-element.42), channel_id=1, source_target_pairs={{0,1},{1,2},{2,3},{3,4},{4,5},{5,6},{6,7},{7,8},{8,9},{9,10},{10,1... | collective-permute-start | bytes 301064 | tf_op jit(solution)/shard_map/ppermute | solution.py:187
  27.9 0.1 broadcast_in_dim.4.potential
  28.0 0.8 gather_row.2.own
  28.8 0.8 collective-permute-done.2.from_y
  29.7 0.7 collective-permute-done.3.above_y
  30.3 1.3 %lift.1 = (bf16[343,512]{1,0:T(8,128)(2,1)S(1)}, f32[448,512]{1,0:T(8,128)S(1)}, bf16[49,512]{1,0:T(8,128)(2,1)S(1)}, bf16[161,512]{1,0:T(8,128)(2,1)S(1)}) custom-call(f32[2]{0:T(128)S(1)} %compare_convert_fusion.inside, bf16[343,56]{1,0:T(8,128)(2,1)S(1)} %get-tuple-element.30.own_y, bf16[49,56]{1,0:T(8,128)(2,1)S(1)} %get-tuple-element.31.side_y, ...), custom_call_target="tpu_custom_call" | custom-call | tf_op jit(solution)/shard_map/lift/pallas_call | solution.py:66
  31.7 2.4 %collective-permute-start.5 = (bf16[161,512]{1,0:T(8,128)(2,1)S(1)}, bf16[161,512]{1,0:T(8,128)(2,1)S(1)}, u32[]{:S(2)}, u32[]{:S(2)}) collective-permute-start(bf16[161,512]{1,0:T(8,128)(2,1)S(1)} %get-tuple-element.47), channel_id=1, source_target_pairs={{0,16},{16,32},{32,48},{48,64},{64,80},{80,96},{96,112},{112,128},... | collective-permute-start | bytes 494600 | tf_op jit(solution)/shard_map/ppermute | solution.py:184
  34.1 2.0 %collective-permute-start.4 = (bf16[49,512]{1,0:T(8,128)(2,1)S(1)}, bf16[49,512]{1,0:T(8,128)(2,1)S(1)}, u32[]{:S(2)}, u32[]{:S(2)}) collective-permute-start(bf16[49,512]{1,0:T(8,128)(2,1)S(1)} %get-tuple-element.46), channel_id=1, source_target_pairs={{16,0},{32,16},{48,32},{64,48},{80,64},{96,80},{112,96},{128,112},... | collective-permute-start | bytes 150536 | tf_op jit(solution)/shard_map/ppermute | solution.py:184
  36.0 8.4 %collective-permute-done.4.above_x = bf16[49,512]{1,0:T(8,128)(2,1)S(1)} collective-permute-done((bf16[49,512]{1,0:T(8,128)(2,1)S(1)}, bf16[49,512]{1,0:T(8,128)(2,1)S(1)}, u32[]{:S(2)}, u32[]{:S(2)}) %collective-permute-start.4) | collective-permute-done | bytes 50208 | tf_op jit(solution)/shard_map/ppermute | solution.py:184
  44.5 0.7 cross.3
  45.2 1.3 %collective-permute-start.7 = (bf16[105,512]{1,0:T(8,128)(2,1)S(1)}, bf16[105,512]{1,0:T(8,128)(2,1)S(1)}, u32[]{:S(2)}, u32[]{:S(2)}) collective-permute-start(bf16[105,512]{1,0:T(8,128)(2,1)S(1)} %get-tuple-element.49.downward), channel_id=1, source_target_pairs={{1,0},{2,1},{3,2},{4,3},{5,4},{6,5},{7,6},{8,7},{9,8},{10,9},{11,1... | collective-permute-start | bytes 322568 | tf_op jit(solution)/shard_map/ppermute | solution.py:187
  46.5 4.0 %collective-permute-start.6 = (f32[49,512]{1,0:T(8,128)S(1)}, f32[49,512]{1,0:T(8,128)S(1)}, u32[]{:S(2)}, u32[]{:S(2)}) collective-permute-start(f32[49,512]{1,0:T(8,128)S(1)} %get-tuple-element.50), channel_id=1, source_target_pairs={{0,1},{1,2},{2,3},{3,4},{4,5},{5,6},{6,7},{7,8},{8,9},{9,10},{10,1... | collective-permute-start | bytes 301064 | tf_op jit(solution)/shard_map/ppermute | solution.py:187
  50.5 0.8 gather_row.3.own
  51.3 0.9 collective-permute-done.6.from_y
  52.3 2.3 %filter_and_gram.1 = (bf16[343,512]{1,0:T(8,128)(2,1)}, bf16[2,2,512,256]{3,2,1,0:T(8,128)(2,1)S(1)}) custom-call(f32[2]{0:T(128)S(1)} %compare_convert_fusion.inside, bf16[343,56]{1,0:T(8,128)(2,1)S(1)} %get-tuple-element.30.own_y, bf16[49,56]{1,0:T(8,128)(2,1)S(1)} %get-tuple-element.31.side_y, f32[343,512]{1,0:T(8,128)S(1)} %gather_row.3.own, ...), custom_call_target="tpu_custom_call" | custom-call | tf_op jit(solution)/shard_map/filter_and_gram/pallas_call | solution.py:66
  54.6 4.2 %all_to_all.15.terms = bf16[2,2,512,256]{3,2,1,0:T(8,128)(2,1)S(1)} all-to-all(bf16[2,2,512,256]{3,2,1,0:T(8,128)(2,1)S(1)} %get-tuple-element.52), channel_id=1, replica_groups=mesh['z'=16,'half'=2,'core'=2,'gy'=16] {'core'}, dimensions={0} | all-to-all | bytes 2097152 | tf_op jit(solution)/shard_map/all_to_all | solution.py:343
  58.9 0.1 pair_sum.1
  59.0 33.9 %all_to_all.16.terms = bf16[32,64,128]{2,1,0:T(8,128)(2,1)S(1)} all-to-all(bf16[32,64,128]{2,1,0:T(8,128)(2,1)S(1)} %bitcast.3), channel_id=1, replica_groups=mesh['z'=16,'half'=2,'core'=2,'gy'=16] {'half','gy'}, dimensions={0} | all-to-all | bytes 1048576 | tf_op jit(solution)/shard_map/all_to_all | solution.py:346
  92.9 0.2 plane_sum.1
  93.1 32.6 %all_to_all.17.terms = f32[16,4,128]{2,1,0:T(4,128)S(1)} all-to-all(f32[16,4,128]{2,1,0:T(4,128)S(1)} %plane_sum.1), channel_id=1, replica_groups=mesh['z'=16,'half'=2,'core'=2,'gy'=16] {'z'}, dimensions={0} | all-to-all | bytes 65536 | tf_op jit(solution)/shard_map/all_to_all | solution.py:348
  125.7 0.7 line_sum.1
  (3 shorter events, 0.0 us)
Async XLA Ops:
  2.8 19.1 %collective-permute-start.1 = (bf16[161,512]{1,0:T(8,128)(2,1)S(1)}, bf16[161,512]{1,0:T(8,128)(2,1)S(1)}, u32[]{:S(2)}, u32[]{:S(2)}) collective-permute-start(bf16[161,512]{1,0:T(8,128)(2,1)S(1)} %get-tuple-element.39), channel_id=1, source_target_pairs={{0,16},{16,32},{32,48},{48,64},{64,80},{80,96},{96,112},{112,128},... | collective-permute-start | bytes 494600 | tf_op jit(solution)/shard_map/ppermute | solution.py:184
  12.4 9.4 %collective-permute-start = (bf16[49,512]{1,0:T(8,128)(2,1)S(1)}, bf16[49,512]{1,0:T(8,128)(2,1)S(1)}, u32[]{:S(2)}, u32[]{:S(2)}) collective-permute-start(bf16[49,512]{1,0:T(8,128)(2,1)S(1)} %slice.3), channel_id=1, source_target_pairs={{16,0},{32,16},{48,32},{64,48},{80,64},{96,80},{112,96},{128,112},... | collective-permute-start | bytes 150536 | tf_op jit(solution)/shard_map/ppermute | solution.py:184
  22.6 5.3 %copy-start = (f32[343]{0:T(512)S(1)}, f32[343]{0:T(512)}, u32[]{:S(2)}) copy-start(f32[343]{0:T(512)} %param.4) | copy-start | bytes 4120
  22.6 7.7 %collective-permute-start.3 = (bf16[105,512]{1,0:T(8,128)(2,1)S(1)}, bf16[105,512]{1,0:T(8,128)(2,1)S(1)}, u32[]{:S(2)}, u32[]{:S(2)}) collective-permute-start(bf16[105,512]{1,0:T(8,128)(2,1)S(1)} %get-tuple-element.41.downward), channel_id=1, source_target_pairs={{1,0},{2,1},{3,2},{4,3},{5,4},{6,5},{7,6},{8,7},{9,8},{10,9},{11,1... | collective-permute-start | bytes 322568 | tf_op jit(solution)/shard_map/ppermute | solution.py:187
  23.9 5.8 %collective-permute-start.2 = (f32[49,512]{1,0:T(8,128)S(1)}, f32[49,512]{1,0:T(8,128)S(1)}, u32[]{:S(2)}, u32[]{:S(2)}) collective-permute-start(f32[49,512]{1,0:T(8,128)S(1)} %get-tuple-element.42), channel_id=1, source_target_pairs={{0,1},{1,2},{2,3},{3,4},{4,5},{5,6},{6,7},{7,8},{8,9},{9,10},{10,1... | collective-permute-start | bytes 301064 | tf_op jit(solution)/shard_map/ppermute | solution.py:187
  31.7 12.8 %collective-permute-start.5 = (bf16[161,512]{1,0:T(8,128)(2,1)S(1)}, bf16[161,512]{1,0:T(8,128)(2,1)S(1)}, u32[]{:S(2)}, u32[]{:S(2)}) collective-permute-start(bf16[161,512]{1,0:T(8,128)(2,1)S(1)} %get-tuple-element.47), channel_id=1, source_target_pairs={{0,16},{16,32},{32,48},{48,64},{64,80},{80,96},{96,112},{112,128},... | collective-permute-start | bytes 494600 | tf_op jit(solution)/shard_map/ppermute | solution.py:184
  34.1 10.4 %collective-permute-start.4 = (bf16[49,512]{1,0:T(8,128)(2,1)S(1)}, bf16[49,512]{1,0:T(8,128)(2,1)S(1)}, u32[]{:S(2)}, u32[]{:S(2)}) collective-permute-start(bf16[49,512]{1,0:T(8,128)(2,1)S(1)} %get-tuple-element.46), channel_id=1, source_target_pairs={{16,0},{32,16},{48,32},{64,48},{80,64},{96,80},{112,96},{128,112},... | collective-permute-start | bytes 150536 | tf_op jit(solution)/shard_map/ppermute | solution.py:184
  45.2 7.1 %collective-permute-start.7 = (bf16[105,512]{1,0:T(8,128)(2,1)S(1)}, bf16[105,512]{1,0:T(8,128)(2,1)S(1)}, u32[]{:S(2)}, u32[]{:S(2)}) collective-permute-start(bf16[105,512]{1,0:T(8,128)(2,1)S(1)} %get-tuple-element.49.downward), channel_id=1, source_target_pairs={{1,0},{2,1},{3,2},{4,3},{5,4},{6,5},{7,6},{8,7},{9,8},{10,9},{11,1... | collective-permute-start | bytes 322568 | tf_op jit(solution)/shard_map/ppermute | solution.py:187
  46.5 5.8 %collective-permute-start.6 = (f32[49,512]{1,0:T(8,128)S(1)}, f32[49,512]{1,0:T(8,128)S(1)}, u32[]{:S(2)}, u32[]{:S(2)}) collective-permute-start(f32[49,512]{1,0:T(8,128)S(1)} %get-tuple-element.50), channel_id=1, source_target_pairs={{0,1},{1,2},{2,3},{3,4},{4,5},{5,6},{6,7},{7,8},{8,9},{9,10},{10,1... | collective-permute-start | bytes 301064 | tf_op jit(solution)/shard_map/ppermute | solution.py:187

commit v3 on v2

--- a/solution.py
+++ b/solution.py
@@ -52,14 +52,12 @@
     return jnp.where(place < OWN, own, jnp.where(place < OWN + RIM, rim, face))
 
 
-def call(kernel, *shapes, scratch=(), results=(), raw=(), scalar=()):
+def call(kernel, *shapes, scratch=(), results=(), raw=()):
     def run(*args):
         vmem = pl.BlockSpec(memory_space=pltpu.VMEM)
         places = [
             pl.BlockSpec(memory_space=pl.ANY)
             if i in raw
-            else pl.BlockSpec(memory_space=pltpu.SMEM)
-            if i in scalar
             else vmem
             for i in range(len(args))
         ]
@@ -75,9 +73,7 @@
             name=kernel.__name__,
         )(
             *[
-                arg
-                if i in scalar
-                else pltpu.with_memory_space_constraint(arg, pltpu.HBM if i in raw else pltpu.VMEM)
+                pltpu.with_memory_space_constraint(arg, pltpu.HBM if i in raw else pltpu.VMEM)
                 for i, arg in enumerate(args)
             ]
         )
@@ -85,17 +81,60 @@
     return run
 
 
-def pack_upward(partial, wide, message, stage):
-    rim = partial[OWN : OWN + RIM, :]
-    high = rim.astype(BF16).astype(F32)
-    stage[:RIM, :] = high
-    stage[RIM : 2 * RIM, :] = rim - high
+def chosen(upper, messages, arrived):
+    far, near = messages
+
+    @pl.when(upper)
+    def _():
+        arrived(near, far)
+
+    @pl.when(jnp.logical_not(upper))
+    def _():
+        arrived(far, near)
+
+
+def send(upper, far, near, upward, downward):
+    @pl.when(upper)
+    def _():
+        far[...] = upward[...].astype(BF16)
+        near[: downward.shape[0], :] = downward[...].astype(BF16)
+
+    @pl.when(jnp.logical_not(upper))
+    def _():
+        near[...] = upward[...].astype(BF16)
+        far[: downward.shape[0], :] = downward[...].astype(BF16)
+
+
+def stage_parts(values, stage):
+    count = values.shape[0]
+    high = values.astype(BF16).astype(F32)
+    stage[:count, :] = high
+    stage[count : 2 * count, :] = values - high
+
+
+def stage_plane(values, stage, start):
     for i in range(DEG):
-        stage[2 * RIM + i * DEG : 2 * RIM + (i + 1) * DEG, :] = wide[i * FACE : i * FACE + DEG, :]
-    message[...] = stage[...].astype(BF16)
-
-
-def prepare(field_in, stiffness_in, field, ordered, own_columns, partial, message, stiffness, wide, stage, sems):
+        stage[start + i * DEG : start + (i + 1) * DEG, :] = values[i * FACE : i * FACE + DEG, :]
+
+
+def pack_x(partial, wide, far, near, upward, downward):
+    stage_parts(partial[OWN : OWN + RIM, :], upward)
+    stage_plane(wide, upward, 2 * RIM)
+    downward[...] = wide[:FACE, :]
+    send(lax.axis_index("core") == 1, far, near, upward, downward)
+
+
+def inside_x():
+    return (lax.axis_index("z") + lax.axis_index("half") + lax.axis_index("core") > 0).astype(F32)
+
+
+def inside_y():
+    return (lax.axis_index("gy") > 0).astype(F32)
+
+
+def prepare(
+    field_in, stiffness_in, field, ordered, own_columns, partial, far, near, stiffness, wide, upward, downward, sems
+):
     copies = [
         pltpu.make_async_copy(stiffness_in, stiffness, sems.at[0]),
         pltpu.make_async_copy(field_in, field, sems.at[1]),
@@ -109,7 +148,7 @@
     copies[1].wait()
     partial[...] = dot(own_columns[...], field[...])
     wide[...] = field[...].astype(F32)
-    pack_upward(partial, wide, message, stage)
+    pack_x(partial, wide, far, near, upward, downward)
 
 
 def split_matrix(ordered, own_x, rim_x, face_x, own_y, side_y, face_y, edge_y):
@@ -123,54 +162,64 @@
     edge_y[...] = ordered[OWN + FACE : OWN + RIM, to_y:].astype(BF16)
 
 
-def cross(inside, rim_x, face_x, partial, field, above_x, message, upward, downward, rim, wide, face, stage):
-    wide[...] = message[...].astype(F32)
-    rim[...] = wide[:RIM, :] + wide[RIM : 2 * RIM, :] + inside[0] * dot(rim_x[...], field[:FACE, :])
-    upward[...] = partial[OWN + RIM :, :] + dot(face_x[...], above_x[...])
-    upward[:DEG, :] += rim[FACE:, :]
-    face[...] = above_x[...].astype(F32)
-    stage[:DEG, :] = face[:DEG, :]
-    own = field[...].astype(F32)
-    for i in range(DEG):
-        stage[DEG + i * DEG : DEG + (i + 1) * DEG, :] = own[i * FACE : i * FACE + DEG, :]
-    stage[RIM:, :] = wide[2 * RIM :, :]
-    downward[...] = stage[...].astype(BF16)
-
-
-def gather_row(inside, own_x, face_y, edge_y, partial, field, above_x, rim, downward, own, corner, face):
+def cross(rim_x, face_x, partial, field, far_in, near_in, far, near, rim, above_x, raw, wide, face, upward, downward):
+    def arrived(below, above):
+        wide[...] = below[...].astype(F32)
+        face[...] = above[:FACE, :].astype(F32)
+
+    chosen(lax.axis_index("core") == 1, (far_in, near_in), arrived)
+    above_x[...] = face[...].astype(BF16)
+    rim[...] = wide[:RIM, :] + wide[RIM : 2 * RIM, :] + inside_x() * dot(rim_x[...], field[:FACE, :])
+    row = partial[OWN + RIM :, :] + dot(face_x[...], above_x[...])
+    wide[:FACE, :] = row
+    wide[:DEG, :] += rim[FACE:, :]
+    upward[...] = jnp.zeros_like(upward)
+    stage_parts(wide[:FACE, :], upward)
+    downward[:DEG, :] = face[:DEG, :]
+    stage_plane(field[...].astype(F32), downward, DEG)
+    downward[RIM:, :] = wide[2 * RIM :, :]
+    raw[...] = downward[...].astype(BF16)
+    send(lax.bitwise_and(lax.axis_index("gy"), 1) == 1, far, near, upward, downward)
+
+
+def gather_row(own_x, face_y, edge_y, partial, field, above_x, rim, raw, own, corner, face):
     own[...] = partial[:OWN, :] + dot(own_x[...], above_x[...])
     own[:FACE, :] += rim[:FACE, :]
-    face[...] = inside[1] * dot(face_y[...], downward[:RIM, :])
+    face[...] = inside_y() * dot(face_y[...], raw[:RIM, :])
     for i in range(DEG):
         own[i * FACE : i * FACE + DEG, :] += face[i * DEG : (i + 1) * DEG, :]
-    wide = downward[...].astype(F32)
+    wide = raw[...].astype(F32)
     corner[:DEG, :] = field[...].astype(F32)[:DEG]
     corner[DEG:, :] = wide[RIM:]
-    own[:DEG, :] += inside[0] * inside[1] * dot(edge_y[...], corner[...].astype(BF16))
-
-
-def close(inside, own_y, side_y, own, from_y, above_y, image, far):
-    wide = above_y[...].astype(F32)
-    far[:DEG, :] = wide[DEG : 2 * DEG]
-    far[DEG:, :] = wide[RIM:]
-    image[:OWN, :] = own[...] + dot(own_y[...], above_y[:RIM, :])
-    image[:FACE, :] += inside[0] * dot(side_y[...], far[...].astype(BF16))
+    own[:DEG, :] += inside_x() * inside_y() * dot(edge_y[...], corner[...].astype(BF16))
+
+
+def close(own_y, side_y, own, far_in, near_in, image, corner, face, wide):
+    def arrived(below, above):
+        parts = below[...].astype(F32)
+        face[...] = parts[:FACE, :] + parts[FACE : 2 * FACE, :]
+        wide[...] = above[...].astype(F32)
+
+    chosen(lax.bitwise_and(lax.axis_index("gy"), 1) == 1, (far_in, near_in), arrived)
+    corner[:DEG, :] = wide[DEG : 2 * DEG, :]
+    corner[DEG:, :] = wide[RIM:, :]
+    image[:OWN, :] = own[...] + dot(own_y[...], wide[:RIM, :].astype(BF16))
+    image[:FACE, :] += inside_x() * dot(side_y[...], corner[...].astype(BF16))
     for i in range(DEG):
-        image[i * FACE : i * FACE + DEG, :] += from_y[i * DEG : (i + 1) * DEG, :]
+        image[i * FACE : i * FACE + DEG, :] += face[i * DEG : (i + 1) * DEG, :]
 
 
 def lift(
-    inside, own_y, side_y, own, from_y, above_y, field, potential, own_columns,
-    lifted, partial, lowest, message, image, far, stage,
+    own_y, side_y, own, far_in, near_in, field, potential, own_columns,
+    lifted, partial, far, near, image, corner, face, wide, upward,
 ):
-    close(inside, own_y, side_y, own, from_y, above_y, image, far)
+    close(own_y, side_y, own, far_in, near_in, image, corner, face, wide)
     field32 = field[...].astype(F32)
     first_image = image[...] + potential[...] * field32
     image[...] = (first_image - SPECTRUM_CENTER * field32) / SPECTRUM_HALF
     lifted[...] = image[...].astype(BF16)
-    lowest[...] = image[:FACE, :].astype(BF16)
     partial[...] = dot(own_columns[...], lifted[...])
-    pack_upward(partial, image, message, stage)
+    pack_x(partial, image, far, near, upward, face)
 
 
 def solution(mesh):
@@ -180,11 +229,11 @@
     gx = ("z", "half", "core")
     every = gx + ("gy",)
 
-    def passed_x(value, by):
-        return lax.ppermute(value, gx, [(i, i + by) for i in range(length_x) if 0 <= i + by < length_x])
-
-    def passed_y(value, by):
-        return lax.ppermute(value, "gy", [(i, i + by) for i in range(length_y) if 0 <= i + by < length_y])
+    def swapped(far, near, axis, length):
+        def pairs(first):
+            return [(i + j, i + 1 - j) for i in range(first, length - 1, 2) for j in range(2)]
+
+        return lax.ppermute(far, axis, pairs(1)), lax.ppermute(near, axis, pairs(0))
 
     def per_device(orbitals, potential, cell_stiffness):
         node_count, orbital_count = orbitals.shape
@@ -202,27 +251,25 @@
             return tuple(pltpu.VMEM(by_orbital(n), F32) for n in rows)
 
         weight = potential[:, None]
-        inside = jnp.stack([lax.axis_index(gx), lax.axis_index("gy")])
-        inside = (inside > 0).astype(F32)
         message_rows = 2 * RIM + FACE
         raw_rows = RIM + FACE
 
-        above_x = passed_x(orbitals[:FACE], -1)
-        field, ordered, own_columns, partial, message = call(
+        field, ordered, own_columns, partial, far, near = call(
             prepare,
             (by_orbital(OWN), BF16),
             ((CELL, CELL), F32),
             ((CELL, OWN), BF16),
             (by_orbital(CELL), F32),
             (by_orbital(message_rows), BF16),
+            (by_orbital(message_rows), BF16),
             scratch=(
                 pltpu.VMEM((SIDE**3, SIDE**3), BF16),
-                *staged(OWN, message_rows),
+                *staged(OWN, message_rows, FACE),
                 pltpu.SemaphoreType.DMA((2,)),
             ),
             raw=(0, 1),
         )(orbitals, cell_stiffness)
-        message = passed_x(message, 1)
+        far, near = swapped(far, near, gx, length_x)
         own_x, rim_x, face_x, own_y, side_y, face_y, edge_y = call(
             split_matrix,
             ((OWN, FACE), BF16),
@@ -234,41 +281,39 @@
             ((DEG, RIM), BF16),
         )(ordered)
 
-        def row_part(partial, values, above_x, message):
-            upward, downward, rim = call(
+        def row_part(partial, values, far, near):
+            far, near, rim, above_x, raw = call(
                 cross,
-                (by_orbital(FACE), F32),
+                (by_orbital(raw_rows), BF16),
                 (by_orbital(raw_rows), BF16),
                 (by_orbital(RIM), F32),
-                scratch=staged(message_rows, FACE, raw_rows),
-                scalar=(0,),
-            )(inside, rim_x, face_x, partial, values, above_x, message)
-            from_y = passed_y(upward, 1)
-            above_y = passed_y(downward, -1)
-            own = call(gather_row, (by_orbital(OWN), F32), scratch=staged(RIM, FACE), scalar=(0,))(
-                inside, own_x, face_y, edge_y, partial, values, above_x, rim, downward
+                (by_orbital(FACE), BF16),
+                (by_orbital(raw_rows), BF16),
+                scratch=staged(message_rows, FACE, raw_rows, raw_rows),
+            )(rim_x, face_x, partial, values, far, near)
+            far, near = swapped(far, near, "gy", length_y)
+            own = call(gather_row, (by_orbital(OWN), F32), scratch=staged(RIM, FACE))(
+                own_x, face_y, edge_y, partial, values, above_x, rim, raw
             )[0]
-            return own, from_y, above_y
-
-        own, from_y, above_y = row_part(partial, field, above_x, message)
-        lifted, partial, lowest, message = call(
+            return own, far, near
+
+        own, far, near = row_part(partial, field, far, near)
+        lifted, partial, far, near = call(
             lift,
             (by_orbital(OWN), BF16),
             (by_orbital(CELL), F32),
-            (by_orbital(FACE), BF16),
             (by_orbital(message_rows), BF16),
-            scratch=staged(OWN, RIM, message_rows),
-            scalar=(0,),
-        )(inside, own_y, side_y, own, from_y, above_y, field, weight, own_columns)
-        above_x = passed_x(lowest, -1)
-        message = passed_x(message, 1)
-        own, from_y, above_y = row_part(partial, lifted, above_x, message)
+            (by_orbital(message_rows), BF16),
+            scratch=staged(OWN, RIM, FACE, raw_rows, message_rows),
+        )(own_y, side_y, own, far, near, field, weight, own_columns)
+        far, near = swapped(far, near, gx, length_x)
+        own, far, near = row_part(partial, lifted, far, near)
 
         def filter_and_gram(
-            inside, own_y, side_y, own, from_y, above_y, field, lifted, potential,
-            filtered, out, image, far, rows,
+            own_y, side_y, own, far_in, near_in, field, lifted, potential,
+            filtered, out, image, corner, face, wide, rows,
         ):
-            close(inside, own_y, side_y, own, from_y, above_y, image, far)
+            close(own_y, side_y, own, far_in, near_in, image, corner, face, wide)
             image[OWN:, :] = jnp.zeros((padded - OWN, orbital_count), F32)
             rows[OWN:, :] = jnp.zeros((padded - OWN, orbital_count), F32)
             rows[:OWN, :] = lifted[...].astype(F32)
@@ -304,10 +349,9 @@
             filter_and_gram,
             (by_orbital(OWN), BF16),
             ((2, 2, orbital_count, half), BF16),
-            scratch=staged(padded, RIM, padded),
+            scratch=staged(padded, RIM, FACE, raw_rows, padded),
             results=(0,),
-            scalar=(0,),
-        )(inside, own_y, side_y, own, from_y, above_y, field, lifted, weight)
+        )(own_y, side_y, own, far, near, field, lifted, weight)
 
         def pair_sum(terms, out):
             for which in range(2):

time: 128 us -> 125 us (0.977)
  starting transfers between devices: 32.2 us -> 36.4 us
  blocking collectives: 70.7 us -> 66.7 us
  Pallas kernels: 10.2 us -> 7.22 us
    all_to_all x1, blocking collectives: 33.9 us -> 28.4 us  [per_device(): terms = lax.all_to_all(terms, ('half', 'gy'), 0, 0, tiled=True)]
    ppermute x8, starting transfers between devices: 32.2 us -> 36.4 us  [the longest x4 20 us: swapped(): lax.ppermute(near, axis, pairs(0))]
    pallas_call x11, Pallas kernels: 10.2 us -> 7.22 us  [run(): pl.pallas_call(kernel, out_shape=[jax.ShapeDtypeStruct(*shape) if i in re...]
    all_to_all x1, blocking collectives: 32.6 us -> 34.1 us  [per_device(): terms = lax.all_to_all(terms, 'z', 0, 0, tiled=True)]
  transfers between devices with their start and end apart: 8 -> 8, of which waited for: 5 -> 4; matrix products, arithmetic and copies ran while one was open for 1% -> 0% of each run, Pallas kernels for 1% -> 1%
where the time goes in v3:
time: 125 us; the launch traced here: 123 us
  blocking collectives  66.7 us (53%)
  starting transfers between devices  36.4 us (29%)
  waiting for transfers between devices  12.1 us (10%)
  Pallas kernels  7.22 us (6%)
    all_to_all x1, blocking collectives, per_device(): terms = lax.all_to_all(terms, 'z', 0, 0, tiled=True)  34.1 us
    all_to_all x1, blocking collectives, per_device(): terms = lax.all_to_all(terms, ('half', 'gy'), 0, 0, tiled=True)  28.4 us
    ppermute x4, starting transfers between devices, swapped(): lax.ppermute(near, axis, pairs(0))  20 us
    ppermute x4, starting transfers between devices, swapped(): lax.ppermute(far, axis, pairs(1))  16.4 us
    ppermute x4, waiting for transfers between devices, swapped(): lax.ppermute(near, axis, pairs(0))  9.49 us
    pallas_call x11, Pallas kernels, run(): pl.pallas_call(kernel, out_shape=[jax.ShapeDtypeStruct(*shape) if i in re...  7.22 us
    all_to_all x1, blocking collectives, per_device(): terms = lax.all_to_all(terms, 'core', 0, 0, tiled=True)  4.21 us
    ppermute x4, waiting for transfers between devices, swapped(): lax.ppermute(far, axis, pairs(1))  2.59 us
  transfers between devices with their start and end apart: 8, of which 4 were waited for; matrix products, arithmetic and copies ran while one was open for 0% of the time, Pallas kernels for 1%

profile of v3, /device:TPU:1, one launch (start us, length us, event | category | flops | bytes accessed | tf_op | source)
XLA Modules:
  0.0 123.4 jit_solution(1817319714774824756)
XLA Ops:
  0.6 2.2 %prepare.1 = (bf16[343,512]{1,0:T(8,128)(2,1)S(1)}, f32[448,448]{1,0:T(8,128)S(1)}, bf16[448,343]{1,0:T(8,128)(2,1)S(1)}, f32[448,512]{1,0:T(8,128)S(1)}, bf16[1...) custom-call(bf16[343,512]{1,0:T(8,128)(2,1)} %field_in.1, bf16[512,512]{1,0:T(8,128)(2,1)} %stiffness_in.1), custom_call_target="tpu_custom_call" | custom-call | tf_op jit(solution)/shard_map/prepare/pallas_call | solution.py:64
  2.8 8.8 %collective-permute-start = (bf16[161,512]{1,0:T(8,128)(2,1)S(1)}, bf16[161,512]{1,0:T(8,128)(2,1)S(1)}, u32[]{:S(2)}, u32[]{:S(2)}) collective-permute-start(bf16[161,512]{1,0:T(8,128)(2,1)S(1)} %get-tuple-element.44), channel_id=1, source_target_pairs={{16,32},{32,16},{48,64},{64,48},{80,96},{96,80},{112,128},{128,112... | collective-permute-start | bytes 494600 | tf_op jit(solution)/shard_map/ppermute | solution.py:236
  11.6 7.9 %collective-permute-start.1 = (bf16[161,512]{1,0:T(8,128)(2,1)S(1)}, bf16[161,512]{1,0:T(8,128)(2,1)S(1)}, u32[]{:S(2)}, u32[]{:S(2)}) collective-permute-start(bf16[161,512]{1,0:T(8,128)(2,1)S(1)} %get-tuple-element.45), channel_id=1, source_target_pairs={{0,16},{16,0},{32,48},{48,32},{64,80},{80,64},{96,112},{112,96},{1... | collective-permute-start | bytes 494600 | tf_op jit(solution)/shard_map/ppermute | solution.py:236
  19.5 0.2 split_matrix.1
  19.7 0.0 collective-permute-done.far_in
  19.7 0.8 collective-permute-done.1.near_in
  20.5 0.3 cross.2
  20.8 0.0 copy-start
  20.8 0.7 collective-permute-start.2
  21.5 3.1 %collective-permute-start.3 = (bf16[105,512]{1,0:T(8,128)(2,1)S(1)}, bf16[105,512]{1,0:T(8,128)(2,1)S(1)}, u32[]{:S(2)}, u32[]{:S(2)}) collective-permute-start(bf16[105,512]{1,0:T(8,128)(2,1)S(1)} %get-tuple-element.50), channel_id=1, source_target_pairs={{0,1},{1,0},{2,3},{3,2},{4,5},{5,4},{6,7},{7,6},{8,9},{9,8},{10,11... | collective-permute-start | bytes 322568 | tf_op jit(solution)/shard_map/ppermute | solution.py:236
  24.6 0.1 broadcast_in_dim.4.potential
  24.8 0.3 gather_row.2.own
  25.0 0.0 collective-permute-done.2.far_in
  25.0 4.3 %collective-permute-done.3.near_in = bf16[105,512]{1,0:T(8,128)(2,1)S(1)} collective-permute-done((bf16[105,512]{1,0:T(8,128)(2,1)S(1)}, bf16[105,512]{1,0:T(8,128)(2,1)S(1)}, u32[]{:S(2)}, u32[]{:S(2)}) %collective-permute-start.3) | collective-permute-done | bytes 107552 | tf_op jit(solution)/shard_map/ppermute | solution.py:236
  29.3 0.9 lift.1
  30.2 6.2 %collective-permute-start.4 = (bf16[161,512]{1,0:T(8,128)(2,1)S(1)}, bf16[161,512]{1,0:T(8,128)(2,1)S(1)}, u32[]{:S(2)}, u32[]{:S(2)}) collective-permute-start(bf16[161,512]{1,0:T(8,128)(2,1)S(1)} %get-tuple-element.54), channel_id=1, source_target_pairs={{16,32},{32,16},{48,64},{64,48},{80,96},{96,80},{112,128},{128,112... | collective-permute-start | bytes 494600 | tf_op jit(solution)/shard_map/ppermute | solution.py:236
  36.4 1.9 %collective-permute-start.5 = (bf16[161,512]{1,0:T(8,128)(2,1)S(1)}, bf16[161,512]{1,0:T(8,128)(2,1)S(1)}, u32[]{:S(2)}, u32[]{:S(2)}) collective-permute-start(bf16[161,512]{1,0:T(8,128)(2,1)S(1)} %get-tuple-element.55), channel_id=1, source_target_pairs={{0,16},{16,0},{32,48},{48,32},{64,80},{80,64},{96,112},{112,96},{1... | collective-permute-start | bytes 494600 | tf_op jit(solution)/shard_map/ppermute | solution.py:236
  38.3 2.6 %collective-permute-done.4.far_in = bf16[161,512]{1,0:T(8,128)(2,1)S(1)} collective-permute-done((bf16[161,512]{1,0:T(8,128)(2,1)S(1)}, bf16[161,512]{1,0:T(8,128)(2,1)S(1)}, u32[]{:S(2)}, u32[]{:S(2)}) %collective-permute-start.4) | collective-permute-done | bytes 164896 | tf_op jit(solution)/shard_map/ppermute | solution.py:236
  40.9 0.0 collective-permute-done.5.near_in
  40.9 0.3 cross.3
  41.2 0.7 collective-permute-start.6
  41.9 7.1 %collective-permute-start.7 = (bf16[105,512]{1,0:T(8,128)(2,1)S(1)}, bf16[105,512]{1,0:T(8,128)(2,1)S(1)}, u32[]{:S(2)}, u32[]{:S(2)}) collective-permute-start(bf16[105,512]{1,0:T(8,128)(2,1)S(1)} %get-tuple-element.60), channel_id=1, source_target_pairs={{0,1},{1,0},{2,3},{3,2},{4,5},{5,4},{6,7},{7,6},{8,9},{9,8},{10,11... | collective-permute-start | bytes 322568 | tf_op jit(solution)/shard_map/ppermute | solution.py:236
  49.0 0.3 gather_row.3.own
  49.2 0.0 collective-permute-done.6.far_in
  49.2 4.4 %collective-permute-done.7.near_in = bf16[105,512]{1,0:T(8,128)(2,1)S(1)} collective-permute-done((bf16[105,512]{1,0:T(8,128)(2,1)S(1)}, bf16[105,512]{1,0:T(8,128)(2,1)S(1)}, u32[]{:S(2)}, u32[]{:S(2)}) %collective-permute-start.7) | collective-permute-done | bytes 107552 | tf_op jit(solution)/shard_map/ppermute | solution.py:236
  53.7 1.9 %filter_and_gram.1 = (bf16[343,512]{1,0:T(8,128)(2,1)}, bf16[2,2,512,256]{3,2,1,0:T(8,128)(2,1)S(1)}) custom-call(bf16[343,56]{1,0:T(8,128)(2,1)S(1)} %get-tuple-element.35.own_y, bf16[49,56]{1,0:T(8,128)(2,1)S(1)} %get-tuple-element.36.side_y, f32[343,512]{1,0:T(8,128)S(1)} %gather_row.3.own, bf16[105,512]{1,0:T(8,128)(2,1)S(1)} %collective-permute-done.6.far_in, ...), custom_call_target="tpu_custom_call" | custom-call | tf_op jit(solution)/shard_map/filter_and_gram/pallas_call | solution.py:64
  55.5 4.2 %all_to_all.15.terms = bf16[2,2,512,256]{3,2,1,0:T(8,128)(2,1)S(1)} all-to-all(bf16[2,2,512,256]{3,2,1,0:T(8,128)(2,1)S(1)} %get-tuple-element.62), channel_id=1, replica_groups=mesh['z'=16,'half'=2,'core'=2,'gy'=16] {'core'}, dimensions={0} | all-to-all | bytes 2097152 | tf_op jit(solution)/shard_map/all_to_all | solution.py:387
  59.8 0.1 pair_sum.1
  59.9 28.4 %all_to_all.16.terms = bf16[32,64,128]{2,1,0:T(8,128)(2,1)S(1)} all-to-all(bf16[32,64,128]{2,1,0:T(8,128)(2,1)S(1)} %bitcast.1), channel_id=1, replica_groups=mesh['z'=16,'half'=2,'core'=2,'gy'=16] {'half','gy'}, dimensions={0} | all-to-all | bytes 1048576 | tf_op jit(solution)/shard_map/all_to_all | solution.py:390
  88.3 0.2 plane_sum.1
  88.6 34.1 %all_to_all.17.terms = f32[16,4,128]{2,1,0:T(4,128)S(1)} all-to-all(f32[16,4,128]{2,1,0:T(4,128)S(1)} %plane_sum.1), channel_id=1, replica_groups=mesh['z'=16,'half'=2,'core'=2,'gy'=16] {'z'}, dimensions={0} | all-to-all | bytes 65536 | tf_op jit(solution)/shard_map/all_to_all | solution.py:392
  122.7 0.7 line_sum.1
  (1 shorter events, 0.0 us)
Async XLA Ops:
  2.8 16.9 %collective-permute-start = (bf16[161,512]{1,0:T(8,128)(2,1)S(1)}, bf16[161,512]{1,0:T(8,128)(2,1)S(1)}, u32[]{:S(2)}, u32[]{:S(2)}) collective-permute-start(bf16[161,512]{1,0:T(8,128)(2,1)S(1)} %get-tuple-element.44), channel_id=1, source_target_pairs={{16,32},{32,16},{48,64},{64,48},{80,96},{96,80},{112,128},{128,112... | collective-permute-start | bytes 494600 | tf_op jit(solution)/shard_map/ppermute | solution.py:236
  11.6 8.9 %collective-permute-start.1 = (bf16[161,512]{1,0:T(8,128)(2,1)S(1)}, bf16[161,512]{1,0:T(8,128)(2,1)S(1)}, u32[]{:S(2)}, u32[]{:S(2)}) collective-permute-start(bf16[161,512]{1,0:T(8,128)(2,1)S(1)} %get-tuple-element.45), channel_id=1, source_target_pairs={{0,16},{16,0},{32,48},{48,32},{64,80},{80,64},{96,112},{112,96},{1... | collective-permute-start | bytes 494600 | tf_op jit(solution)/shard_map/ppermute | solution.py:236
  20.8 3.8 %copy-start = (f32[343]{0:T(512)S(1)}, f32[343]{0:T(512)}, u32[]{:S(2)}) copy-start(f32[343]{0:T(512)} %param.4) | copy-start | bytes 4120
  20.8 4.2 %collective-permute-start.2 = (bf16[105,512]{1,0:T(8,128)(2,1)S(1)}, bf16[105,512]{1,0:T(8,128)(2,1)S(1)}, u32[]{:S(2)}, u32[]{:S(2)}) collective-permute-start(bf16[105,512]{1,0:T(8,128)(2,1)S(1)} %get-tuple-element.49), channel_id=1, source_target_pairs={{1,2},{2,1},{3,4},{4,3},{5,6},{6,5},{7,8},{8,7},{9,10},{10,9},{11,... | collective-permute-start | bytes 322568 | tf_op jit(solution)/shard_map/ppermute | solution.py:236
  21.5 7.8 %collective-permute-start.3 = (bf16[105,512]{1,0:T(8,128)(2,1)S(1)}, bf16[105,512]{1,0:T(8,128)(2,1)S(1)}, u32[]{:S(2)}, u32[]{:S(2)}) collective-permute-start(bf16[105,512]{1,0:T(8,128)(2,1)S(1)} %get-tuple-element.50), channel_id=1, source_target_pairs={{0,1},{1,0},{2,3},{3,2},{4,5},{5,4},{6,7},{7,6},{8,9},{9,8},{10,11... | collective-permute-start | bytes 322568 | tf_op jit(solution)/shard_map/ppermute | solution.py:236
  30.2 10.7 %collective-permute-start.4 = (bf16[161,512]{1,0:T(8,128)(2,1)S(1)}, bf16[161,512]{1,0:T(8,128)(2,1)S(1)}, u32[]{:S(2)}, u32[]{:S(2)}) collective-permute-start(bf16[161,512]{1,0:T(8,128)(2,1)S(1)} %get-tuple-element.54), channel_id=1, source_target_pairs={{16,32},{32,16},{48,64},{64,48},{80,96},{96,80},{112,128},{128,112... | collective-permute-start | bytes 494600 | tf_op jit(solution)/shard_map/ppermute | solution.py:236
  36.4 4.5 %collective-permute-start.5 = (bf16[161,512]{1,0:T(8,128)(2,1)S(1)}, bf16[161,512]{1,0:T(8,128)(2,1)S(1)}, u32[]{:S(2)}, u32[]{:S(2)}) collective-permute-start(bf16[161,512]{1,0:T(8,128)(2,1)S(1)} %get-tuple-element.55), channel_id=1, source_target_pairs={{0,16},{16,0},{32,48},{48,32},{64,80},{80,64},{96,112},{112,96},{1... | collective-permute-start | bytes 494600 | tf_op jit(solution)/shard_map/ppermute | solution.py:236
  41.2 8.1 %collective-permute-start.6 = (bf16[105,512]{1,0:T(8,128)(2,1)S(1)}, bf16[105,512]{1,0:T(8,128)(2,1)S(1)}, u32[]{:S(2)}, u32[]{:S(2)}) collective-permute-start(bf16[105,512]{1,0:T(8,128)(2,1)S(1)} %get-tuple-element.59), channel_id=1, source_target_pairs={{1,2},{2,1},{3,4},{4,3},{5,6},{6,5},{7,8},{8,7},{9,10},{10,9},{11,... | collective-permute-start | bytes 322568 | tf_op jit(solution)/shard_map/ppermute | solution.py:236
  41.9 11.8 %collective-permute-start.7 = (bf16[105,512]{1,0:T(8,128)(2,1)S(1)}, bf16[105,512]{1,0:T(8,128)(2,1)S(1)}, u32[]{:S(2)}, u32[]{:S(2)}) collective-permute-start(bf16[105,512]{1,0:T(8,128)(2,1)S(1)} %get-tuple-element.60), channel_id=1, source_target_pairs={{0,1},{1,0},{2,3},{3,2},{4,5},{5,4},{6,7},{7,6},{8,9},{9,8},{10,11... | collective-permute-start | bytes 322568 | tf_op jit(solution)/shard_map/ppermute | solution.py:236

commit v4 on v3

--- a/solution.py
+++ b/solution.py
@@ -6,6 +6,7 @@
 from jax.experimental import pallas as pl
 from jax.experimental.pallas import tpu as pltpu
 from jax.sharding import Mesh, PartitionSpec as P
+
 
 DEG = 7
 SIDE = DEG + 1
@@ -36,8 +37,8 @@
     return (column == lax.broadcasted_iota(jnp.int32, (column.shape[0], width), 1)).astype(F32).astype(BF16)
 
 
-def node_order():
-    place = lax.broadcasted_iota(jnp.int32, (CELL, 1), 0)
+def node_order(first, count):
+    place = first + lax.broadcasted_iota(jnp.int32, (count, 1), 0)
 
     def seventh(n):
         return lax.shift_right_logical(n * 9363, 16)
@@ -70,7 +71,6 @@
             out_specs=[vmem] * len(shapes),
             scratch_shapes=list(scratch),
             compiler_params=pltpu.CompilerParams(vmem_limit_bytes=VMEM_LIMIT),
-            name=kernel.__name__,
         )(
             *[
                 pltpu.with_memory_space_constraint(arg, pltpu.HBM if i in raw else pltpu.VMEM)
@@ -117,9 +117,9 @@
         stage[start + i * DEG : start + (i + 1) * DEG, :] = values[i * FACE : i * FACE + DEG, :]
 
 
-def pack_x(partial, wide, far, near, upward, downward):
-    stage_parts(partial[OWN : OWN + RIM, :], upward)
-    stage_plane(wide, upward, 2 * RIM)
+def pack_x(rim, wide, far, near, upward, downward):
+    upward[:RIM, :] = rim
+    stage_plane(wide, upward, RIM)
     downward[...] = wide[:FACE, :]
     send(lax.axis_index("core") == 1, far, near, upward, downward)
 
@@ -132,26 +132,27 @@
     return (lax.axis_index("gy") > 0).astype(F32)
 
 
-def prepare(
-    field_in, stiffness_in, field, ordered, own_columns, partial, far, near, stiffness, wide, upward, downward, sems
-):
+def prepare(field_in, stiffness_in, field, stiffness, rim_own, far, near, wide, upward, downward, sems):
     copies = [
         pltpu.make_async_copy(stiffness_in, stiffness, sems.at[0]),
         pltpu.make_async_copy(field_in, field, sems.at[1]),
     ]
     for copy in copies:
         copy.start()
-    order = one_hot(node_order(), SIDE**3)
+    nodes = one_hot(node_order(0, OWN), SIDE**3)
+    rim = one_hot(node_order(OWN, RIM), SIDE**3)
     copies[0].wait()
+    rim_own[...] = dot_columns(dot(rim, stiffness[...]).astype(BF16), nodes).astype(BF16)
+    copies[1].wait()
+    wide[...] = field[...].astype(F32)
+    pack_x(dot(rim_own[...], field[...]), wide, far, near, upward, downward)
+
+
+def arrange(stiffness, field, own_columns, partial, own_x, rim_x, face_x, own_y, side_y, face_y, edge_y, ordered):
+    order = one_hot(node_order(0, CELL), SIDE**3)
     ordered[...] = dot_columns(dot(order, stiffness[...]).astype(BF16), order)
     own_columns[...] = ordered[:, :OWN].astype(BF16)
-    copies[1].wait()
     partial[...] = dot(own_columns[...], field[...])
-    wide[...] = field[...].astype(F32)
-    pack_x(partial, wide, far, near, upward, downward)
-
-
-def split_matrix(ordered, own_x, rim_x, face_x, own_y, side_y, face_y, edge_y):
     to_x, to_y = OWN, OWN + FACE
     own_x[...] = ordered[:OWN, to_x:to_y].astype(BF16)
     rim_x[...] = ordered[OWN : OWN + RIM, to_x:to_y].astype(BF16)
@@ -162,6 +163,10 @@
     edge_y[...] = ordered[OWN + FACE : OWN + RIM, to_y:].astype(BF16)
 
 
+def multiply(own_columns, field, partial):
+    partial[...] = dot(own_columns[...], field[...])
+
+
 def cross(rim_x, face_x, partial, field, far_in, near_in, far, near, rim, above_x, raw, wide, face, upward, downward):
     def arrived(below, above):
         wide[...] = below[...].astype(F32)
@@ -169,15 +174,15 @@
 
     chosen(lax.axis_index("core") == 1, (far_in, near_in), arrived)
     above_x[...] = face[...].astype(BF16)
-    rim[...] = wide[:RIM, :] + wide[RIM : 2 * RIM, :] + inside_x() * dot(rim_x[...], field[:FACE, :])
+    rim[...] = wide[:RIM, :] + inside_x() * dot(rim_x[...], field[:FACE, :])
     row = partial[OWN + RIM :, :] + dot(face_x[...], above_x[...])
+    downward[:DEG, :] = face[:DEG, :]
+    stage_plane(field[...].astype(F32), downward, DEG)
+    downward[RIM:, :] = wide[RIM:, :]
     wide[:FACE, :] = row
     wide[:DEG, :] += rim[FACE:, :]
     upward[...] = jnp.zeros_like(upward)
     stage_parts(wide[:FACE, :], upward)
-    downward[:DEG, :] = face[:DEG, :]
-    stage_plane(field[...].astype(F32), downward, DEG)
-    downward[RIM:, :] = wide[2 * RIM :, :]
     raw[...] = downward[...].astype(BF16)
     send(lax.bitwise_and(lax.axis_index("gy"), 1) == 1, far, near, upward, downward)
 
@@ -210,16 +215,15 @@
 
 
 def lift(
-    own_y, side_y, own, far_in, near_in, field, potential, own_columns,
-    lifted, partial, far, near, image, corner, face, wide, upward,
+    own_y, side_y, own, far_in, near_in, field, potential, rim_own,
+    lifted, far, near, image, corner, face, wide, upward,
 ):
     close(own_y, side_y, own, far_in, near_in, image, corner, face, wide)
     field32 = field[...].astype(F32)
     first_image = image[...] + potential[...] * field32
     image[...] = (first_image - SPECTRUM_CENTER * field32) / SPECTRUM_HALF
     lifted[...] = image[...].astype(BF16)
-    partial[...] = dot(own_columns[...], lifted[...])
-    pack_x(partial, image, far, near, upward, face)
+    pack_x(dot(rim_own[...], lifted[...]), image, far, near, upward, face)
 
 
 def solution(mesh):
@@ -251,27 +255,24 @@
             return tuple(pltpu.VMEM(by_orbital(n), F32) for n in rows)
 
         weight = potential[:, None]
-        message_rows = 2 * RIM + FACE
-        raw_rows = RIM + FACE
-
-        field, ordered, own_columns, partial, far, near = call(
+        message_rows = RIM + FACE
+        message = (by_orbital(message_rows), BF16)
+
+        field, stiffness, rim_own, far, near = call(
             prepare,
             (by_orbital(OWN), BF16),
-            ((CELL, CELL), F32),
-            ((CELL, OWN), BF16),
-            (by_orbital(CELL), F32),
-            (by_orbital(message_rows), BF16),
-            (by_orbital(message_rows), BF16),
-            scratch=(
-                pltpu.VMEM((SIDE**3, SIDE**3), BF16),
-                *staged(OWN, message_rows, FACE),
-                pltpu.SemaphoreType.DMA((2,)),
-            ),
+            ((SIDE**3, SIDE**3), BF16),
+            ((RIM, OWN), BF16),
+            message,
+            message,
+            scratch=(*staged(OWN, message_rows, FACE), pltpu.SemaphoreType.DMA((2,))),
             raw=(0, 1),
         )(orbitals, cell_stiffness)
         far, near = swapped(far, near, gx, length_x)
-        own_x, rim_x, face_x, own_y, side_y, face_y, edge_y = call(
-            split_matrix,
+        own_columns, partial, own_x, rim_x, face_x, own_y, side_y, face_y, edge_y = call(
+            arrange,
+            ((CELL, OWN), BF16),
+            (by_orbital(CELL), F32),
             ((OWN, FACE), BF16),
             ((RIM, FACE), BF16),
             ((FACE, FACE), BF16),
@@ -279,17 +280,18 @@
             ((FACE, RIM), BF16),
             ((FACE, RIM), BF16),
             ((DEG, RIM), BF16),
-        )(ordered)
+            scratch=(pltpu.VMEM((CELL, CELL), F32),),
+        )(stiffness, field)
 
         def row_part(partial, values, far, near):
             far, near, rim, above_x, raw = call(
                 cross,
-                (by_orbital(raw_rows), BF16),
-                (by_orbital(raw_rows), BF16),
+                message,
+                message,
                 (by_orbital(RIM), F32),
                 (by_orbital(FACE), BF16),
-                (by_orbital(raw_rows), BF16),
-                scratch=staged(message_rows, FACE, raw_rows, raw_rows),
+                message,
+                scratch=staged(message_rows, FACE, message_rows, message_rows),
             )(rim_x, face_x, partial, values, far, near)
             far, near = swapped(far, near, "gy", length_y)
             own = call(gather_row, (by_orbital(OWN), F32), scratch=staged(RIM, FACE))(
@@ -298,27 +300,18 @@
             return own, far, near
 
         own, far, near = row_part(partial, field, far, near)
-        lifted, partial, far, near = call(
+        lifted, far, near = call(
             lift,
             (by_orbital(OWN), BF16),
-            (by_orbital(CELL), F32),
-            (by_orbital(message_rows), BF16),
-            (by_orbital(message_rows), BF16),
-            scratch=staged(OWN, RIM, FACE, raw_rows, message_rows),
-        )(own_y, side_y, own, far, near, field, weight, own_columns)
+            message,
+            message,
+            scratch=staged(OWN, RIM, FACE, message_rows, message_rows),
+        )(own_y, side_y, own, far, near, field, weight, rim_own)
         far, near = swapped(far, near, gx, length_x)
+        partial = call(multiply, (by_orbital(CELL), F32))(own_columns, lifted)[0]
         own, far, near = row_part(partial, lifted, far, near)
 
-        def filter_and_gram(
-            own_y, side_y, own, far_in, near_in, field, lifted, potential,
-            filtered, out, image, corner, face, wide, rows,
-        ):
-            close(own_y, side_y, own, far_in, near_in, image, corner, face, wide)
-            image[OWN:, :] = jnp.zeros((padded - OWN, orbital_count), F32)
-            rows[OWN:, :] = jnp.zeros((padded - OWN, orbital_count), F32)
-            rows[:OWN, :] = lifted[...].astype(F32)
-            lifted32 = rows[:OWN, :]
-            image[:OWN, :] += potential[...] * lifted32
+        def shuffle():
             place = lax.broadcasted_iota(jnp.int32, (orbital_count, 1), 0)
             low = lax.bitwise_and(place, quarter - 1)
             line = lax.shift_right_logical(low, block_rows.bit_length() - 1)
@@ -329,33 +322,68 @@
                 + lax.shift_right_logical(side, 1) * block_rows
                 + lax.bitwise_and(low, block_rows - 1)
             )
-            shuffle = one_hot(order, orbital_count)
-
-            def gram(which, left, right):
-                shuffled = dot_columns(right, shuffle).astype(BF16)
-                product = (dot_rows(left, shuffled) * norm_scale).astype(BF16)
-                out[0, which] = product[:, :half]
-                out[1, which] = product[:, half:]
-
-            gram(0, image[...].astype(BF16), rows[...].astype(BF16))
-            image[:OWN, :] = (
-                2.0 * (image[:OWN, :] - SPECTRUM_CENTER * lifted32) / SPECTRUM_HALF - field[...].astype(F32)
+            return one_hot(order, orbital_count)
+
+        def gram(left, right, keep, give):
+            shuffled = dot_columns(right, shuffle()).astype(BF16)
+            product = (dot_rows(left, shuffled) * norm_scale).astype(BF16)
+            core = lax.axis_index("core")
+
+            @pl.when(core == 0)
+            def _():
+                keep[...] = product[:, :half]
+                give[...] = product[:, half:]
+
+            @pl.when(core == 1)
+            def _():
+                keep[...] = product[:, half:]
+                give[...] = product[:, :half]
+
+        def image_gram(
+            own_y, side_y, own, far_in, near_in, lifted, potential,
+            second_image, keep, give, image, corner, face, wide, rows,
+        ):
+            close(own_y, side_y, own, far_in, near_in, image, corner, face, wide)
+            image[OWN:, :] = jnp.zeros((padded - OWN, orbital_count), F32)
+            rows[OWN:, :] = jnp.zeros((padded - OWN, orbital_count), F32)
+            rows[:OWN, :] = lifted[...].astype(F32)
+            image[:OWN, :] += potential[...] * rows[:OWN, :]
+            second_image[...] = image[:OWN, :]
+            gram(image[...].astype(BF16), rows[...].astype(BF16), keep, give)
+
+        def filter_gram(second_image, field, lifted, filtered, keep, give, rows):
+            rows[OWN:, :] = jnp.zeros((padded - OWN, orbital_count), F32)
+            rows[:OWN, :] = (
+                2.0 * (second_image[...] - SPECTRUM_CENTER * lifted[...].astype(F32)) / SPECTRUM_HALF
+                - field[...].astype(F32)
             )
-            filtered[...] = image[:OWN, :].astype(BF16)
-            values = image[...].astype(BF16)
-            gram(1, values, values)
-
-        filtered, terms = call(
-            filter_and_gram,
+            filtered[...] = rows[:OWN, :].astype(BF16)
+            values = rows[...].astype(BF16)
+            gram(values, values, keep, give)
+
+        half_gram = ((orbital_count, half), BF16)
+        pair = [(0, 1), (1, 0)]
+        second_image, ham_kept, ham_given = call(
+            image_gram,
+            (by_orbital(OWN), F32),
+            half_gram,
+            half_gram,
+            scratch=staged(padded, RIM, FACE, message_rows, padded),
+        )(own_y, side_y, own, far, near, lifted, weight)
+        ham_taken = lax.ppermute(ham_given, "core", pair)
+        filtered, kept, given = call(
+            filter_gram,
             (by_orbital(OWN), BF16),
-            ((2, 2, orbital_count, half), BF16),
-            scratch=staged(padded, RIM, FACE, raw_rows, padded),
+            half_gram,
+            half_gram,
+            scratch=staged(padded),
             results=(0,),
-        )(own_y, side_y, own, far, near, field, lifted, weight)
-
-        def pair_sum(terms, out):
-            for which in range(2):
-                total = (terms[0, which].astype(F32) + terms[1, which].astype(F32)).astype(BF16)
+        )(second_image, field, lifted)
+        taken = lax.ppermute(given, "core", pair)
+
+        def pair_sum(ham_kept, ham_taken, kept, taken, out):
+            for which, (mine, other) in enumerate(((ham_kept, ham_taken), (kept, taken))):
+                total = (mine[...].astype(F32) + other[...].astype(F32)).astype(BF16)
                 for side in range(2):
                     part = total[:, side * quarter : (side + 1) * quarter]
                     for j in range(length_y):
@@ -384,8 +412,7 @@
                 ham[part * short : (part + 1) * short, :] = block[:, :block_cols]
                 correlation[part * short : (part + 1) * short, :] = block[:, block_cols:]
 
-        terms = lax.all_to_all(terms, "core", 0, 0, tiled=True)
-        terms = call(pair_sum, ((2, length_y, wide, quarter), BF16))(terms)[0]
+        terms = call(pair_sum, ((2, length_y, wide, quarter), BF16))(ham_kept, ham_taken, kept, taken)[0]
         terms = terms.reshape(2 * length_y, wide, quarter)
         terms = lax.all_to_all(terms, ("half", "gy"), 0, 0, tiled=True)
         terms = call(plane_sum, ((length_z, short, fold * wide), F32))(terms)[0]

time: 125 us -> 120 us (0.960)
  blocking collectives: 66.7 us -> 59.1 us
  starting transfers between devices: 36.4 us -> 39.7 us
  Pallas kernels: 7.22 us -> 8.81 us
    ppermute x0 -> x2, starting transfers between devices: none -> 4.31 us  [the longest x1 2.27 us: per_device(): ham_taken = lax.ppermute(ham_given, 'core', pair)]
    all_to_all x1 -> x0, blocking collectives: 4.21 us -> none  [per_device(): terms = lax.all_to_all(terms, 'core', 0, 0, tiled=True)]
    all_to_all x1, blocking collectives: 34.1 us -> 31.6 us  [per_device(): terms = lax.all_to_all(terms, 'z', 0, 0, tiled=True)]
    ppermute x4, waiting for transfers between devices: 2.59 us -> 0.66 us  [swapped(): lax.ppermute(far, axis, pairs(1))]
    ppermute x4, starting transfers between devices: 20 us -> 18.1 us  [swapped(): lax.ppermute(near, axis, pairs(0))]
    pallas_call x11 -> x13, Pallas kernels: 7.22 us -> 8.81 us  [run(): pl.pallas_call(kernel, out_shape=[jax.ShapeDtypeStruct(*shape) if i in re...]
  transfers between devices with their start and end apart: 8 -> 10, of which waited for: 4 -> 5; matrix products, arithmetic and copies ran while one was open for 0% -> 0% of each run, Pallas kernels for 1% -> 2%
where the time goes in v4:
time: 120 us
  blocking collectives  59.1 us (49%)
  starting transfers between devices  39.7 us (33%)
  waiting for transfers between devices  11 us (9%)
  Pallas kernels  8.81 us (7%)
    all_to_all x1, blocking collectives, per_device(): terms = lax.all_to_all(terms, 'z', 0, 0, tiled=True)  31.6 us
    all_to_all x1, blocking collectives, per_device(): terms = lax.all_to_all(terms, ('half', 'gy'), 0, 0, tiled=True)  27.5 us
    ppermute x4, starting transfers between devices, swapped(): lax.ppermute(near, axis, pairs(0))  18.1 us
    ppermute x4, starting transfers between devices, swapped(): lax.ppermute(far, axis, pairs(1))  17.3 us
    ppermute x4, waiting for transfers between devices, swapped(): lax.ppermute(near, axis, pairs(0))  9.21 us
    pallas_call x13, Pallas kernels, run(): pl.pallas_call(kernel, out_shape=[jax.ShapeDtypeStruct(*shape) if i in re...  8.81 us
  transfers between devices with their start and end apart: 10, of which 5 were waited for; matrix products, arithmetic and copies ran while one was open for 0% of the time, Pallas kernels for 2%

profile of v4, /device:TPU:1, one launch (start us, length us, event | category | flops | bytes accessed | tf_op | source)
XLA Modules:
  0.0 119.6 jit_solution(4213239715316068464)
XLA Ops:
  0.6 1.7 %shard_map.58 = (bf16[343,512]{1,0:T(8,128)(2,1)S(1)}, bf16[512,512]{1,0:T(8,128)(2,1)S(1)}, bf16[56,343]{1,0:T(8,128)(2,1)S(1)}, bf16[105,512]{1,0:T(8,128)(2,1)S(1)}, bf16[105,512]{1,0:T(8,128)(2,1)S(1)}) custom-call(bf16[343,512]{1,0:T(8,128)(2,1)} %field_in.1, bf16[512,512]{1,0:T(8,128)(2,1)} %stiffness_in.1), custom_call_target="tpu_custom_call" | custom-call | tf_op jit(solution)/shard_map/pallas_call | solution.py:65
  2.4 8.8 %collective-permute-start = (bf16[105,512]{1,0:T(8,128)(2,1)S(1)}, bf16[105,512]{1,0:T(8,128)(2,1)S(1)}, u32[]{:S(2)}, u32[]{:S(2)}) collective-permute-start(bf16[105,512]{1,0:T(8,128)(2,1)S(1)} %get-tuple-element.49), channel_id=1, source_target_pairs={{16,32},{32,16},{48,64},{64,48},{80,96},{96,80},{112,128},{128,112... | collective-permute-start | bytes 322568 | tf_op jit(solution)/shard_map/ppermute | solution.py:240
  11.2 7.9 %collective-permute-start.1 = (bf16[105,512]{1,0:T(8,128)(2,1)S(1)}, bf16[105,512]{1,0:T(8,128)(2,1)S(1)}, u32[]{:S(2)}, u32[]{:S(2)}) collective-permute-start(bf16[105,512]{1,0:T(8,128)(2,1)S(1)} %get-tuple-element.50), channel_id=1, source_target_pairs={{0,16},{16,0},{32,48},{48,32},{64,80},{80,64},{96,112},{112,96},{1... | collective-permute-start | bytes 322568 | tf_op jit(solution)/shard_map/ppermute | solution.py:240
  19.1 1.0 shard_map.59
  20.1 0.3 shard_map.60
  20.4 0.0 copy-start
  20.4 0.7 collective-permute-start.2
  21.0 1.9 %collective-permute-start.3 = (bf16[105,512]{1,0:T(8,128)(2,1)S(1)}, bf16[105,512]{1,0:T(8,128)(2,1)S(1)}, u32[]{:S(2)}, u32[]{:S(2)}) collective-permute-start(bf16[105,512]{1,0:T(8,128)(2,1)S(1)} %get-tuple-element.55), channel_id=1, source_target_pairs={{0,1},{1,0},{2,3},{3,2},{4,5},{5,4},{6,7},{7,6},{8,9},{9,8},{10,11... | collective-permute-start | bytes 322568 | tf_op jit(solution)/shard_map/ppermute | solution.py:240
  23.0 0.1 broadcast_in_dim.4.potential
  23.1 0.3 shard_map.61.own
  23.4 3.9 %collective-permute-done.3.near_in = bf16[105,512]{1,0:T(8,128)(2,1)S(1)} collective-permute-done((bf16[105,512]{1,0:T(8,128)(2,1)S(1)}, bf16[105,512]{1,0:T(8,128)(2,1)S(1)}, u32[]{:S(2)}, u32[]{:S(2)}) %collective-permute-start.3) | collective-permute-done | bytes 107552 | tf_op jit(solution)/shard_map/ppermute | solution.py:240
  27.3 0.7 shard_map.62
  28.0 7.1 %collective-permute-start.4 = (bf16[105,512]{1,0:T(8,128)(2,1)S(1)}, bf16[105,512]{1,0:T(8,128)(2,1)S(1)}, u32[]{:S(2)}, u32[]{:S(2)}) collective-permute-start(bf16[105,512]{1,0:T(8,128)(2,1)S(1)} %get-tuple-element.58), channel_id=1, source_target_pairs={{16,32},{32,16},{48,64},{64,48},{80,96},{96,80},{112,128},{128,112... | collective-permute-start | bytes 322568 | tf_op jit(solution)/shard_map/ppermute | solution.py:240
  35.1 1.9 %collective-permute-start.5 = (bf16[105,512]{1,0:T(8,128)(2,1)S(1)}, bf16[105,512]{1,0:T(8,128)(2,1)S(1)}, u32[]{:S(2)}, u32[]{:S(2)}) collective-permute-start(bf16[105,512]{1,0:T(8,128)(2,1)S(1)} %get-tuple-element.59), channel_id=1, source_target_pairs={{0,16},{16,0},{32,48},{48,32},{64,80},{80,64},{96,112},{112,96},{1... | collective-permute-start | bytes 322568 | tf_op jit(solution)/shard_map/ppermute | solution.py:240
  37.1 0.4 shard_map.63.partial
  37.5 0.7 collective-permute-done.4.far_in
  38.1 0.2 collective-permute-done.5.near_in
  38.4 0.2 shard_map.64
  38.6 0.7 collective-permute-start.6
  39.3 6.4 %collective-permute-start.7 = (bf16[105,512]{1,0:T(8,128)(2,1)S(1)}, bf16[105,512]{1,0:T(8,128)(2,1)S(1)}, u32[]{:S(2)}, u32[]{:S(2)}) collective-permute-start(bf16[105,512]{1,0:T(8,128)(2,1)S(1)} %get-tuple-element.64), channel_id=1, source_target_pairs={{0,1},{1,0},{2,3},{3,2},{4,5},{5,4},{6,7},{7,6},{8,9},{9,8},{10,11... | collective-permute-start | bytes 322568 | tf_op jit(solution)/shard_map/ppermute | solution.py:240
  45.7 0.3 shard_map.65.own
  46.0 5.0 %collective-permute-done.7.near_in = bf16[105,512]{1,0:T(8,128)(2,1)S(1)} collective-permute-done((bf16[105,512]{1,0:T(8,128)(2,1)S(1)}, bf16[105,512]{1,0:T(8,128)(2,1)S(1)}, u32[]{:S(2)}, u32[]{:S(2)}) %collective-permute-start.7) | collective-permute-done | bytes 107552 | tf_op jit(solution)/shard_map/ppermute | solution.py:240
  51.0 1.2 %shard_map.66 = (f32[343,512]{1,0:T(8,128)S(1)}, bf16[512,256]{1,0:T(8,128)(2,1)S(1)}, bf16[512,256]{1,0:T(8,128)(2,1)S(1)}) custom-call(bf16[343,56]{1,0:T(8,128)(2,1)S(1)} %get-tuple-element.40.own_y, bf16[49,56]{1,0:T(8,128)(2,1)S(1)} %get-tuple-element.41.side_y, f32[343,512]{1,0:T(8,128)S(1)} %shard_map.65.own, ...), custom_call_target="tpu_custom_call" | custom-call | tf_op jit(solution)/shard_map/pallas_call | solution.py:65
  52.2 1.7 %shard_map.67 = (bf16[343,512]{1,0:T(8,128)(2,1)}, bf16[512,256]{1,0:T(8,128)(2,1)S(1)}, bf16[512,256]{1,0:T(8,128)(2,1)S(1)}) custom-call(f32[343,512]{1,0:T(8,128)S(1)} %get-tuple-element.65.second_image, bf16[343,512]{1,0:T(8,128)(2,1)S(1)} %get-tuple-element.39.field, bf16[343,512]{1,0:T(8,128)(2,1)S(1)} %get-tuple-element.57.field.lifted), custom_call_target="tpu_custom_call" | custom-call | tf_op jit(solution)/shard_map/pallas_call | solution.py:65
  53.9 2.0 %collective-permute-start.9 = (bf16[512,256]{1,0:T(8,128)(2,1)S(1)}, bf16[512,256]{1,0:T(8,128)(2,1)S(1)}, u32[]{:S(2)}, u32[]{:S(2)}) collective-permute-start(bf16[512,256]{1,0:T(8,128)(2,1)S(1)} %get-tuple-element.70), channel_id=1, source_target_pairs={{0,16},{16,0},{1,17},{17,1},{2,18},{18,2},{3,19},{19,3},{4,20},{20... | collective-permute-start | bytes 786440 | tf_op jit(solution)/shard_map/ppermute | solution.py:382
  56.0 2.3 %collective-permute-start.8 = (bf16[512,256]{1,0:T(8,128)(2,1)S(1)}, bf16[512,256]{1,0:T(8,128)(2,1)S(1)}, u32[]{:S(2)}, u32[]{:S(2)}) collective-permute-start(bf16[512,256]{1,0:T(8,128)(2,1)S(1)} %get-tuple-element.68), channel_id=1, source_target_pairs={{0,16},{16,0},{1,17},{17,1},{2,18},{18,2},{3,19},{19,3},{4,20},{20... | collective-permute-start | bytes 786440 | tf_op jit(solution)/shard_map/ppermute | solution.py:373
  58.3 1.1 collective-permute-done.8.ham_taken
  59.4 0.1 shard_map.68
  59.5 27.5 %all_to_all.10.terms = bf16[32,64,128]{2,1,0:T(8,128)(2,1)S(1)} all-to-all(bf16[32,64,128]{2,1,0:T(8,128)(2,1)S(1)} %bitcast.1), channel_id=1, replica_groups=mesh['z'=16,'half'=2,'core'=2,'gy'=16] {'half','gy'}, dimensions={0} | all-to-all | bytes 1048576 | tf_op jit(solution)/shard_map/all_to_all | solution.py:417
  87.1 0.2 shard_map.69
  87.3 31.6 %all_to_all.11.terms = f32[16,4,128]{2,1,0:T(4,128)S(1)} all-to-all(f32[16,4,128]{2,1,0:T(4,128)S(1)} %shard_map.69), channel_id=1, replica_groups=mesh['z'=16,'half'=2,'core'=2,'gy'=16] {'z'}, dimensions={0} | all-to-all | bytes 65536 | tf_op jit(solution)/shard_map/all_to_all | solution.py:419
  118.9 0.7 shard_map.70
  (6 shorter events, 0.0 us)
Async XLA Ops:
  2.4 17.7 %collective-permute-start = (bf16[105,512]{1,0:T(8,128)(2,1)S(1)}, bf16[105,512]{1,0:T(8,128)(2,1)S(1)}, u32[]{:S(2)}, u32[]{:S(2)}) collective-permute-start(bf16[105,512]{1,0:T(8,128)(2,1)S(1)} %get-tuple-element.49), channel_id=1, source_target_pairs={{16,32},{32,16},{48,64},{64,48},{80,96},{96,80},{112,128},{128,112... | collective-permute-start | bytes 322568 | tf_op jit(solution)/shard_map/ppermute | solution.py:240
  11.2 8.8 %collective-permute-start.1 = (bf16[105,512]{1,0:T(8,128)(2,1)S(1)}, bf16[105,512]{1,0:T(8,128)(2,1)S(1)}, u32[]{:S(2)}, u32[]{:S(2)}) collective-permute-start(bf16[105,512]{1,0:T(8,128)(2,1)S(1)} %get-tuple-element.50), channel_id=1, source_target_pairs={{0,16},{16,0},{32,48},{48,32},{64,80},{80,64},{96,112},{112,96},{1... | collective-permute-start | bytes 322568 | tf_op jit(solution)/shard_map/ppermute | solution.py:240
  20.4 2.6 %copy-start = (f32[343]{0:T(512)S(1)}, f32[343]{0:T(512)}, u32[]{:S(2)}) copy-start(f32[343]{0:T(512)} %param.4) | copy-start | bytes 4120
  20.4 3.0 %collective-permute-start.2 = (bf16[105,512]{1,0:T(8,128)(2,1)S(1)}, bf16[105,512]{1,0:T(8,128)(2,1)S(1)}, u32[]{:S(2)}, u32[]{:S(2)}) collective-permute-start(bf16[105,512]{1,0:T(8,128)(2,1)S(1)} %get-tuple-element.54), channel_id=1, source_target_pairs={{1,2},{2,1},{3,4},{4,3},{5,6},{6,5},{7,8},{8,7},{9,10},{10,9},{11,... | collective-permute-start | bytes 322568 | tf_op jit(solution)/shard_map/ppermute | solution.py:240
  21.0 6.3 %collective-permute-start.3 = (bf16[105,512]{1,0:T(8,128)(2,1)S(1)}, bf16[105,512]{1,0:T(8,128)(2,1)S(1)}, u32[]{:S(2)}, u32[]{:S(2)}) collective-permute-start(bf16[105,512]{1,0:T(8,128)(2,1)S(1)} %get-tuple-element.55), channel_id=1, source_target_pairs={{0,1},{1,0},{2,3},{3,2},{4,5},{5,4},{6,7},{7,6},{8,9},{9,8},{10,11... | collective-permute-start | bytes 322568 | tf_op jit(solution)/shard_map/ppermute | solution.py:240
  28.0 10.1 %collective-permute-start.4 = (bf16[105,512]{1,0:T(8,128)(2,1)S(1)}, bf16[105,512]{1,0:T(8,128)(2,1)S(1)}, u32[]{:S(2)}, u32[]{:S(2)}) collective-permute-start(bf16[105,512]{1,0:T(8,128)(2,1)S(1)} %get-tuple-element.58), channel_id=1, source_target_pairs={{16,32},{32,16},{48,64},{64,48},{80,96},{96,80},{112,128},{128,112... | collective-permute-start | bytes 322568 | tf_op jit(solution)/shard_map/ppermute | solution.py:240
  35.1 3.2 %collective-permute-start.5 = (bf16[105,512]{1,0:T(8,128)(2,1)S(1)}, bf16[105,512]{1,0:T(8,128)(2,1)S(1)}, u32[]{:S(2)}, u32[]{:S(2)}) collective-permute-start(bf16[105,512]{1,0:T(8,128)(2,1)S(1)} %get-tuple-element.59), channel_id=1, source_target_pairs={{0,16},{16,0},{32,48},{48,32},{64,80},{80,64},{96,112},{112,96},{1... | collective-permute-start | bytes 322568 | tf_op jit(solution)/shard_map/ppermute | solution.py:240
  38.6 7.3 %collective-permute-start.6 = (bf16[105,512]{1,0:T(8,128)(2,1)S(1)}, bf16[105,512]{1,0:T(8,128)(2,1)S(1)}, u32[]{:S(2)}, u32[]{:S(2)}) collective-permute-start(bf16[105,512]{1,0:T(8,128)(2,1)S(1)} %get-tuple-element.63), channel_id=1, source_target_pairs={{1,2},{2,1},{3,4},{4,3},{5,6},{6,5},{7,8},{8,7},{9,10},{10,9},{11,... | collective-permute-start | bytes 322568 | tf_op jit(solution)/shard_map/ppermute | solution.py:240
  39.3 11.7 %collective-permute-start.7 = (bf16[105,512]{1,0:T(8,128)(2,1)S(1)}, bf16[105,512]{1,0:T(8,128)(2,1)S(1)}, u32[]{:S(2)}, u32[]{:S(2)}) collective-permute-start(bf16[105,512]{1,0:T(8,128)(2,1)S(1)} %get-tuple-element.64), channel_id=1, source_target_pairs={{0,1},{1,0},{2,3},{3,2},{4,5},{5,4},{6,7},{7,6},{8,9},{9,8},{10,11... | collective-permute-start | bytes 322568 | tf_op jit(solution)/shard_map/ppermute | solution.py:240
  53.9 4.3 %collective-permute-start.9 = (bf16[512,256]{1,0:T(8,128)(2,1)S(1)}, bf16[512,256]{1,0:T(8,128)(2,1)S(1)}, u32[]{:S(2)}, u32[]{:S(2)}) collective-permute-start(bf16[512,256]{1,0:T(8,128)(2,1)S(1)} %get-tuple-element.70), channel_id=1, source_target_pairs={{0,16},{16,0},{1,17},{17,1},{2,18},{18,2},{3,19},{19,3},{4,20},{20... | collective-permute-start | bytes 786440 | tf_op jit(solution)/shard_map/ppermute | solution.py:382
  56.0 3.4 %collective-permute-start.8 = (bf16[512,256]{1,0:T(8,128)(2,1)S(1)}, bf16[512,256]{1,0:T(8,128)(2,1)S(1)}, u32[]{:S(2)}, u32[]{:S(2)}) collective-permute-start(bf16[512,256]{1,0:T(8,128)(2,1)S(1)} %get-tuple-element.68), channel_id=1, source_target_pairs={{0,16},{16,0},{1,17},{17,1},{2,18},{18,2},{3,19},{19,3},{4,20},{20... | collective-permute-start | bytes 786440 | tf_op jit(solution)/shard_map/ppermute | solution.py:373

commit v5 on v4

--- a/solution.py
+++ b/solution.py
@@ -6,7 +6,6 @@
 from jax.experimental import pallas as pl
 from jax.experimental.pallas import tpu as pltpu
 from jax.sharding import Mesh, PartitionSpec as P
-
 
 DEG = 7
 SIDE = DEG + 1
@@ -71,6 +70,7 @@
             out_specs=[vmem] * len(shapes),
             scratch_shapes=list(scratch),
             compiler_params=pltpu.CompilerParams(vmem_limit_bytes=VMEM_LIMIT),
+            name=kernel.__name__,
         )(
             *[
                 pltpu.with_memory_space_constraint(arg, pltpu.HBM if i in raw else pltpu.VMEM)
@@ -161,10 +161,6 @@
     side_y[...] = ordered[OWN : OWN + FACE, to_y:].astype(BF16)
     face_y[...] = ordered[OWN + RIM :, to_y:].astype(BF16)
     edge_y[...] = ordered[OWN + FACE : OWN + RIM, to_y:].astype(BF16)
-
-
-def multiply(own_columns, field, partial):
-    partial[...] = dot(own_columns[...], field[...])
 
 
 def cross(rim_x, face_x, partial, field, far_in, near_in, far, near, rim, above_x, raw, wide, face, upward, downward):
@@ -308,8 +304,6 @@
             scratch=staged(OWN, RIM, FACE, message_rows, message_rows),
         )(own_y, side_y, own, far, near, field, weight, rim_own)
         far, near = swapped(far, near, gx, length_x)
-        partial = call(multiply, (by_orbital(CELL), F32))(own_columns, lifted)[0]
-        own, far, near = row_part(partial, lifted, far, near)
 
         def shuffle():
             place = lax.broadcasted_iota(jnp.int32, (orbital_count, 1), 0)
@@ -324,66 +318,66 @@
             )
             return one_hot(order, orbital_count)
 
-        def gram(left, right, keep, give):
-            shuffled = dot_columns(right, shuffle()).astype(BF16)
-            product = (dot_rows(left, shuffled) * norm_scale).astype(BF16)
+        def shuffled_product(own_columns, lifted, partial, order, shuffled):
+            partial[...] = dot(own_columns[...], lifted[...])
+            order[...] = shuffle()
+            shuffled[...] = dot_columns(lifted[...], order[...]).astype(BF16)
+
+        partial, order, shuffled = call(
+            shuffled_product,
+            (by_orbital(CELL), F32),
+            ((orbital_count, orbital_count), BF16),
+            (by_orbital(OWN), BF16),
+        )(own_columns, lifted)
+        own, far, near = row_part(partial, lifted, far, near)
+
+        def filter_and_gram(
+            own_y, side_y, own, far_in, near_in, field, lifted, potential, order, shuffled,
+            filtered, keep, give, image, corner, face, wide, rows,
+        ):
             core = lax.axis_index("core")
 
-            @pl.when(core == 0)
-            def _():
-                keep[...] = product[:, :half]
-                give[...] = product[:, half:]
-
-            @pl.when(core == 1)
-            def _():
-                keep[...] = product[:, half:]
-                give[...] = product[:, :half]
-
-        def image_gram(
-            own_y, side_y, own, far_in, near_in, lifted, potential,
-            second_image, keep, give, image, corner, face, wide, rows,
-        ):
+            def gram(which, left, right):
+                product = (dot_rows(left, right) * norm_scale).astype(BF16)
+
+                @pl.when(core == 0)
+                def _():
+                    keep[which] = product[:, :half]
+                    give[which] = product[:, half:]
+
+                @pl.when(core == 1)
+                def _():
+                    keep[which] = product[:, half:]
+                    give[which] = product[:, :half]
+
             close(own_y, side_y, own, far_in, near_in, image, corner, face, wide)
             image[OWN:, :] = jnp.zeros((padded - OWN, orbital_count), F32)
             rows[OWN:, :] = jnp.zeros((padded - OWN, orbital_count), F32)
-            rows[:OWN, :] = lifted[...].astype(F32)
-            image[:OWN, :] += potential[...] * rows[:OWN, :]
-            second_image[...] = image[:OWN, :]
-            gram(image[...].astype(BF16), rows[...].astype(BF16), keep, give)
-
-        def filter_gram(second_image, field, lifted, filtered, keep, give, rows):
-            rows[OWN:, :] = jnp.zeros((padded - OWN, orbital_count), F32)
-            rows[:OWN, :] = (
-                2.0 * (second_image[...] - SPECTRUM_CENTER * lifted[...].astype(F32)) / SPECTRUM_HALF
-                - field[...].astype(F32)
+            rows[:OWN, :] = shuffled[...].astype(F32)
+            lifted32 = lifted[...].astype(F32)
+            image[:OWN, :] += potential[...] * lifted32
+            gram(0, image[...].astype(BF16), rows[...].astype(BF16))
+            image[:OWN, :] = (
+                2.0 * (image[:OWN, :] - SPECTRUM_CENTER * lifted32) / SPECTRUM_HALF - field[...].astype(F32)
             )
-            filtered[...] = rows[:OWN, :].astype(BF16)
-            values = rows[...].astype(BF16)
-            gram(values, values, keep, give)
-
-        half_gram = ((orbital_count, half), BF16)
-        pair = [(0, 1), (1, 0)]
-        second_image, ham_kept, ham_given = call(
-            image_gram,
-            (by_orbital(OWN), F32),
-            half_gram,
-            half_gram,
+            filtered[...] = image[:OWN, :].astype(BF16)
+            values = image[...].astype(BF16)
+            gram(1, values, dot_columns(values, order[...]).astype(BF16))
+
+        half_grams = ((2, orbital_count, half), BF16)
+        filtered, kept, given = call(
+            filter_and_gram,
+            (by_orbital(OWN), BF16),
+            half_grams,
+            half_grams,
             scratch=staged(padded, RIM, FACE, message_rows, padded),
-        )(own_y, side_y, own, far, near, lifted, weight)
-        ham_taken = lax.ppermute(ham_given, "core", pair)
-        filtered, kept, given = call(
-            filter_gram,
-            (by_orbital(OWN), BF16),
-            half_gram,
-            half_gram,
-            scratch=staged(padded),
             results=(0,),
-        )(second_image, field, lifted)
-        taken = lax.ppermute(given, "core", pair)
-
-        def pair_sum(ham_kept, ham_taken, kept, taken, out):
-            for which, (mine, other) in enumerate(((ham_kept, ham_taken), (kept, taken))):
-                total = (mine[...].astype(F32) + other[...].astype(F32)).astype(BF16)
+        )(own_y, side_y, own, far, near, field, lifted, weight, order, shuffled)
+        taken = lax.ppermute(given, "core", [(0, 1), (1, 0)])
+
+        def pair_sum(kept, taken, out):
+            for which in range(2):
+                total = (kept[which].astype(F32) + taken[which].astype(F32)).astype(BF16)
                 for side in range(2):
                     part = total[:, side * quarter : (side + 1) * quarter]
                     for j in range(length_y):
@@ -401,21 +395,21 @@
                 total += terms[source].astype(F32)
             total = total.T.reshape(length_z, block_rows, wide)
             for part in range(fold):
-                out[:, :, part * wide : (part + 1) * wide] = total[:, part * short : (part + 1) * short, :]
+                out[:, :, part * wide : (part + 1) * wide] = total[:, part * short : (part + 1) * short, :].astype(BF16)
 
         def line_sum(terms, ham, correlation):
-            total = terms[0]
+            total = terms[0].astype(F32)
             for source in range(1, length_z):
-                total += terms[source]
+                total += terms[source].astype(F32)
             for part in range(fold):
                 block = total[:, part * wide : (part + 1) * wide]
                 ham[part * short : (part + 1) * short, :] = block[:, :block_cols]
                 correlation[part * short : (part + 1) * short, :] = block[:, block_cols:]
 
-        terms = call(pair_sum, ((2, length_y, wide, quarter), BF16))(ham_kept, ham_taken, kept, taken)[0]
+        terms = call(pair_sum, ((2, length_y, wide, quarter), BF16))(kept, taken)[0]
         terms = terms.reshape(2 * length_y, wide, quarter)
         terms = lax.all_to_all(terms, ("half", "gy"), 0, 0, tiled=True)
-        terms = call(plane_sum, ((length_z, short, fold * wide), F32))(terms)[0]
+        terms = call(plane_sum, ((length_z, short, fold * wide), BF16))(terms)[0]
         terms = lax.all_to_all(terms, "z", 0, 0, tiled=True)
         block = (block_rows, block_cols)
         projected_ham, correlation = call(line_sum, (block, F32), (block, F32), results=(0, 1))(terms)

time: 120 us -> 118 us (0.983)
  starting transfers between devices: 39.7 us -> 37.5 us
    ppermute x2 -> x1, starting transfers between devices: 4.31 us -> 2.03 us  [per_device(): taken = lax.ppermute(given, 'core', [(0, 1), (1, 0)])]
    pallas_call x13 -> x12, Pallas kernels: 8.81 us -> 8.66 us  [run(): pl.pallas_call(kernel, out_shape=[jax.ShapeDtypeStruct(*shape) if i in re...]
  transfers between devices with their start and end apart: 10 -> 9, of which waited for: 5 -> 5; matrix products, arithmetic and copies ran while one was open for 0% -> 0% of each run, Pallas kernels for 2% -> 2%
where the time goes in v5:
time: 118 us; the launch traced here: 117 us
  blocking collectives  58.5 us (50%)
  starting transfers between devices  37.5 us (32%)
  waiting for transfers between devices  11.4 us (10%)
  Pallas kernels  8.66 us (7%)
    all_to_all x1, blocking collectives, per_device(): terms = lax.all_to_all(terms, 'z', 0, 0, tiled=True)  31.5 us
    all_to_all x1, blocking collectives, per_device(): terms = lax.all_to_all(terms, ('half', 'gy'), 0, 0, tiled=True)  27 us
    ppermute x4, starting transfers between devices, swapped(): lax.ppermute(near, axis, pairs(0))  18.1 us
    ppermute x4, starting transfers between devices, swapped(): lax.ppermute(far, axis, pairs(1))  17.3 us
    ppermute x4, waiting for transfers between devices, swapped(): lax.ppermute(near, axis, pairs(0))  9.23 us
    pallas_call x12, Pallas kernels, run(): pl.pallas_call(kernel, out_shape=[jax.ShapeDtypeStruct(*shape) if i in re...  8.66 us
  transfers between devices with their start and end apart: 9, of which 5 were waited for; matrix products, arithmetic and copies ran while one was open for 0% of the time, Pallas kernels for 2%

profile of v5, /device:TPU:1, one launch (start us, length us, event | category | flops | bytes accessed | tf_op | source)
XLA Modules:
  0.0 116.9 jit_solution(2009518081916589801)
XLA Ops:
  0.6 1.7 %prepare.1 = (bf16[343,512]{1,0:T(8,128)(2,1)S(1)}, bf16[512,512]{1,0:T(8,128)(2,1)S(1)}, bf16[56,343]{1,0:T(8,128)(2,1)S(1)}, bf16[105,512]{1,0:T(8,128)(2,1)S(1)}, bf16[105,512]{1,0:T(8,128)(2,1)S(1)}) custom-call(bf16[343,512]{1,0:T(8,128)(2,1)} %field_in.1, bf16[512,512]{1,0:T(8,128)(2,1)} %stiffness_in.1), custom_call_target="tpu_custom_call" | custom-call | tf_op jit(solution)/shard_map/prepare/pallas_call | solution.py:64
  2.4 8.8 %collective-permute-start = (bf16[105,512]{1,0:T(8,128)(2,1)S(1)}, bf16[105,512]{1,0:T(8,128)(2,1)S(1)}, u32[]{:S(2)}, u32[]{:S(2)}) collective-permute-start(bf16[105,512]{1,0:T(8,128)(2,1)S(1)} %get-tuple-element.49), channel_id=1, source_target_pairs={{16,32},{32,16},{48,64},{64,48},{80,96},{96,80},{112,128},{128,112... | collective-permute-start | bytes 322568 | tf_op jit(solution)/shard_map/ppermute | solution.py:236
  11.2 7.9 %collective-permute-start.1 = (bf16[105,512]{1,0:T(8,128)(2,1)S(1)}, bf16[105,512]{1,0:T(8,128)(2,1)S(1)}, u32[]{:S(2)}, u32[]{:S(2)}) collective-permute-start(bf16[105,512]{1,0:T(8,128)(2,1)S(1)} %get-tuple-element.50), channel_id=1, source_target_pairs={{0,16},{16,0},{32,48},{48,32},{64,80},{80,64},{96,112},{112,96},{1... | collective-permute-start | bytes 322568 | tf_op jit(solution)/shard_map/ppermute | solution.py:236
  19.1 1.0 arrange.1
  20.1 0.0 collective-permute-done.1.near_in
  20.1 0.3 cross.2
  20.4 0.0 copy-start
  20.4 0.7 collective-permute-start.2
  21.0 1.9 %collective-permute-start.3 = (bf16[105,512]{1,0:T(8,128)(2,1)S(1)}, bf16[105,512]{1,0:T(8,128)(2,1)S(1)}, u32[]{:S(2)}, u32[]{:S(2)}) collective-permute-start(bf16[105,512]{1,0:T(8,128)(2,1)S(1)} %get-tuple-element.55), channel_id=1, source_target_pairs={{0,1},{1,0},{2,3},{3,2},{4,5},{5,4},{6,7},{7,6},{8,9},{9,8},{10,11... | collective-permute-start | bytes 322568 | tf_op jit(solution)/shard_map/ppermute | solution.py:236
  23.0 0.1 broadcast_in_dim.4.potential
  23.1 0.3 gather_row.2.own
  23.4 4.0 %collective-permute-done.3.near_in = bf16[105,512]{1,0:T(8,128)(2,1)S(1)} collective-permute-done((bf16[105,512]{1,0:T(8,128)(2,1)S(1)}, bf16[105,512]{1,0:T(8,128)(2,1)S(1)}, u32[]{:S(2)}, u32[]{:S(2)}) %collective-permute-start.3) | collective-permute-done | bytes 107552 | tf_op jit(solution)/shard_map/ppermute | solution.py:236
  27.3 0.7 lift.1
  28.0 7.2 %collective-permute-start.4 = (bf16[105,512]{1,0:T(8,128)(2,1)S(1)}, bf16[105,512]{1,0:T(8,128)(2,1)S(1)}, u32[]{:S(2)}, u32[]{:S(2)}) collective-permute-start(bf16[105,512]{1,0:T(8,128)(2,1)S(1)} %get-tuple-element.59), channel_id=1, source_target_pairs={{16,32},{32,16},{48,64},{64,48},{80,96},{96,80},{112,128},{128,112... | collective-permute-start | bytes 322568 | tf_op jit(solution)/shard_map/ppermute | solution.py:236
  35.2 1.9 %collective-permute-start.5 = (bf16[105,512]{1,0:T(8,128)(2,1)S(1)}, bf16[105,512]{1,0:T(8,128)(2,1)S(1)}, u32[]{:S(2)}, u32[]{:S(2)}) collective-permute-start(bf16[105,512]{1,0:T(8,128)(2,1)S(1)} %get-tuple-element.60), channel_id=1, source_target_pairs={{0,16},{16,0},{32,48},{48,32},{64,80},{80,64},{96,112},{112,96},{1... | collective-permute-start | bytes 322568 | tf_op jit(solution)/shard_map/ppermute | solution.py:236
  37.1 0.6 shuffled_product.1
  37.7 0.4 collective-permute-done.4.far_in
  38.1 0.3 collective-permute-done.5.near_in
  38.4 0.2 cross.3
  38.6 0.7 collective-permute-start.6
  39.3 6.4 %collective-permute-start.7 = (bf16[105,512]{1,0:T(8,128)(2,1)S(1)}, bf16[105,512]{1,0:T(8,128)(2,1)S(1)}, u32[]{:S(2)}, u32[]{:S(2)}) collective-permute-start(bf16[105,512]{1,0:T(8,128)(2,1)S(1)} %get-tuple-element.65), channel_id=1, source_target_pairs={{0,1},{1,0},{2,3},{3,2},{4,5},{5,4},{6,7},{7,6},{8,9},{9,8},{10,11... | collective-permute-start | bytes 322568 | tf_op jit(solution)/shard_map/ppermute | solution.py:236
  45.7 0.3 gather_row.3.own
  46.0 0.0 collective-permute-done.6.far_in
  46.0 5.0 %collective-permute-done.7.near_in = bf16[105,512]{1,0:T(8,128)(2,1)S(1)} collective-permute-done((bf16[105,512]{1,0:T(8,128)(2,1)S(1)}, bf16[105,512]{1,0:T(8,128)(2,1)S(1)}, u32[]{:S(2)}, u32[]{:S(2)}) %collective-permute-start.7) | collective-permute-done | bytes 107552 | tf_op jit(solution)/shard_map/ppermute | solution.py:236
  51.0 2.5 %filter_and_gram.1 = (bf16[343,512]{1,0:T(8,128)(2,1)}, bf16[2,512,256]{2,1,0:T(8,128)(2,1)S(1)}, bf16[2,512,256]{2,1,0:T(8,128)(2,1)S(1)}) custom-call(bf16[343,56]{1,0:T(8,128)(2,1)S(1)} %get-tuple-element.40.own_y, bf16[49,56]{1,0:T(8,128)(2,1)S(1)} %get-tuple-element.41.side_y, f32[343,512]{1,0:T(8,128)S(1)} %gather_row.3.own, ...), custom_call_target="tpu_custom_call" | custom-call | tf_op jit(solution)/shard_map/filter_and_gram/pallas_call | solution.py:64
  53.5 2.0 %collective-permute-start.8 = (bf16[2,512,256]{2,1,0:T(8,128)(2,1)S(1)}, bf16[2,512,256]{2,1,0:T(8,128)(2,1)S(1)}, u32[]{:S(2)}, u32[]{:S(2)}) collective-permute-start(bf16[2,512,256]{2,1,0:T(8,128)(2,1)S(1)} %get-tuple-element.70), channel_id=1, source_target_pairs={{0,16},{16,0},{1,17},{17,1},{2,18},{18,2},{3,19},{19,3},{4,20},{20... | collective-permute-start | bytes 1572872 | tf_op jit(solution)/shard_map/ppermute | solution.py:376
  55.6 1.8 %collective-permute-done.8.taken = bf16[2,512,256]{2,1,0:T(8,128)(2,1)S(1)} collective-permute-done((bf16[2,512,256]{2,1,0:T(8,128)(2,1)S(1)}, bf16[2,512,256]{2,1,0:T(8,128)(2,1)S(1)}, u32[]{:S(2)}, u32[]{:S(2)}) %collective-permute-start.8) | collective-permute-done | bytes 524320 | tf_op jit(solution)/shard_map/ppermute | solution.py:376
  57.3 0.1 pair_sum.1
  57.5 27.0 %all_to_all.10.terms = bf16[32,64,128]{2,1,0:T(8,128)(2,1)S(1)} all-to-all(bf16[32,64,128]{2,1,0:T(8,128)(2,1)S(1)} %bitcast.1), channel_id=1, replica_groups=mesh['z'=16,'half'=2,'core'=2,'gy'=16] {'half','gy'}, dimensions={0} | all-to-all | bytes 1048576 | tf_op jit(solution)/shard_map/all_to_all | solution.py:411
  84.5 0.2 plane_sum.1
  84.7 31.5 %all_to_all.11.terms = bf16[16,4,128]{2,1,0:T(4,128)(2,1)S(1)} all-to-all(bf16[16,4,128]{2,1,0:T(4,128)(2,1)S(1)} %plane_sum.1), channel_id=1, replica_groups=mesh['z'=16,'half'=2,'core'=2,'gy'=16] {'z'}, dimensions={0} | all-to-all | bytes 32768 | tf_op jit(solution)/shard_map/all_to_all | solution.py:413
  116.2 0.7 line_sum.1
  (3 shorter events, 0.0 us)
Async XLA Ops:
  2.4 17.7 %collective-permute-start = (bf16[105,512]{1,0:T(8,128)(2,1)S(1)}, bf16[105,512]{1,0:T(8,128)(2,1)S(1)}, u32[]{:S(2)}, u32[]{:S(2)}) collective-permute-start(bf16[105,512]{1,0:T(8,128)(2,1)S(1)} %get-tuple-element.49), channel_id=1, source_target_pairs={{16,32},{32,16},{48,64},{64,48},{80,96},{96,80},{112,128},{128,112... | collective-permute-start | bytes 322568 | tf_op jit(solution)/shard_map/ppermute | solution.py:236
  11.2 8.8 %collective-permute-start.1 = (bf16[105,512]{1,0:T(8,128)(2,1)S(1)}, bf16[105,512]{1,0:T(8,128)(2,1)S(1)}, u32[]{:S(2)}, u32[]{:S(2)}) collective-permute-start(bf16[105,512]{1,0:T(8,128)(2,1)S(1)} %get-tuple-element.50), channel_id=1, source_target_pairs={{0,16},{16,0},{32,48},{48,32},{64,80},{80,64},{96,112},{112,96},{1... | collective-permute-start | bytes 322568 | tf_op jit(solution)/shard_map/ppermute | solution.py:236
  20.4 2.6 %copy-start = (f32[343]{0:T(512)S(1)}, f32[343]{0:T(512)}, u32[]{:S(2)}) copy-start(f32[343]{0:T(512)} %param.4) | copy-start | bytes 4120
  20.4 3.0 %collective-permute-start.2 = (bf16[105,512]{1,0:T(8,128)(2,1)S(1)}, bf16[105,512]{1,0:T(8,128)(2,1)S(1)}, u32[]{:S(2)}, u32[]{:S(2)}) collective-permute-start(bf16[105,512]{1,0:T(8,128)(2,1)S(1)} %get-tuple-element.54), channel_id=1, source_target_pairs={{1,2},{2,1},{3,4},{4,3},{5,6},{6,5},{7,8},{8,7},{9,10},{10,9},{11,... | collective-permute-start | bytes 322568 | tf_op jit(solution)/shard_map/ppermute | solution.py:236
  21.0 6.3 %collective-permute-start.3 = (bf16[105,512]{1,0:T(8,128)(2,1)S(1)}, bf16[105,512]{1,0:T(8,128)(2,1)S(1)}, u32[]{:S(2)}, u32[]{:S(2)}) collective-permute-start(bf16[105,512]{1,0:T(8,128)(2,1)S(1)} %get-tuple-element.55), channel_id=1, source_target_pairs={{0,1},{1,0},{2,3},{3,2},{4,5},{5,4},{6,7},{7,6},{8,9},{9,8},{10,11... | collective-permute-start | bytes 322568 | tf_op jit(solution)/shard_map/ppermute | solution.py:236
  28.0 10.1 %collective-permute-start.4 = (bf16[105,512]{1,0:T(8,128)(2,1)S(1)}, bf16[105,512]{1,0:T(8,128)(2,1)S(1)}, u32[]{:S(2)}, u32[]{:S(2)}) collective-permute-start(bf16[105,512]{1,0:T(8,128)(2,1)S(1)} %get-tuple-element.59), channel_id=1, source_target_pairs={{16,32},{32,16},{48,64},{64,48},{80,96},{96,80},{112,128},{128,112... | collective-permute-start | bytes 322568 | tf_op jit(solution)/shard_map/ppermute | solution.py:236
  35.2 3.2 %collective-permute-start.5 = (bf16[105,512]{1,0:T(8,128)(2,1)S(1)}, bf16[105,512]{1,0:T(8,128)(2,1)S(1)}, u32[]{:S(2)}, u32[]{:S(2)}) collective-permute-start(bf16[105,512]{1,0:T(8,128)(2,1)S(1)} %get-tuple-element.60), channel_id=1, source_target_pairs={{0,16},{16,0},{32,48},{48,32},{64,80},{80,64},{96,112},{112,96},{1... | collective-permute-start | bytes 322568 | tf_op jit(solution)/shard_map/ppermute | solution.py:236
  38.6 7.4 %collective-permute-start.6 = (bf16[105,512]{1,0:T(8,128)(2,1)S(1)}, bf16[105,512]{1,0:T(8,128)(2,1)S(1)}, u32[]{:S(2)}, u32[]{:S(2)}) collective-permute-start(bf16[105,512]{1,0:T(8,128)(2,1)S(1)} %get-tuple-element.64), channel_id=1, source_target_pairs={{1,2},{2,1},{3,4},{4,3},{5,6},{6,5},{7,8},{8,7},{9,10},{10,9},{11,... | collective-permute-start | bytes 322568 | tf_op jit(solution)/shard_map/ppermute | solution.py:236
  39.3 11.7 %collective-permute-start.7 = (bf16[105,512]{1,0:T(8,128)(2,1)S(1)}, bf16[105,512]{1,0:T(8,128)(2,1)S(1)}, u32[]{:S(2)}, u32[]{:S(2)}) collective-permute-start(bf16[105,512]{1,0:T(8,128)(2,1)S(1)} %get-tuple-element.65), channel_id=1, source_target_pairs={{0,1},{1,0},{2,3},{3,2},{4,5},{5,4},{6,7},{7,6},{8,9},{9,8},{10,11... | collective-permute-start | bytes 322568 | tf_op jit(solution)/shard_map/ppermute | solution.py:236
  53.5 3.8 %collective-permute-start.8 = (bf16[2,512,256]{2,1,0:T(8,128)(2,1)S(1)}, bf16[2,512,256]{2,1,0:T(8,128)(2,1)S(1)}, u32[]{:S(2)}, u32[]{:S(2)}) collective-permute-start(bf16[2,512,256]{2,1,0:T(8,128)(2,1)S(1)} %get-tuple-element.70), channel_id=1, source_target_pairs={{0,16},{16,0},{1,17},{17,1},{2,18},{18,2},{3,19},{19,3},{4,20},{20... | collective-permute-start | bytes 1572872 | tf_op jit(solution)/shard_map/ppermute | solution.py:376

commit v6 on v5

--- a/solution.py
+++ b/solution.py
@@ -241,7 +241,6 @@
         block_rows = orbital_count // length_x
         block_cols = orbital_count // length_y
         half = orbital_count // 2
-        quarter = orbital_count // 4
         padded = -(-OWN // 128) * 128
 
         def by_orbital(rows):
@@ -307,15 +306,9 @@
 
         def shuffle():
             place = lax.broadcasted_iota(jnp.int32, (orbital_count, 1), 0)
-            low = lax.bitwise_and(place, quarter - 1)
-            line = lax.shift_right_logical(low, block_rows.bit_length() - 1)
-            side = lax.shift_right_logical(place, quarter.bit_length() - 1)
-            order = (
-                line * (4 * block_rows)
-                + lax.bitwise_and(side, 1) * (2 * block_rows)
-                + lax.shift_right_logical(side, 1) * block_rows
-                + lax.bitwise_and(low, block_rows - 1)
-            )
+            block = lax.shift_right_logical(lax.bitwise_and(place, half - 1), block_rows.bit_length() - 1)
+            side = lax.bitwise_xor(lax.shift_right_logical(place, half.bit_length() - 1), lax.axis_index("core"))
+            order = block * (2 * block_rows) + side * block_rows + lax.bitwise_and(place, block_rows - 1)
             return one_hot(order, orbital_count)
 
         def shuffled_product(own_columns, lifted, partial, order, shuffled):
@@ -335,20 +328,10 @@
             own_y, side_y, own, far_in, near_in, field, lifted, potential, order, shuffled,
             filtered, keep, give, image, corner, face, wide, rows,
         ):
-            core = lax.axis_index("core")
-
             def gram(which, left, right):
                 product = (dot_rows(left, right) * norm_scale).astype(BF16)
-
-                @pl.when(core == 0)
-                def _():
-                    keep[which] = product[:, :half]
-                    give[which] = product[:, half:]
-
-                @pl.when(core == 1)
-                def _():
-                    keep[which] = product[:, half:]
-                    give[which] = product[:, :half]
+                keep[which] = product[:, :half]
+                give[which] = product[:, half:]
 
             close(own_y, side_y, own, far_in, near_in, image, corner, face, wide)
             image[OWN:, :] = jnp.zeros((padded - OWN, orbital_count), F32)
@@ -378,12 +361,8 @@
         def pair_sum(kept, taken, out):
             for which in range(2):
                 total = (kept[which].astype(F32) + taken[which].astype(F32)).astype(BF16)
-                for side in range(2):
-                    part = total[:, side * quarter : (side + 1) * quarter]
-                    for j in range(length_y):
-                        out[side, j, which * block_cols : (which + 1) * block_cols] = part[
-                            j * block_cols : (j + 1) * block_cols
-                        ]
+                for j in range(length_y):
+                    out[j, which * block_cols : (which + 1) * block_cols] = total[j * block_cols : (j + 1) * block_cols]
 
         wide = 2 * block_cols
         fold = max(1, 128 // wide)
@@ -391,26 +370,25 @@
 
         def plane_sum(terms, out):
             total = terms[0].astype(F32)
-            for source in range(1, 2 * length_y):
+            for source in range(1, length_y):
                 total += terms[source].astype(F32)
-            total = total.T.reshape(length_z, block_rows, wide)
+            total = total.T.reshape(length_x // 2, block_rows, wide)
             for part in range(fold):
                 out[:, :, part * wide : (part + 1) * wide] = total[:, part * short : (part + 1) * short, :].astype(BF16)
 
         def line_sum(terms, ham, correlation):
             total = terms[0].astype(F32)
-            for source in range(1, length_z):
+            for source in range(1, length_x // 2):
                 total += terms[source].astype(F32)
             for part in range(fold):
                 block = total[:, part * wide : (part + 1) * wide]
                 ham[part * short : (part + 1) * short, :] = block[:, :block_cols]
                 correlation[part * short : (part + 1) * short, :] = block[:, block_cols:]
 
-        terms = call(pair_sum, ((2, length_y, wide, quarter), BF16))(kept, taken)[0]
-        terms = terms.reshape(2 * length_y, wide, quarter)
-        terms = lax.all_to_all(terms, ("half", "gy"), 0, 0, tiled=True)
-        terms = call(plane_sum, ((length_z, short, fold * wide), BF16))(terms)[0]
-        terms = lax.all_to_all(terms, "z", 0, 0, tiled=True)
+        terms = call(pair_sum, ((length_y, wide, half), BF16))(kept, taken)[0]
+        terms = lax.all_to_all(terms, "gy", 0, 0, tiled=True)
+        terms = call(plane_sum, ((length_x // 2, short, fold * wide), BF16))(terms)[0]
+        terms = lax.all_to_all(terms, ("z", "half"), 0, 0, tiled=True)
         block = (block_rows, block_cols)
         projected_ham, correlation = call(line_sum, (block, F32), (block, F32), results=(0, 1))(terms)
         return filtered, projected_ham, correlation

time: 118 us -> 120 us (1.017)
  blocking collectives: 58.5 us -> 62.5 us
    all_to_all x2, blocking collectives: 58.5 us -> 62.5 us  [the longest x1 41.3 us: per_device(): terms = lax.all_to_all(terms, ('z', 'half'), 0, 0, tiled=True)]
where the time goes in v6:
time: 120 us
  blocking collectives  62.5 us (52%)
  starting transfers between devices  37.5 us (31%)
  waiting for transfers between devices  11.4 us (10%)
  Pallas kernels  7.61 us (6%)
    all_to_all x1, blocking collectives, per_device(): terms = lax.all_to_all(terms, ('z', 'half'), 0, 0, tiled=True)  41.3 us
    all_to_all x1, blocking collectives, per_device(): terms = lax.all_to_all(terms, 'gy', 0, 0, tiled=True)  21.2 us
    ppermute x4, starting transfers between devices, swapped(): lax.ppermute(near, axis, pairs(0))  18.1 us
    ppermute x4, starting transfers between devices, swapped(): lax.ppermute(far, axis, pairs(1))  17.3 us
    ppermute x4, waiting for transfers between devices, swapped(): lax.ppermute(near, axis, pairs(0))  9.23 us
    pallas_call x12, Pallas kernels, run(): pl.pallas_call(kernel, out_shape=[jax.ShapeDtypeStruct(*shape) if i in re...  7.61 us
  transfers between devices with their start and end apart: 9, of which 5 were waited for; matrix products, arithmetic and copies ran while one was open for 0% of the time, Pallas kernels for 2%

profile of v6, /device:TPU:1, one launch (start us, length us, event | category | flops | bytes accessed | tf_op | source)
XLA Modules:
  0.0 119.9 jit_solution(7492415699091627611)
XLA Ops:
  0.6 1.7 %prepare.1 = (bf16[343,512]{1,0:T(8,128)(2,1)S(1)}, bf16[512,512]{1,0:T(8,128)(2,1)S(1)}, bf16[56,343]{1,0:T(8,128)(2,1)S(1)}, bf16[105,512]{1,0:T(8,128)(2,1)S(1)}, bf16[105,512]{1,0:T(8,128)(2,1)S(1)}) custom-call(bf16[343,512]{1,0:T(8,128)(2,1)} %field_in.1, bf16[512,512]{1,0:T(8,128)(2,1)} %stiffness_in.1), custom_call_target="tpu_custom_call" | custom-call | tf_op jit(solution)/shard_map/prepare/pallas_call | solution.py:64
  2.4 8.8 %collective-permute-start = (bf16[105,512]{1,0:T(8,128)(2,1)S(1)}, bf16[105,512]{1,0:T(8,128)(2,1)S(1)}, u32[]{:S(2)}, u32[]{:S(2)}) collective-permute-start(bf16[105,512]{1,0:T(8,128)(2,1)S(1)} %get-tuple-element.49), channel_id=1, source_target_pairs={{16,32},{32,16},{48,64},{64,48},{80,96},{96,80},{112,128},{128,112... | collective-permute-start | bytes 322568 | tf_op jit(solution)/shard_map/ppermute | solution.py:236
  11.2 7.9 %collective-permute-start.1 = (bf16[105,512]{1,0:T(8,128)(2,1)S(1)}, bf16[105,512]{1,0:T(8,128)(2,1)S(1)}, u32[]{:S(2)}, u32[]{:S(2)}) collective-permute-start(bf16[105,512]{1,0:T(8,128)(2,1)S(1)} %get-tuple-element.50), channel_id=1, source_target_pairs={{0,16},{16,0},{32,48},{48,32},{64,80},{80,64},{96,112},{112,96},{1... | collective-permute-start | bytes 322568 | tf_op jit(solution)/shard_map/ppermute | solution.py:236
  19.1 1.0 arrange.1
  20.1 0.0 collective-permute-done.far_in
  20.1 0.0 collective-permute-done.1.near_in
  20.1 0.3 cross.2
  20.4 0.0 copy-start
  20.4 0.7 collective-permute-start.2
  21.0 1.9 %collective-permute-start.3 = (bf16[105,512]{1,0:T(8,128)(2,1)S(1)}, bf16[105,512]{1,0:T(8,128)(2,1)S(1)}, u32[]{:S(2)}, u32[]{:S(2)}) collective-permute-start(bf16[105,512]{1,0:T(8,128)(2,1)S(1)} %get-tuple-element.55), channel_id=1, source_target_pairs={{0,1},{1,0},{2,3},{3,2},{4,5},{5,4},{6,7},{7,6},{8,9},{9,8},{10,11... | collective-permute-start | bytes 322568 | tf_op jit(solution)/shard_map/ppermute | solution.py:236
  23.0 0.1 broadcast_in_dim.4.potential
  23.1 0.3 gather_row.2.own
  23.4 4.0 %collective-permute-done.3.near_in = bf16[105,512]{1,0:T(8,128)(2,1)S(1)} collective-permute-done((bf16[105,512]{1,0:T(8,128)(2,1)S(1)}, bf16[105,512]{1,0:T(8,128)(2,1)S(1)}, u32[]{:S(2)}, u32[]{:S(2)}) %collective-permute-start.3) | collective-permute-done | bytes 107552 | tf_op jit(solution)/shard_map/ppermute | solution.py:236
  27.3 0.7 lift.1
  28.0 7.2 %collective-permute-start.4 = (bf16[105,512]{1,0:T(8,128)(2,1)S(1)}, bf16[105,512]{1,0:T(8,128)(2,1)S(1)}, u32[]{:S(2)}, u32[]{:S(2)}) collective-permute-start(bf16[105,512]{1,0:T(8,128)(2,1)S(1)} %get-tuple-element.59), channel_id=1, source_target_pairs={{16,32},{32,16},{48,64},{64,48},{80,96},{96,80},{112,128},{128,112... | collective-permute-start | bytes 322568 | tf_op jit(solution)/shard_map/ppermute | solution.py:236
  35.2 1.9 %collective-permute-start.5 = (bf16[105,512]{1,0:T(8,128)(2,1)S(1)}, bf16[105,512]{1,0:T(8,128)(2,1)S(1)}, u32[]{:S(2)}, u32[]{:S(2)}) collective-permute-start(bf16[105,512]{1,0:T(8,128)(2,1)S(1)} %get-tuple-element.60), channel_id=1, source_target_pairs={{0,16},{16,0},{32,48},{48,32},{64,80},{80,64},{96,112},{112,96},{1... | collective-permute-start | bytes 322568 | tf_op jit(solution)/shard_map/ppermute | solution.py:236
  37.1 0.6 shuffled_product.1
  37.7 0.4 collective-permute-done.4.far_in
  38.1 0.3 collective-permute-done.5.near_in
  38.4 0.2 cross.3
  38.6 0.7 collective-permute-start.6
  39.3 6.4 %collective-permute-start.7 = (bf16[105,512]{1,0:T(8,128)(2,1)S(1)}, bf16[105,512]{1,0:T(8,128)(2,1)S(1)}, u32[]{:S(2)}, u32[]{:S(2)}) collective-permute-start(bf16[105,512]{1,0:T(8,128)(2,1)S(1)} %get-tuple-element.65), channel_id=1, source_target_pairs={{0,1},{1,0},{2,3},{3,2},{4,5},{5,4},{6,7},{7,6},{8,9},{9,8},{10,11... | collective-permute-start | bytes 322568 | tf_op jit(solution)/shard_map/ppermute | solution.py:236
  45.7 0.3 gather_row.3.own
  46.0 5.0 %collective-permute-done.7.near_in = bf16[105,512]{1,0:T(8,128)(2,1)S(1)} collective-permute-done((bf16[105,512]{1,0:T(8,128)(2,1)S(1)}, bf16[105,512]{1,0:T(8,128)(2,1)S(1)}, u32[]{:S(2)}, u32[]{:S(2)}) %collective-permute-start.7) | collective-permute-done | bytes 107552 | tf_op jit(solution)/shard_map/ppermute | solution.py:236
  51.0 1.5 %filter_and_gram.1 = (bf16[343,512]{1,0:T(8,128)(2,1)}, bf16[2,512,256]{2,1,0:T(8,128)(2,1)S(1)}, bf16[2,512,256]{2,1,0:T(8,128)(2,1)S(1)}) custom-call(bf16[343,56]{1,0:T(8,128)(2,1)S(1)} %get-tuple-element.40.own_y, bf16[49,56]{1,0:T(8,128)(2,1)S(1)} %get-tuple-element.41.side_y, f32[343,512]{1,0:T(8,128)S(1)} %gather_row.3.own, ...), custom_call_target="tpu_custom_call" | custom-call | tf_op jit(solution)/shard_map/filter_and_gram/pallas_call | solution.py:64
  52.5 2.1 %collective-permute-start.8 = (bf16[2,512,256]{2,1,0:T(8,128)(2,1)S(1)}, bf16[2,512,256]{2,1,0:T(8,128)(2,1)S(1)}, u32[]{:S(2)}, u32[]{:S(2)}) collective-permute-start(bf16[2,512,256]{2,1,0:T(8,128)(2,1)S(1)} %get-tuple-element.70), channel_id=1, source_target_pairs={{0,16},{16,0},{1,17},{17,1},{2,18},{18,2},{3,19},{19,3},{4,20},{20... | collective-permute-start | bytes 1572872 | tf_op jit(solution)/shard_map/ppermute | solution.py:359
  54.6 1.7 %collective-permute-done.8.taken = bf16[2,512,256]{2,1,0:T(8,128)(2,1)S(1)} collective-permute-done((bf16[2,512,256]{2,1,0:T(8,128)(2,1)S(1)}, bf16[2,512,256]{2,1,0:T(8,128)(2,1)S(1)}, u32[]{:S(2)}, u32[]{:S(2)}) %collective-permute-start.8) | collective-permute-done | bytes 524320 | tf_op jit(solution)/shard_map/ppermute | solution.py:359
  56.3 0.1 pair_sum.1
  56.5 21.2 %all_to_all.10.terms = bf16[16,64,256]{2,1,0:T(8,128)(2,1)S(1)} all-to-all(bf16[16,64,256]{2,1,0:T(8,128)(2,1)S(1)} %pair_sum.1), channel_id=1, replica_groups=mesh['z'=16,'half'=2,'core'=2,'gy'=16] {'gy'}, dimensions={0} | all-to-all | bytes 1048576 | tf_op jit(solution)/shard_map/all_to_all | solution.py:389
  77.6 0.2 plane_sum.1
  77.9 41.3 %all_to_all.11.terms = bf16[32,4,128]{2,1,0:T(4,128)(2,1)S(1)} all-to-all(bf16[32,4,128]{2,1,0:T(4,128)(2,1)S(1)} %plane_sum.1), channel_id=1, replica_groups=mesh['z'=16,'half'=2,'core'=2,'gy'=16] {'z','half'}, dimensions={0} | all-to-all | bytes 65536 | tf_op jit(solution)/shard_map/all_to_all | solution.py:391
  119.2 0.7 line_sum.1
  (3 shorter events, 0.0 us)
Async XLA Ops:
  2.4 17.7 %collective-permute-start = (bf16[105,512]{1,0:T(8,128)(2,1)S(1)}, bf16[105,512]{1,0:T(8,128)(2,1)S(1)}, u32[]{:S(2)}, u32[]{:S(2)}) collective-permute-start(bf16[105,512]{1,0:T(8,128)(2,1)S(1)} %get-tuple-element.49), channel_id=1, source_target_pairs={{16,32},{32,16},{48,64},{64,48},{80,96},{96,80},{112,128},{128,112... | collective-permute-start | bytes 322568 | tf_op jit(solution)/shard_map/ppermute | solution.py:236
  11.2 8.8 %collective-permute-start.1 = (bf16[105,512]{1,0:T(8,128)(2,1)S(1)}, bf16[105,512]{1,0:T(8,128)(2,1)S(1)}, u32[]{:S(2)}, u32[]{:S(2)}) collective-permute-start(bf16[105,512]{1,0:T(8,128)(2,1)S(1)} %get-tuple-element.50), channel_id=1, source_target_pairs={{0,16},{16,0},{32,48},{48,32},{64,80},{80,64},{96,112},{112,96},{1... | collective-permute-start | bytes 322568 | tf_op jit(solution)/shard_map/ppermute | solution.py:236
  20.4 2.6 %copy-start = (f32[343]{0:T(512)S(1)}, f32[343]{0:T(512)}, u32[]{:S(2)}) copy-start(f32[343]{0:T(512)} %param.4) | copy-start | bytes 4120
  20.4 3.0 %collective-permute-start.2 = (bf16[105,512]{1,0:T(8,128)(2,1)S(1)}, bf16[105,512]{1,0:T(8,128)(2,1)S(1)}, u32[]{:S(2)}, u32[]{:S(2)}) collective-permute-start(bf16[105,512]{1,0:T(8,128)(2,1)S(1)} %get-tuple-element.54), channel_id=1, source_target_pairs={{1,2},{2,1},{3,4},{4,3},{5,6},{6,5},{7,8},{8,7},{9,10},{10,9},{11,... | collective-permute-start | bytes 322568 | tf_op jit(solution)/shard_map/ppermute | solution.py:236
  21.0 6.3 %collective-permute-start.3 = (bf16[105,512]{1,0:T(8,128)(2,1)S(1)}, bf16[105,512]{1,0:T(8,128)(2,1)S(1)}, u32[]{:S(2)}, u32[]{:S(2)}) collective-permute-start(bf16[105,512]{1,0:T(8,128)(2,1)S(1)} %get-tuple-element.55), channel_id=1, source_target_pairs={{0,1},{1,0},{2,3},{3,2},{4,5},{5,4},{6,7},{7,6},{8,9},{9,8},{10,11... | collective-permute-start | bytes 322568 | tf_op jit(solution)/shard_map/ppermute | solution.py:236
  28.0 10.1 %collective-permute-start.4 = (bf16[105,512]{1,0:T(8,128)(2,1)S(1)}, bf16[105,512]{1,0:T(8,128)(2,1)S(1)}, u32[]{:S(2)}, u32[]{:S(2)}) collective-permute-start(bf16[105,512]{1,0:T(8,128)(2,1)S(1)} %get-tuple-element.59), channel_id=1, source_target_pairs={{16,32},{32,16},{48,64},{64,48},{80,96},{96,80},{112,128},{128,112... | collective-permute-start | bytes 322568 | tf_op jit(solution)/shard_map/ppermute | solution.py:236
  35.2 3.2 %collective-permute-start.5 = (bf16[105,512]{1,0:T(8,128)(2,1)S(1)}, bf16[105,512]{1,0:T(8,128)(2,1)S(1)}, u32[]{:S(2)}, u32[]{:S(2)}) collective-permute-start(bf16[105,512]{1,0:T(8,128)(2,1)S(1)} %get-tuple-element.60), channel_id=1, source_target_pairs={{0,16},{16,0},{32,48},{48,32},{64,80},{80,64},{96,112},{112,96},{1... | collective-permute-start | bytes 322568 | tf_op jit(solution)/shard_map/ppermute | solution.py:236
  38.6 7.4 %collective-permute-start.6 = (bf16[105,512]{1,0:T(8,128)(2,1)S(1)}, bf16[105,512]{1,0:T(8,128)(2,1)S(1)}, u32[]{:S(2)}, u32[]{:S(2)}) collective-permute-start(bf16[105,512]{1,0:T(8,128)(2,1)S(1)} %get-tuple-element.64), channel_id=1, source_target_pairs={{1,2},{2,1},{3,4},{4,3},{5,6},{6,5},{7,8},{8,7},{9,10},{10,9},{11,... | collective-permute-start | bytes 322568 | tf_op jit(solution)/shard_map/ppermute | solution.py:236
  39.3 11.7 %collective-permute-start.7 = (bf16[105,512]{1,0:T(8,128)(2,1)S(1)}, bf16[105,512]{1,0:T(8,128)(2,1)S(1)}, u32[]{:S(2)}, u32[]{:S(2)}) collective-permute-start(bf16[105,512]{1,0:T(8,128)(2,1)S(1)} %get-tuple-element.65), channel_id=1, source_target_pairs={{0,1},{1,0},{2,3},{3,2},{4,5},{5,4},{6,7},{7,6},{8,9},{9,8},{10,11... | collective-permute-start | bytes 322568 | tf_op jit(solution)/shard_map/ppermute | solution.py:236
  52.5 3.8 %collective-permute-start.8 = (bf16[2,512,256]{2,1,0:T(8,128)(2,1)S(1)}, bf16[2,512,256]{2,1,0:T(8,128)(2,1)S(1)}, u32[]{:S(2)}, u32[]{:S(2)}) collective-permute-start(bf16[2,512,256]{2,1,0:T(8,128)(2,1)S(1)} %get-tuple-element.70), channel_id=1, source_target_pairs={{0,16},{16,0},{1,17},{17,1},{2,18},{18,2},{3,19},{19,3},{4,20},{20... | collective-permute-start | bytes 1572872 | tf_op jit(solution)/shard_map/ppermute | solution.py:359

commit v7 on v5

--- a/solution.py
+++ b/solution.py
@@ -307,15 +307,11 @@
 
         def shuffle():
             place = lax.broadcasted_iota(jnp.int32, (orbital_count, 1), 0)
-            low = lax.bitwise_and(place, quarter - 1)
-            line = lax.shift_right_logical(low, block_rows.bit_length() - 1)
+            line = lax.shift_right_logical(lax.bitwise_and(place, quarter - 1), block_rows.bit_length() - 1)
             side = lax.shift_right_logical(place, quarter.bit_length() - 1)
-            order = (
-                line * (4 * block_rows)
-                + lax.bitwise_and(side, 1) * (2 * block_rows)
-                + lax.shift_right_logical(side, 1) * block_rows
-                + lax.bitwise_and(low, block_rows - 1)
-            )
+            core = lax.bitwise_xor(lax.shift_right_logical(side, 1), lax.axis_index("core"))
+            block = line * 4 + lax.bitwise_and(side, 1) * 2 + core
+            order = block * block_rows + lax.bitwise_and(place, block_rows - 1)
             return one_hot(order, orbital_count)
 
         def shuffled_product(own_columns, lifted, partial, order, shuffled):
@@ -335,20 +331,10 @@
             own_y, side_y, own, far_in, near_in, field, lifted, potential, order, shuffled,
             filtered, keep, give, image, corner, face, wide, rows,
         ):
-            core = lax.axis_index("core")
-
             def gram(which, left, right):
                 product = (dot_rows(left, right) * norm_scale).astype(BF16)
-
-                @pl.when(core == 0)
-                def _():
-                    keep[which] = product[:, :half]
-                    give[which] = product[:, half:]
-
-                @pl.when(core == 1)
-                def _():
-                    keep[which] = product[:, half:]
-                    give[which] = product[:, :half]
+                keep[which] = product[:, :half]
+                give[which] = product[:, half:]
 
             close(own_y, side_y, own, far_in, near_in, image, corner, face, wide)
             image[OWN:, :] = jnp.zeros((padded - OWN, orbital_count), F32)
@@ -371,7 +357,6 @@
             half_grams,
             half_grams,
             scratch=staged(padded, RIM, FACE, message_rows, padded),
-            results=(0,),
         )(own_y, side_y, own, far, near, field, lifted, weight, order, shuffled)
         taken = lax.ppermute(given, "core", [(0, 1), (1, 0)])
 

time: 118 us -> 118 us (level)
  blocking collectives: 58.5 us -> 27 us
  starting transfers between devices: 37.5 us -> 57.8 us
  waiting for transfers between devices: 11.4 us -> 22 us
    all_to_all x1 -> x0, blocking collectives: 31.5 us -> none  [per_device(): terms = lax.all_to_all(terms, 'z', 0, 0, tiled=True)]
    all_to_all x0 -> x1, starting transfers between devices: none -> 20.3 us  [per_device(): terms = lax.all_to_all(terms, 'z', 0, 0, tiled=True)]
    all_to_all x0 -> x1, waiting for transfers between devices: none -> 10.7 us  [per_device(): terms = lax.all_to_all(terms, 'z', 0, 0, tiled=True)]
  transfers between devices with their start and end apart: 9 -> 10, of which waited for: 5 -> 6; matrix products, arithmetic and copies ran while one was open for 0% -> 1% of each run, Pallas kernels for 2% -> 2%
where the time goes in v7:
time: 118 us; the launch traced here: 117 us
  starting transfers between devices  57.8 us (49%)
  blocking collectives  27 us (23%)
  waiting for transfers between devices  22 us (19%)
  Pallas kernels  8.23 us (7%)
    all_to_all x1, blocking collectives, per_device(): terms = lax.all_to_all(terms, ('half', 'gy'), 0, 0, tiled=True)  27 us
    all_to_all x1, starting transfers between devices, per_device(): terms = lax.all_to_all(terms, 'z', 0, 0, tiled=True)  20.3 us
    ppermute x4, starting transfers between devices, swapped(): lax.ppermute(near, axis, pairs(0))  18.1 us
    ppermute x4, starting transfers between devices, swapped(): lax.ppermute(far, axis, pairs(1))  17.3 us
    all_to_all x1, waiting for transfers between devices, per_device(): terms = lax.all_to_all(terms, 'z', 0, 0, tiled=True)  10.7 us
    ppermute x4, waiting for transfers between devices, swapped(): lax.ppermute(near, axis, pairs(0))  9.23 us
    pallas_call x12, Pallas kernels, run(): pl.pallas_call(kernel, out_shape=[jax.ShapeDtypeStruct(*shape) if i in re...  8.23 us
  transfers between devices with their start and end apart: 10, of which 6 were waited for; matrix products, arithmetic and copies ran while one was open for 1% of the time, Pallas kernels for 2%

profile of v7, /device:TPU:1, one launch (start us, length us, event | category | flops | bytes accessed | tf_op | source)
XLA Modules:
  0.0 116.7 jit_solution(527266543709232523)
XLA Ops:
  0.6 1.7 %prepare.1 = (bf16[343,512]{1,0:T(8,128)(2,1)S(1)}, bf16[512,512]{1,0:T(8,128)(2,1)S(1)}, bf16[56,343]{1,0:T(8,128)(2,1)S(1)}, bf16[105,512]{1,0:T(8,128)(2,1)S(1)}, bf16[105,512]{1,0:T(8,128)(2,1)S(1)}) custom-call(bf16[343,512]{1,0:T(8,128)(2,1)} %field_in.1, bf16[512,512]{1,0:T(8,128)(2,1)} %stiffness_in.1), custom_call_target="tpu_custom_call" | custom-call | tf_op jit(solution)/shard_map/prepare/pallas_call | solution.py:64
  2.4 8.8 %collective-permute-start = (bf16[105,512]{1,0:T(8,128)(2,1)S(1)}, bf16[105,512]{1,0:T(8,128)(2,1)S(1)}, u32[]{:S(2)}, u32[]{:S(2)}) collective-permute-start(bf16[105,512]{1,0:T(8,128)(2,1)S(1)} %get-tuple-element.49), channel_id=1, source_target_pairs={{16,32},{32,16},{48,64},{64,48},{80,96},{96,80},{112,128},{128,112... | collective-permute-start | bytes 322568 | tf_op jit(solution)/shard_map/ppermute | solution.py:236
  11.2 7.9 %collective-permute-start.1 = (bf16[105,512]{1,0:T(8,128)(2,1)S(1)}, bf16[105,512]{1,0:T(8,128)(2,1)S(1)}, u32[]{:S(2)}, u32[]{:S(2)}) collective-permute-start(bf16[105,512]{1,0:T(8,128)(2,1)S(1)} %get-tuple-element.50), channel_id=1, source_target_pairs={{0,16},{16,0},{32,48},{48,32},{64,80},{80,64},{96,112},{112,96},{1... | collective-permute-start | bytes 322568 | tf_op jit(solution)/shard_map/ppermute | solution.py:236
  19.1 1.0 arrange.1
  20.1 0.3 cross.2
  20.4 0.0 copy-start
  20.4 0.7 collective-permute-start.2
  21.0 1.9 %collective-permute-start.3 = (bf16[105,512]{1,0:T(8,128)(2,1)S(1)}, bf16[105,512]{1,0:T(8,128)(2,1)S(1)}, u32[]{:S(2)}, u32[]{:S(2)}) collective-permute-start(bf16[105,512]{1,0:T(8,128)(2,1)S(1)} %get-tuple-element.55), channel_id=1, source_target_pairs={{0,1},{1,0},{2,3},{3,2},{4,5},{5,4},{6,7},{7,6},{8,9},{9,8},{10,11... | collective-permute-start | bytes 322568 | tf_op jit(solution)/shard_map/ppermute | solution.py:236
  23.0 0.1 broadcast_in_dim.4.potential
  23.1 0.3 gather_row.2.own
  23.4 4.0 %collective-permute-done.3.near_in = bf16[105,512]{1,0:T(8,128)(2,1)S(1)} collective-permute-done((bf16[105,512]{1,0:T(8,128)(2,1)S(1)}, bf16[105,512]{1,0:T(8,128)(2,1)S(1)}, u32[]{:S(2)}, u32[]{:S(2)}) %collective-permute-start.3) | collective-permute-done | bytes 107552 | tf_op jit(solution)/shard_map/ppermute | solution.py:236
  27.3 0.7 lift.1
  28.0 7.2 %collective-permute-start.4 = (bf16[105,512]{1,0:T(8,128)(2,1)S(1)}, bf16[105,512]{1,0:T(8,128)(2,1)S(1)}, u32[]{:S(2)}, u32[]{:S(2)}) collective-permute-start(bf16[105,512]{1,0:T(8,128)(2,1)S(1)} %get-tuple-element.59), channel_id=1, source_target_pairs={{16,32},{32,16},{48,64},{64,48},{80,96},{96,80},{112,128},{128,112... | collective-permute-start | bytes 322568 | tf_op jit(solution)/shard_map/ppermute | solution.py:236
  35.2 1.9 %collective-permute-start.5 = (bf16[105,512]{1,0:T(8,128)(2,1)S(1)}, bf16[105,512]{1,0:T(8,128)(2,1)S(1)}, u32[]{:S(2)}, u32[]{:S(2)}) collective-permute-start(bf16[105,512]{1,0:T(8,128)(2,1)S(1)} %get-tuple-element.60), channel_id=1, source_target_pairs={{0,16},{16,0},{32,48},{48,32},{64,80},{80,64},{96,112},{112,96},{1... | collective-permute-start | bytes 322568 | tf_op jit(solution)/shard_map/ppermute | solution.py:236
  37.1 0.7 shuffled_product.1
  37.7 0.4 collective-permute-done.4.far_in
  38.1 0.3 collective-permute-done.5.near_in
  38.4 0.2 cross.3
  38.6 0.7 collective-permute-start.6
  39.3 6.4 %collective-permute-start.7 = (bf16[105,512]{1,0:T(8,128)(2,1)S(1)}, bf16[105,512]{1,0:T(8,128)(2,1)S(1)}, u32[]{:S(2)}, u32[]{:S(2)}) collective-permute-start(bf16[105,512]{1,0:T(8,128)(2,1)S(1)} %get-tuple-element.65), channel_id=1, source_target_pairs={{0,1},{1,0},{2,3},{3,2},{4,5},{5,4},{6,7},{7,6},{8,9},{9,8},{10,11... | collective-permute-start | bytes 322568 | tf_op jit(solution)/shard_map/ppermute | solution.py:236
  45.7 0.3 gather_row.3.own
  46.0 5.0 %collective-permute-done.7.near_in = bf16[105,512]{1,0:T(8,128)(2,1)S(1)} collective-permute-done((bf16[105,512]{1,0:T(8,128)(2,1)S(1)}, bf16[105,512]{1,0:T(8,128)(2,1)S(1)}, u32[]{:S(2)}, u32[]{:S(2)}) %collective-permute-start.7) | collective-permute-done | bytes 107552 | tf_op jit(solution)/shard_map/ppermute | solution.py:236
  51.0 1.5 %filter_and_gram.1 = (bf16[343,512]{1,0:T(8,128)(2,1)S(1)}, bf16[2,512,256]{2,1,0:T(8,128)(2,1)S(1)}, bf16[2,512,256]{2,1,0:T(8,128)(2,1)S(1)}) custom-call(bf16[343,56]{1,0:T(8,128)(2,1)S(1)} %get-tuple-element.40.own_y, bf16[49,56]{1,0:T(8,128)(2,1)S(1)} %get-tuple-element.41.side_y, f32[343,512]{1,0:T(8,128)S(1)} %gather_row.3.own, ...), custom_call_target="tpu_custom_call" | custom-call | tf_op jit(solution)/shard_map/filter_and_gram/pallas_call | solution.py:64
  52.5 2.1 %collective-permute-start.8 = (bf16[2,512,256]{2,1,0:T(8,128)(2,1)S(1)}, bf16[2,512,256]{2,1,0:T(8,128)(2,1)S(1)}, u32[]{:S(2)}, u32[]{:S(2)}) collective-permute-start(bf16[2,512,256]{2,1,0:T(8,128)(2,1)S(1)} %get-tuple-element.70), channel_id=1, source_target_pairs={{0,16},{16,0},{1,17},{17,1},{2,18},{18,2},{3,19},{19,3},{4,20},{20... | collective-permute-start | bytes 1572872 | tf_op jit(solution)/shard_map/ppermute | solution.py:361
  54.6 1.7 %collective-permute-done.8.taken = bf16[2,512,256]{2,1,0:T(8,128)(2,1)S(1)} collective-permute-done((bf16[2,512,256]{2,1,0:T(8,128)(2,1)S(1)}, bf16[2,512,256]{2,1,0:T(8,128)(2,1)S(1)}, u32[]{:S(2)}, u32[]{:S(2)}) %collective-permute-start.8) | collective-permute-done | bytes 524320 | tf_op jit(solution)/shard_map/ppermute | solution.py:361
  56.3 0.1 pair_sum.1
  56.5 27.0 %all_to_all.10.terms = bf16[32,64,128]{2,1,0:T(8,128)(2,1)S(1)} all-to-all(bf16[32,64,128]{2,1,0:T(8,128)(2,1)S(1)} %bitcast.1), channel_id=1, replica_groups=mesh['z'=16,'half'=2,'core'=2,'gy'=16] {'half','gy'}, dimensions={0} | all-to-all | bytes 1048576 | tf_op jit(solution)/shard_map/all_to_all | solution.py:396
  83.5 0.8 plane_sum.1
  84.3 20.3 %all-to-all-start.1 = ((bf16[16,4,128]{2,1,0:T(4,128)(2,1)}), bf16[16,4,128]{2,1,0:T(4,128)(2,1)S(1)}, u32[]{:S(2)}, u32[]{:S(2)}) async-start(bf16[16,4,128]{2,1,0:T(4,128)(2,1)} %plane_sum.1), calls=%async_computation.1 | async-start | bytes 32768 | tf_op jit(solution)/shard_map/all_to_all | solution.py:398
  104.6 0.7 copy.8
  105.3 10.7 %all-to-all-done.1.terms = bf16[16,4,128]{2,1,0:T(4,128)(2,1)S(1)} async-done(((bf16[16,4,128]{2,1,0:T(4,128)(2,1)}), bf16[16,4,128]{2,1,0:T(4,128)(2,1)S(1)}, u32[]{:S(2)}, u32[]{:S(2)}) %all-to-all-start.1) | async-done | bytes 16416 | tf_op jit(solution)/shard_map/all_to_all | solution.py:398
  116.0 0.7 line_sum.1
  (5 shorter events, 0.0 us)
Async XLA Ops:
  2.4 17.7 %collective-permute-start = (bf16[105,512]{1,0:T(8,128)(2,1)S(1)}, bf16[105,512]{1,0:T(8,128)(2,1)S(1)}, u32[]{:S(2)}, u32[]{:S(2)}) collective-permute-start(bf16[105,512]{1,0:T(8,128)(2,1)S(1)} %get-tuple-element.49), channel_id=1, source_target_pairs={{16,32},{32,16},{48,64},{64,48},{80,96},{96,80},{112,128},{128,112... | collective-permute-start | bytes 322568 | tf_op jit(solution)/shard_map/ppermute | solution.py:236
  11.2 8.8 %collective-permute-start.1 = (bf16[105,512]{1,0:T(8,128)(2,1)S(1)}, bf16[105,512]{1,0:T(8,128)(2,1)S(1)}, u32[]{:S(2)}, u32[]{:S(2)}) collective-permute-start(bf16[105,512]{1,0:T(8,128)(2,1)S(1)} %get-tuple-element.50), channel_id=1, source_target_pairs={{0,16},{16,0},{32,48},{48,32},{64,80},{80,64},{96,112},{112,96},{1... | collective-permute-start | bytes 322568 | tf_op jit(solution)/shard_map/ppermute | solution.py:236
  20.4 2.6 %copy-start = (f32[343]{0:T(512)S(1)}, f32[343]{0:T(512)}, u32[]{:S(2)}) copy-start(f32[343]{0:T(512)} %param.4) | copy-start | bytes 4120
  20.4 3.0 %collective-permute-start.2 = (bf16[105,512]{1,0:T(8,128)(2,1)S(1)}, bf16[105,512]{1,0:T(8,128)(2,1)S(1)}, u32[]{:S(2)}, u32[]{:S(2)}) collective-permute-start(bf16[105,512]{1,0:T(8,128)(2,1)S(1)} %get-tuple-element.54), channel_id=1, source_target_pairs={{1,2},{2,1},{3,4},{4,3},{5,6},{6,5},{7,8},{8,7},{9,10},{10,9},{11,... | collective-permute-start | bytes 322568 | tf_op jit(solution)/shard_map/ppermute | solution.py:236
  21.0 6.3 %collective-permute-start.3 = (bf16[105,512]{1,0:T(8,128)(2,1)S(1)}, bf16[105,512]{1,0:T(8,128)(2,1)S(1)}, u32[]{:S(2)}, u32[]{:S(2)}) collective-permute-start(bf16[105,512]{1,0:T(8,128)(2,1)S(1)} %get-tuple-element.55), channel_id=1, source_target_pairs={{0,1},{1,0},{2,3},{3,2},{4,5},{5,4},{6,7},{7,6},{8,9},{9,8},{10,11... | collective-permute-start | bytes 322568 | tf_op jit(solution)/shard_map/ppermute | solution.py:236
  28.0 10.1 %collective-permute-start.4 = (bf16[105,512]{1,0:T(8,128)(2,1)S(1)}, bf16[105,512]{1,0:T(8,128)(2,1)S(1)}, u32[]{:S(2)}, u32[]{:S(2)}) collective-permute-start(bf16[105,512]{1,0:T(8,128)(2,1)S(1)} %get-tuple-element.59), channel_id=1, source_target_pairs={{16,32},{32,16},{48,64},{64,48},{80,96},{96,80},{112,128},{128,112... | collective-permute-start | bytes 322568 | tf_op jit(solution)/shard_map/ppermute | solution.py:236
  35.2 3.2 %collective-permute-start.5 = (bf16[105,512]{1,0:T(8,128)(2,1)S(1)}, bf16[105,512]{1,0:T(8,128)(2,1)S(1)}, u32[]{:S(2)}, u32[]{:S(2)}) collective-permute-start(bf16[105,512]{1,0:T(8,128)(2,1)S(1)} %get-tuple-element.60), channel_id=1, source_target_pairs={{0,16},{16,0},{32,48},{48,32},{64,80},{80,64},{96,112},{112,96},{1... | collective-permute-start | bytes 322568 | tf_op jit(solution)/shard_map/ppermute | solution.py:236
  38.6 7.4 %collective-permute-start.6 = (bf16[105,512]{1,0:T(8,128)(2,1)S(1)}, bf16[105,512]{1,0:T(8,128)(2,1)S(1)}, u32[]{:S(2)}, u32[]{:S(2)}) collective-permute-start(bf16[105,512]{1,0:T(8,128)(2,1)S(1)} %get-tuple-element.64), channel_id=1, source_target_pairs={{1,2},{2,1},{3,4},{4,3},{5,6},{6,5},{7,8},{8,7},{9,10},{10,9},{11,... | collective-permute-start | bytes 322568 | tf_op jit(solution)/shard_map/ppermute | solution.py:236
  39.3 11.7 %collective-permute-start.7 = (bf16[105,512]{1,0:T(8,128)(2,1)S(1)}, bf16[105,512]{1,0:T(8,128)(2,1)S(1)}, u32[]{:S(2)}, u32[]{:S(2)}) collective-permute-start(bf16[105,512]{1,0:T(8,128)(2,1)S(1)} %get-tuple-element.65), channel_id=1, source_target_pairs={{0,1},{1,0},{2,3},{3,2},{4,5},{5,4},{6,7},{7,6},{8,9},{9,8},{10,11... | collective-permute-start | bytes 322568 | tf_op jit(solution)/shard_map/ppermute | solution.py:236
  52.5 3.8 %collective-permute-start.8 = (bf16[2,512,256]{2,1,0:T(8,128)(2,1)S(1)}, bf16[2,512,256]{2,1,0:T(8,128)(2,1)S(1)}, u32[]{:S(2)}, u32[]{:S(2)}) collective-permute-start(bf16[2,512,256]{2,1,0:T(8,128)(2,1)S(1)} %get-tuple-element.70), channel_id=1, source_target_pairs={{0,16},{16,0},{1,17},{17,1},{2,18},{18,2},{3,19},{19,3},{4,20},{20... | collective-permute-start | bytes 1572872 | tf_op jit(solution)/shard_map/ppermute | solution.py:361
  84.3 31.7 %all-to-all-start.1 = ((bf16[16,4,128]{2,1,0:T(4,128)(2,1)}), bf16[16,4,128]{2,1,0:T(4,128)(2,1)S(1)}, u32[]{:S(2)}, u32[]{:S(2)}) async-start(bf16[16,4,128]{2,1,0:T(4,128)(2,1)} %plane_sum.1), calls=%async_computation.1 | async-start | bytes 32768 | tf_op jit(solution)/shard_map/all_to_all | solution.py:398

commit v8 on v7

--- a/solution.py
+++ b/solution.py
@@ -357,6 +357,7 @@
             half_grams,
             half_grams,
             scratch=staged(padded, RIM, FACE, message_rows, padded),
+            results=(0,),
         )(own_y, side_y, own, far, near, field, lifted, weight, order, shuffled)
         taken = lax.ppermute(given, "core", [(0, 1), (1, 0)])
 

time: 118 us -> 117 us (level)
  blocking collectives: 27 us -> 58.5 us
  starting transfers between devices: 57.8 us -> 37.5 us
  waiting for transfers between devices: 22 us -> 11.3 us
    all_to_all x0 -> x1, blocking collectives: none -> 31.5 us  [per_device(): terms = lax.all_to_all(terms, 'z', 0, 0, tiled=True)]
    all_to_all x1 -> x0, starting transfers between devices: 20.3 us -> none  [per_device(): terms = lax.all_to_all(terms, 'z', 0, 0, tiled=True)]
    all_to_all x1 -> x0, waiting for transfers between devices: 10.7 us -> none  [per_device(): terms = lax.all_to_all(terms, 'z', 0, 0, tiled=True)]
  transfers between devices with their start and end apart: 10 -> 9, of which waited for: 6 -> 5; matrix products, arithmetic and copies ran while one was open for 1% -> 0% of each run, Pallas kernels for 2% -> 2%
where the time goes in v8:
time: 117 us; the launch traced here: 116 us
  blocking collectives  58.5 us (50%)
  starting transfers between devices  37.5 us (32%)
  waiting for transfers between devices  11.3 us (10%)
  Pallas kernels  7.64 us (7%)
    all_to_all x1, blocking collectives, per_device(): terms = lax.all_to_all(terms, 'z', 0, 0, tiled=True)  31.5 us
    all_to_all x1, blocking collectives, per_device(): terms = lax.all_to_all(terms, ('half', 'gy'), 0, 0, tiled=True)  27 us
    ppermute x4, starting transfers between devices, swapped(): lax.ppermute(near, axis, pairs(0))  18.1 us
    ppermute x4, starting transfers between devices, swapped(): lax.ppermute(far, axis, pairs(1))  17.3 us
    ppermute x4, waiting for transfers between devices, swapped(): lax.ppermute(near, axis, pairs(0))  9.23 us
    pallas_call x12, Pallas kernels, run(): pl.pallas_call(kernel, out_shape=[jax.ShapeDtypeStruct(*shape) if i in re...  7.64 us
  transfers between devices with their start and end apart: 9, of which 5 were waited for; matrix products, arithmetic and copies ran while one was open for 0% of the time, Pallas kernels for 2%

profile of v8, /device:TPU:1, one launch (start us, length us, event | category | flops | bytes accessed | tf_op | source)
XLA Modules:
  0.0 115.9 jit_solution(5788564378240616022)
XLA Ops:
  0.6 1.7 %prepare.1 = (bf16[343,512]{1,0:T(8,128)(2,1)S(1)}, bf16[512,512]{1,0:T(8,128)(2,1)S(1)}, bf16[56,343]{1,0:T(8,128)(2,1)S(1)}, bf16[105,512]{1,0:T(8,128)(2,1)S(1)}, bf16[105,512]{1,0:T(8,128)(2,1)S(1)}) custom-call(bf16[343,512]{1,0:T(8,128)(2,1)} %field_in.1, bf16[512,512]{1,0:T(8,128)(2,1)} %stiffness_in.1), custom_call_target="tpu_custom_call" | custom-call | tf_op jit(solution)/shard_map/prepare/pallas_call | solution.py:64
  2.4 8.8 %collective-permute-start = (bf16[105,512]{1,0:T(8,128)(2,1)S(1)}, bf16[105,512]{1,0:T(8,128)(2,1)S(1)}, u32[]{:S(2)}, u32[]{:S(2)}) collective-permute-start(bf16[105,512]{1,0:T(8,128)(2,1)S(1)} %get-tuple-element.49), channel_id=1, source_target_pairs={{16,32},{32,16},{48,64},{64,48},{80,96},{96,80},{112,128},{128,112... | collective-permute-start | bytes 322568 | tf_op jit(solution)/shard_map/ppermute | solution.py:236
  11.2 7.9 %collective-permute-start.1 = (bf16[105,512]{1,0:T(8,128)(2,1)S(1)}, bf16[105,512]{1,0:T(8,128)(2,1)S(1)}, u32[]{:S(2)}, u32[]{:S(2)}) collective-permute-start(bf16[105,512]{1,0:T(8,128)(2,1)S(1)} %get-tuple-element.50), channel_id=1, source_target_pairs={{0,16},{16,0},{32,48},{48,32},{64,80},{80,64},{96,112},{112,96},{1... | collective-permute-start | bytes 322568 | tf_op jit(solution)/shard_map/ppermute | solution.py:236
  19.1 1.0 arrange.1
  20.1 0.0 collective-permute-done.1.near_in
  20.1 0.3 cross.2
  20.4 0.0 copy-start
  20.4 0.7 collective-permute-start.2
  21.0 1.9 %collective-permute-start.3 = (bf16[105,512]{1,0:T(8,128)(2,1)S(1)}, bf16[105,512]{1,0:T(8,128)(2,1)S(1)}, u32[]{:S(2)}, u32[]{:S(2)}) collective-permute-start(bf16[105,512]{1,0:T(8,128)(2,1)S(1)} %get-tuple-element.55), channel_id=1, source_target_pairs={{0,1},{1,0},{2,3},{3,2},{4,5},{5,4},{6,7},{7,6},{8,9},{9,8},{10,11... | collective-permute-start | bytes 322568 | tf_op jit(solution)/shard_map/ppermute | solution.py:236
  23.0 0.1 broadcast_in_dim.4.potential
  23.1 0.3 gather_row.2.own
  23.4 4.0 %collective-permute-done.3.near_in = bf16[105,512]{1,0:T(8,128)(2,1)S(1)} collective-permute-done((bf16[105,512]{1,0:T(8,128)(2,1)S(1)}, bf16[105,512]{1,0:T(8,128)(2,1)S(1)}, u32[]{:S(2)}, u32[]{:S(2)}) %collective-permute-start.3) | collective-permute-done | bytes 107552 | tf_op jit(solution)/shard_map/ppermute | solution.py:236
  27.3 0.7 lift.1
  28.0 7.2 %collective-permute-start.4 = (bf16[105,512]{1,0:T(8,128)(2,1)S(1)}, bf16[105,512]{1,0:T(8,128)(2,1)S(1)}, u32[]{:S(2)}, u32[]{:S(2)}) collective-permute-start(bf16[105,512]{1,0:T(8,128)(2,1)S(1)} %get-tuple-element.59), channel_id=1, source_target_pairs={{16,32},{32,16},{48,64},{64,48},{80,96},{96,80},{112,128},{128,112... | collective-permute-start | bytes 322568 | tf_op jit(solution)/shard_map/ppermute | solution.py:236
  35.2 1.9 %collective-permute-start.5 = (bf16[105,512]{1,0:T(8,128)(2,1)S(1)}, bf16[105,512]{1,0:T(8,128)(2,1)S(1)}, u32[]{:S(2)}, u32[]{:S(2)}) collective-permute-start(bf16[105,512]{1,0:T(8,128)(2,1)S(1)} %get-tuple-element.60), channel_id=1, source_target_pairs={{0,16},{16,0},{32,48},{48,32},{64,80},{80,64},{96,112},{112,96},{1... | collective-permute-start | bytes 322568 | tf_op jit(solution)/shard_map/ppermute | solution.py:236
  37.1 0.7 shuffled_product.1
  37.7 0.4 collective-permute-done.4.far_in
  38.1 0.3 collective-permute-done.5.near_in
  38.4 0.2 cross.3
  38.6 0.7 collective-permute-start.6
  39.3 6.4 %collective-permute-start.7 = (bf16[105,512]{1,0:T(8,128)(2,1)S(1)}, bf16[105,512]{1,0:T(8,128)(2,1)S(1)}, u32[]{:S(2)}, u32[]{:S(2)}) collective-permute-start(bf16[105,512]{1,0:T(8,128)(2,1)S(1)} %get-tuple-element.65), channel_id=1, source_target_pairs={{0,1},{1,0},{2,3},{3,2},{4,5},{5,4},{6,7},{7,6},{8,9},{9,8},{10,11... | collective-permute-start | bytes 322568 | tf_op jit(solution)/shard_map/ppermute | solution.py:236
  45.7 0.3 gather_row.3.own
  46.0 0.0 collective-permute-done.6.far_in
  46.0 5.0 %collective-permute-done.7.near_in = bf16[105,512]{1,0:T(8,128)(2,1)S(1)} collective-permute-done((bf16[105,512]{1,0:T(8,128)(2,1)S(1)}, bf16[105,512]{1,0:T(8,128)(2,1)S(1)}, u32[]{:S(2)}, u32[]{:S(2)}) %collective-permute-start.7) | collective-permute-done | bytes 107552 | tf_op jit(solution)/shard_map/ppermute | solution.py:236
  51.0 1.5 %filter_and_gram.1 = (bf16[343,512]{1,0:T(8,128)(2,1)}, bf16[2,512,256]{2,1,0:T(8,128)(2,1)S(1)}, bf16[2,512,256]{2,1,0:T(8,128)(2,1)S(1)}) custom-call(bf16[343,56]{1,0:T(8,128)(2,1)S(1)} %get-tuple-element.40.own_y, bf16[49,56]{1,0:T(8,128)(2,1)S(1)} %get-tuple-element.41.side_y, f32[343,512]{1,0:T(8,128)S(1)} %gather_row.3.own, ...), custom_call_target="tpu_custom_call" | custom-call | tf_op jit(solution)/shard_map/filter_and_gram/pallas_call | solution.py:64
  52.5 2.1 %collective-permute-start.8 = (bf16[2,512,256]{2,1,0:T(8,128)(2,1)S(1)}, bf16[2,512,256]{2,1,0:T(8,128)(2,1)S(1)}, u32[]{:S(2)}, u32[]{:S(2)}) collective-permute-start(bf16[2,512,256]{2,1,0:T(8,128)(2,1)S(1)} %get-tuple-element.70), channel_id=1, source_target_pairs={{0,16},{16,0},{1,17},{17,1},{2,18},{18,2},{3,19},{19,3},{4,20},{20... | collective-permute-start | bytes 1572872 | tf_op jit(solution)/shard_map/ppermute | solution.py:362
  54.6 1.7 %collective-permute-done.8.taken = bf16[2,512,256]{2,1,0:T(8,128)(2,1)S(1)} collective-permute-done((bf16[2,512,256]{2,1,0:T(8,128)(2,1)S(1)}, bf16[2,512,256]{2,1,0:T(8,128)(2,1)S(1)}, u32[]{:S(2)}, u32[]{:S(2)}) %collective-permute-start.8) | collective-permute-done | bytes 524320 | tf_op jit(solution)/shard_map/ppermute | solution.py:362
  56.3 0.1 pair_sum.1
  56.5 27.0 %all_to_all.10.terms = bf16[32,64,128]{2,1,0:T(8,128)(2,1)S(1)} all-to-all(bf16[32,64,128]{2,1,0:T(8,128)(2,1)S(1)} %bitcast.1), channel_id=1, replica_groups=mesh['z'=16,'half'=2,'core'=2,'gy'=16] {'half','gy'}, dimensions={0} | all-to-all | bytes 1048576 | tf_op jit(solution)/shard_map/all_to_all | solution.py:397
  83.5 0.2 plane_sum.1
  83.7 31.5 %all_to_all.11.terms = bf16[16,4,128]{2,1,0:T(4,128)(2,1)S(1)} all-to-all(bf16[16,4,128]{2,1,0:T(4,128)(2,1)S(1)} %plane_sum.1), channel_id=1, replica_groups=mesh['z'=16,'half'=2,'core'=2,'gy'=16] {'z'}, dimensions={0} | all-to-all | bytes 32768 | tf_op jit(solution)/shard_map/all_to_all | solution.py:399
  115.2 0.7 line_sum.1
  (3 shorter events, 0.0 us)
Async XLA Ops:
  2.4 17.7 %collective-permute-start = (bf16[105,512]{1,0:T(8,128)(2,1)S(1)}, bf16[105,512]{1,0:T(8,128)(2,1)S(1)}, u32[]{:S(2)}, u32[]{:S(2)}) collective-permute-start(bf16[105,512]{1,0:T(8,128)(2,1)S(1)} %get-tuple-element.49), channel_id=1, source_target_pairs={{16,32},{32,16},{48,64},{64,48},{80,96},{96,80},{112,128},{128,112... | collective-permute-start | bytes 322568 | tf_op jit(solution)/shard_map/ppermute | solution.py:236
  11.2 8.8 %collective-permute-start.1 = (bf16[105,512]{1,0:T(8,128)(2,1)S(1)}, bf16[105,512]{1,0:T(8,128)(2,1)S(1)}, u32[]{:S(2)}, u32[]{:S(2)}) collective-permute-start(bf16[105,512]{1,0:T(8,128)(2,1)S(1)} %get-tuple-element.50), channel_id=1, source_target_pairs={{0,16},{16,0},{32,48},{48,32},{64,80},{80,64},{96,112},{112,96},{1... | collective-permute-start | bytes 322568 | tf_op jit(solution)/shard_map/ppermute | solution.py:236
  20.4 2.6 %copy-start = (f32[343]{0:T(512)S(1)}, f32[343]{0:T(512)}, u32[]{:S(2)}) copy-start(f32[343]{0:T(512)} %param.4) | copy-start | bytes 4120
  20.4 3.0 %collective-permute-start.2 = (bf16[105,512]{1,0:T(8,128)(2,1)S(1)}, bf16[105,512]{1,0:T(8,128)(2,1)S(1)}, u32[]{:S(2)}, u32[]{:S(2)}) collective-permute-start(bf16[105,512]{1,0:T(8,128)(2,1)S(1)} %get-tuple-element.54), channel_id=1, source_target_pairs={{1,2},{2,1},{3,4},{4,3},{5,6},{6,5},{7,8},{8,7},{9,10},{10,9},{11,... | collective-permute-start | bytes 322568 | tf_op jit(solution)/shard_map/ppermute | solution.py:236
  21.0 6.3 %collective-permute-start.3 = (bf16[105,512]{1,0:T(8,128)(2,1)S(1)}, bf16[105,512]{1,0:T(8,128)(2,1)S(1)}, u32[]{:S(2)}, u32[]{:S(2)}) collective-permute-start(bf16[105,512]{1,0:T(8,128)(2,1)S(1)} %get-tuple-element.55), channel_id=1, source_target_pairs={{0,1},{1,0},{2,3},{3,2},{4,5},{5,4},{6,7},{7,6},{8,9},{9,8},{10,11... | collective-permute-start | bytes 322568 | tf_op jit(solution)/shard_map/ppermute | solution.py:236
  28.0 10.1 %collective-permute-start.4 = (bf16[105,512]{1,0:T(8,128)(2,1)S(1)}, bf16[105,512]{1,0:T(8,128)(2,1)S(1)}, u32[]{:S(2)}, u32[]{:S(2)}) collective-permute-start(bf16[105,512]{1,0:T(8,128)(2,1)S(1)} %get-tuple-element.59), channel_id=1, source_target_pairs={{16,32},{32,16},{48,64},{64,48},{80,96},{96,80},{112,128},{128,112... | collective-permute-start | bytes 322568 | tf_op jit(solution)/shard_map/ppermute | solution.py:236
  35.2 3.2 %collective-permute-start.5 = (bf16[105,512]{1,0:T(8,128)(2,1)S(1)}, bf16[105,512]{1,0:T(8,128)(2,1)S(1)}, u32[]{:S(2)}, u32[]{:S(2)}) collective-permute-start(bf16[105,512]{1,0:T(8,128)(2,1)S(1)} %get-tuple-element.60), channel_id=1, source_target_pairs={{0,16},{16,0},{32,48},{48,32},{64,80},{80,64},{96,112},{112,96},{1... | collective-permute-start | bytes 322568 | tf_op jit(solution)/shard_map/ppermute | solution.py:236
  38.6 7.4 %collective-permute-start.6 = (bf16[105,512]{1,0:T(8,128)(2,1)S(1)}, bf16[105,512]{1,0:T(8,128)(2,1)S(1)}, u32[]{:S(2)}, u32[]{:S(2)}) collective-permute-start(bf16[105,512]{1,0:T(8,128)(2,1)S(1)} %get-tuple-element.64), channel_id=1, source_target_pairs={{1,2},{2,1},{3,4},{4,3},{5,6},{6,5},{7,8},{8,7},{9,10},{10,9},{11,... | collective-permute-start | bytes 322568 | tf_op jit(solution)/shard_map/ppermute | solution.py:236
  39.3 11.7 %collective-permute-start.7 = (bf16[105,512]{1,0:T(8,128)(2,1)S(1)}, bf16[105,512]{1,0:T(8,128)(2,1)S(1)}, u32[]{:S(2)}, u32[]{:S(2)}) collective-permute-start(bf16[105,512]{1,0:T(8,128)(2,1)S(1)} %get-tuple-element.65), channel_id=1, source_target_pairs={{0,1},{1,0},{2,3},{3,2},{4,5},{5,4},{6,7},{7,6},{8,9},{9,8},{10,11... | collective-permute-start | bytes 322568 | tf_op jit(solution)/shard_map/ppermute | solution.py:236
  52.5 3.8 %collective-permute-start.8 = (bf16[2,512,256]{2,1,0:T(8,128)(2,1)S(1)}, bf16[2,512,256]{2,1,0:T(8,128)(2,1)S(1)}, u32[]{:S(2)}, u32[]{:S(2)}) collective-permute-start(bf16[2,512,256]{2,1,0:T(8,128)(2,1)S(1)} %get-tuple-element.70), channel_id=1, source_target_pairs={{0,16},{16,0},{1,17},{17,1},{2,18},{18,2},{3,19},{19,3},{4,20},{20... | collective-permute-start | bytes 1572872 | tf_op jit(solution)/shard_map/ppermute | solution.py:362

commit v9 on v8

--- a/solution.py
+++ b/solution.py
@@ -129,7 +129,7 @@
 
 
 def inside_y():
-    return (lax.axis_index("gy") > 0).astype(F32)
+    return (lax.axis_index("row") + lax.axis_index("line") > 0).astype(F32)
 
 
 def prepare(field_in, stiffness_in, field, stiffness, rim_own, far, near, wide, upward, downward, sems):
@@ -180,7 +180,7 @@
     upward[...] = jnp.zeros_like(upward)
     stage_parts(wide[:FACE, :], upward)
     raw[...] = downward[...].astype(BF16)
-    send(lax.bitwise_and(lax.axis_index("gy"), 1) == 1, far, near, upward, downward)
+    send(lax.bitwise_and(lax.axis_index("line"), 1) == 1, far, near, upward, downward)
 
 
 def gather_row(own_x, face_y, edge_y, partial, field, above_x, rim, raw, own, corner, face):
@@ -201,7 +201,7 @@
         face[...] = parts[:FACE, :] + parts[FACE : 2 * FACE, :]
         wide[...] = above[...].astype(F32)
 
-    chosen(lax.bitwise_and(lax.axis_index("gy"), 1) == 1, (far_in, near_in), arrived)
+    chosen(lax.bitwise_and(lax.axis_index("line"), 1) == 1, (far_in, near_in), arrived)
     corner[:DEG, :] = wide[DEG : 2 * DEG, :]
     corner[DEG:, :] = wide[RIM:, :]
     image[:OWN, :] = own[...] + dot(own_y[...], wide[:RIM, :].astype(BF16))
@@ -225,9 +225,13 @@
 def solution(mesh):
     length_x, length_y = mesh.shape["gx"], mesh.shape["gy"]
     length_z = length_x // 4
-    split_mesh = Mesh(mesh.devices.reshape(length_z, 2, 2, length_y), ("z", "half", "core", "gy"))
-    gx = ("z", "half", "core")
-    every = gx + ("gy",)
+    length_row = max(1, length_y // 4)
+    line = length_y // length_row
+    split_mesh = Mesh(
+        mesh.devices.reshape(length_z, 2, 2, length_row, line), ("z", "half", "core", "row", "line")
+    )
+    gx, gy = ("z", "half", "core"), ("row", "line")
+    every = gx + gy
 
     def swapped(far, near, axis, length):
         def pairs(first):
@@ -289,7 +293,7 @@
                 message,
                 scratch=staged(message_rows, FACE, message_rows, message_rows),
             )(rim_x, face_x, partial, values, far, near)
-            far, near = swapped(far, near, "gy", length_y)
+            far, near = swapped(far, near, gy, length_y)
             own = call(gather_row, (by_orbital(OWN), F32), scratch=staged(RIM, FACE))(
                 own_x, face_y, edge_y, partial, values, above_x, rim, raw
             )[0]
@@ -367,9 +371,15 @@
                 for side in range(2):
                     part = total[:, side * quarter : (side + 1) * quarter]
                     for j in range(length_y):
-                        out[side, j, which * block_cols : (which + 1) * block_cols] = part[
+                        out[j // line, side * line + j % line, which * block_cols : (which + 1) * block_cols] = part[
                             j * block_cols : (j + 1) * block_cols
                         ]
+
+        def row_sum(terms, out):
+            total = terms[0].astype(F32)
+            for source in range(1, length_row):
+                total += terms[source].astype(F32)
+            out[...] = total.astype(BF16)
 
         wide = 2 * block_cols
         fold = max(1, 128 // wide)
@@ -377,7 +387,7 @@
 
         def plane_sum(terms, out):
             total = terms[0].astype(F32)
-            for source in range(1, 2 * length_y):
+            for source in range(1, 2 * line):
                 total += terms[source].astype(F32)
             total = total.T.reshape(length_z, block_rows, wide)
             for part in range(fold):
@@ -392,9 +402,10 @@
                 ham[part * short : (part + 1) * short, :] = block[:, :block_cols]
                 correlation[part * short : (part + 1) * short, :] = block[:, block_cols:]
 
-        terms = call(pair_sum, ((2, length_y, wide, quarter), BF16))(kept, taken)[0]
-        terms = terms.reshape(2 * length_y, wide, quarter)
-        terms = lax.all_to_all(terms, ("half", "gy"), 0, 0, tiled=True)
+        terms = call(pair_sum, ((length_row, 2 * line, wide, quarter), BF16))(kept, taken)[0]
+        terms = lax.all_to_all(terms, "row", 0, 0, tiled=True)
+        terms = call(row_sum, ((2 * line, wide, quarter), BF16))(terms)[0]
+        terms = lax.all_to_all(terms, ("half", "line"), 0, 0, tiled=True)
         terms = call(plane_sum, ((length_z, short, fold * wide), BF16))(terms)[0]
         terms = lax.all_to_all(terms, "z", 0, 0, tiled=True)
         block = (block_rows, block_cols)
@@ -405,6 +416,6 @@
         per_device,
         mesh=split_mesh,
         in_specs=(P(every, None), P(every), P()),
-        out_specs=(P(every, None), P(gx, "gy"), P(gx, "gy")),
+        out_specs=(P(every, None), P(gx, gy), P(gx, gy)),
         check_vma=False,
     )

time: 117 us -> 118 us (level)
  the two profiles are of different devices: /device:TPU:1 before, /device:TPU:2 now
where the time goes in v9:
time: 118 us
  blocking collectives  61.4 us (52%)
  starting transfers between devices  32.8 us (28%)
  waiting for transfers between devices  15.3 us (13%)
  Pallas kernels  7.66 us (6%)
    all_to_all x1, blocking collectives, per_device(): terms = lax.all_to_all(terms, 'z', 0, 0, tiled=True)  32.9 us
    ppermute x4, starting transfers between devices, swapped(): lax.ppermute(near, axis, pairs(0))  22.4 us
    all_to_all x1, blocking collectives, per_device(): terms = lax.all_to_all(terms, ('half', 'line'), 0, 0, tiled=True)  16.3 us
    all_to_all x1, blocking collectives, per_device(): terms = lax.all_to_all(terms, 'row', 0, 0, tiled=True)  12.2 us
    ppermute x4, waiting for transfers between devices, swapped(): lax.ppermute(far, axis, pairs(1))  8.95 us
    ppermute x4, starting transfers between devices, swapped(): lax.ppermute(far, axis, pairs(1))  8.32 us
    pallas_call x13, Pallas kernels, run(): pl.pallas_call(kernel, out_shape=[jax.ShapeDtypeStruct(*shape) if i in re...  7.66 us
    ppermute x4, waiting for transfers between devices, swapped(): lax.ppermute(near, axis, pairs(0))  4.59 us
  transfers between devices with their start and end apart: 9, of which 6 were waited for; matrix products, arithmetic and copies ran while one was open for 0% of the time, Pallas kernels for 2%

profile of v9, /device:TPU:2, one launch (start us, length us, event | category | flops | bytes accessed | tf_op | source)
XLA Modules:
  0.0 118.0 jit_solution(11797804630024613921)
XLA Ops:
  0.6 1.8 %prepare.1 = (bf16[343,512]{1,0:T(8,128)(2,1)S(1)}, bf16[512,512]{1,0:T(8,128)(2,1)S(1)}, bf16[56,343]{1,0:T(8,128)(2,1)S(1)}, bf16[105,512]{1,0:T(8,128)(2,1)S(1)}, bf16[105,512]{1,0:T(8,128)(2,1)S(1)}) custom-call(bf16[343,512]{1,0:T(8,128)(2,1)} %field_in.1, bf16[512,512]{1,0:T(8,128)(2,1)} %stiffness_in.1), custom_call_target="tpu_custom_call" | custom-call | tf_op jit(solution)/shard_map/prepare/pallas_call | solution.py:64
  2.4 0.7 collective-permute-start
  3.1 9.1 %collective-permute-start.1 = (bf16[105,512]{1,0:T(8,128)(2,1)S(1)}, bf16[105,512]{1,0:T(8,128)(2,1)S(1)}, u32[]{:S(2)}, u32[]{:S(2)}) collective-permute-start(bf16[105,512]{1,0:T(8,128)(2,1)S(1)} %get-tuple-element.50), channel_id=1, source_target_pairs={{0,16},{16,0},{32,48},{48,32},{64,80},{80,64},{96,112},{112,96},{1... | collective-permute-start | bytes 322568 | tf_op jit(solution)/shard_map/ppermute | solution.py:240
  12.2 1.0 arrange.1
  13.2 0.3 cross.2
  13.4 2.8 %collective-permute-start.2 = (bf16[105,512]{1,0:T(8,128)(2,1)S(1)}, bf16[105,512]{1,0:T(8,128)(2,1)S(1)}, u32[]{:S(2)}, u32[]{:S(2)}) collective-permute-start(bf16[105,512]{1,0:T(8,128)(2,1)S(1)} %get-tuple-element.54), channel_id=1, source_target_pairs={{1,2},{2,1},{3,4},{4,3},{5,6},{6,5},{7,8},{8,7},{9,10},{10,9},{11,... | collective-permute-start | bytes 322568 | tf_op jit(solution)/shard_map/ppermute | solution.py:240
  16.2 2.4 %collective-permute-start.3 = (bf16[105,512]{1,0:T(8,128)(2,1)S(1)}, bf16[105,512]{1,0:T(8,128)(2,1)S(1)}, u32[]{:S(2)}, u32[]{:S(2)}) collective-permute-start(bf16[105,512]{1,0:T(8,128)(2,1)S(1)} %get-tuple-element.55), channel_id=1, source_target_pairs={{0,1},{1,0},{2,3},{3,2},{4,5},{5,4},{6,7},{7,6},{8,9},{9,8},{10,11... | collective-permute-start | bytes 322568 | tf_op jit(solution)/shard_map/ppermute | solution.py:240
  18.6 0.1 broadcast_in_dim.4.potential
  18.7 0.3 gather_row.2.own
  19.0 4.7 %collective-permute-done.2.far_in = bf16[105,512]{1,0:T(8,128)(2,1)S(1)} collective-permute-done((bf16[105,512]{1,0:T(8,128)(2,1)S(1)}, bf16[105,512]{1,0:T(8,128)(2,1)S(1)}, u32[]{:S(2)}, u32[]{:S(2)}) %collective-permute-start.2) | collective-permute-done | bytes 107552 | tf_op jit(solution)/shard_map/ppermute | solution.py:240
  23.8 2.7 %collective-permute-done.3.near_in = bf16[105,512]{1,0:T(8,128)(2,1)S(1)} collective-permute-done((bf16[105,512]{1,0:T(8,128)(2,1)S(1)}, bf16[105,512]{1,0:T(8,128)(2,1)S(1)}, u32[]{:S(2)}, u32[]{:S(2)}) %collective-permute-start.3) | collective-permute-done | bytes 107552 | tf_op jit(solution)/shard_map/ppermute | solution.py:240
  26.5 0.7 lift.1
  27.1 0.7 collective-permute-start.4
  27.8 9.0 %collective-permute-start.5 = (bf16[105,512]{1,0:T(8,128)(2,1)S(1)}, bf16[105,512]{1,0:T(8,128)(2,1)S(1)}, u32[]{:S(2)}, u32[]{:S(2)}) collective-permute-start(bf16[105,512]{1,0:T(8,128)(2,1)S(1)} %get-tuple-element.60), channel_id=1, source_target_pairs={{0,16},{16,0},{32,48},{48,32},{64,80},{80,64},{96,112},{112,96},{1... | collective-permute-start | bytes 322568 | tf_op jit(solution)/shard_map/ppermute | solution.py:240
  36.8 0.7 shuffled_product.1
  37.4 0.3 collective-permute-done.5.near_in
  37.7 0.2 cross.3
  38.0 4.2 %collective-permute-start.6 = (bf16[105,512]{1,0:T(8,128)(2,1)S(1)}, bf16[105,512]{1,0:T(8,128)(2,1)S(1)}, u32[]{:S(2)}, u32[]{:S(2)}) collective-permute-start(bf16[105,512]{1,0:T(8,128)(2,1)S(1)} %get-tuple-element.64), channel_id=1, source_target_pairs={{1,2},{2,1},{3,4},{4,3},{5,6},{6,5},{7,8},{8,7},{9,10},{10,9},{11,... | collective-permute-start | bytes 322568 | tf_op jit(solution)/shard_map/ppermute | solution.py:240
  42.2 1.9 %collective-permute-start.7 = (bf16[105,512]{1,0:T(8,128)(2,1)S(1)}, bf16[105,512]{1,0:T(8,128)(2,1)S(1)}, u32[]{:S(2)}, u32[]{:S(2)}) collective-permute-start(bf16[105,512]{1,0:T(8,128)(2,1)S(1)} %get-tuple-element.65), channel_id=1, source_target_pairs={{0,1},{1,0},{2,3},{3,2},{4,5},{5,4},{6,7},{7,6},{8,9},{9,8},{10,11... | collective-permute-start | bytes 322568 | tf_op jit(solution)/shard_map/ppermute | solution.py:240
  44.1 0.3 gather_row.3.own
  44.4 4.2 %collective-permute-done.6.far_in = bf16[105,512]{1,0:T(8,128)(2,1)S(1)} collective-permute-done((bf16[105,512]{1,0:T(8,128)(2,1)S(1)}, bf16[105,512]{1,0:T(8,128)(2,1)S(1)}, u32[]{:S(2)}, u32[]{:S(2)}) %collective-permute-start.6) | collective-permute-done | bytes 107552 | tf_op jit(solution)/shard_map/ppermute | solution.py:240
  48.6 1.6 %collective-permute-done.7.near_in = bf16[105,512]{1,0:T(8,128)(2,1)S(1)} collective-permute-done((bf16[105,512]{1,0:T(8,128)(2,1)S(1)}, bf16[105,512]{1,0:T(8,128)(2,1)S(1)}, u32[]{:S(2)}, u32[]{:S(2)}) %collective-permute-start.7) | collective-permute-done | bytes 107552 | tf_op jit(solution)/shard_map/ppermute | solution.py:240
  50.2 1.5 %filter_and_gram.1 = (bf16[343,512]{1,0:T(8,128)(2,1)}, bf16[2,512,256]{2,1,0:T(8,128)(2,1)S(1)}, bf16[2,512,256]{2,1,0:T(8,128)(2,1)S(1)}) custom-call(bf16[343,56]{1,0:T(8,128)(2,1)S(1)} %get-tuple-element.40.own_y, bf16[49,56]{1,0:T(8,128)(2,1)S(1)} %get-tuple-element.41.side_y, f32[343,512]{1,0:T(8,128)S(1)} %gather_row.3.own, ...), custom_call_target="tpu_custom_call" | custom-call | tf_op jit(solution)/shard_map/filter_and_gram/pallas_call | solution.py:64
  51.7 2.1 %collective-permute-start.8 = (bf16[2,512,256]{2,1,0:T(8,128)(2,1)S(1)}, bf16[2,512,256]{2,1,0:T(8,128)(2,1)S(1)}, u32[]{:S(2)}, u32[]{:S(2)}) collective-permute-start(bf16[2,512,256]{2,1,0:T(8,128)(2,1)S(1)} %get-tuple-element.70), channel_id=1, source_target_pairs={{0,16},{16,0},{1,17},{17,1},{2,18},{18,2},{3,19},{19,3},{4,20},{20... | collective-permute-start | bytes 1572872 | tf_op jit(solution)/shard_map/ppermute | solution.py:366
  53.8 1.7 %collective-permute-done.8.taken = bf16[2,512,256]{2,1,0:T(8,128)(2,1)S(1)} collective-permute-done((bf16[2,512,256]{2,1,0:T(8,128)(2,1)S(1)}, bf16[2,512,256]{2,1,0:T(8,128)(2,1)S(1)}, u32[]{:S(2)}, u32[]{:S(2)}) %collective-permute-start.8) | collective-permute-done | bytes 524320 | tf_op jit(solution)/shard_map/ppermute | solution.py:366
  55.5 0.1 pair_sum.1
  55.7 12.2 %all_to_all.15.terms = bf16[4,8,64,128]{3,2,1,0:T(8,128)(2,1)S(1)} all-to-all(bf16[4,8,64,128]{3,2,1,0:T(8,128)(2,1)S(1)} %pair_sum.1), channel_id=1, replica_groups=mesh['z'=16,'half'=2,'core'=2,'row'=4,'line'=4] {'row'}, dimensions={0} | all-to-all | bytes 1048576 | tf_op jit(solution)/shard_map/all_to_all | solution.py:406
  67.9 0.1 row_sum.1
  67.9 16.3 %all_to_all.16.terms = bf16[8,64,128]{2,1,0:T(8,128)(2,1)S(1)} all-to-all(bf16[8,64,128]{2,1,0:T(8,128)(2,1)S(1)} %row_sum.1), channel_id=1, replica_groups=mesh['z'=16,'half'=2,'core'=2,'row'=4,'line'=4] {'half','line'}, dimensions={0} | all-to-all | bytes 262144 | tf_op jit(solution)/shard_map/all_to_all | solution.py:408
  84.2 0.2 plane_sum.1
  84.4 32.9 %all_to_all.17.terms = bf16[16,4,128]{2,1,0:T(4,128)(2,1)S(1)} all-to-all(bf16[16,4,128]{2,1,0:T(4,128)(2,1)S(1)} %plane_sum.1), channel_id=1, replica_groups=mesh['z'=16,'half'=2,'core'=2,'row'=4,'line'=4] {'z'}, dimensions={0} | all-to-all | bytes 32768 | tf_op jit(solution)/shard_map/all_to_all | solution.py:410
  117.3 0.7 line_sum.1
  (5 shorter events, 0.0 us)
Async XLA Ops:
  2.4 10.7 %collective-permute-start = (bf16[105,512]{1,0:T(8,128)(2,1)S(1)}, bf16[105,512]{1,0:T(8,128)(2,1)S(1)}, u32[]{:S(2)}, u32[]{:S(2)}) collective-permute-start(bf16[105,512]{1,0:T(8,128)(2,1)S(1)} %get-tuple-element.49), channel_id=1, source_target_pairs={{16,32},{32,16},{48,64},{64,48},{80,96},{96,80},{112,128},{128,112... | collective-permute-start | bytes 322568 | tf_op jit(solution)/shard_map/ppermute | solution.py:240
  3.1 10.1 %collective-permute-start.1 = (bf16[105,512]{1,0:T(8,128)(2,1)S(1)}, bf16[105,512]{1,0:T(8,128)(2,1)S(1)}, u32[]{:S(2)}, u32[]{:S(2)}) collective-permute-start(bf16[105,512]{1,0:T(8,128)(2,1)S(1)} %get-tuple-element.50), channel_id=1, source_target_pairs={{0,16},{16,0},{32,48},{48,32},{64,80},{80,64},{96,112},{112,96},{1... | collective-permute-start | bytes 322568 | tf_op jit(solution)/shard_map/ppermute | solution.py:240
  13.4 5.2 %copy-start = (f32[343]{0:T(512)S(1)}, f32[343]{0:T(512)}, u32[]{:S(2)}) copy-start(f32[343]{0:T(512)} %param.4) | copy-start | bytes 4120
  13.4 10.3 %collective-permute-start.2 = (bf16[105,512]{1,0:T(8,128)(2,1)S(1)}, bf16[105,512]{1,0:T(8,128)(2,1)S(1)}, u32[]{:S(2)}, u32[]{:S(2)}) collective-permute-start(bf16[105,512]{1,0:T(8,128)(2,1)S(1)} %get-tuple-element.54), channel_id=1, source_target_pairs={{1,2},{2,1},{3,4},{4,3},{5,6},{6,5},{7,8},{8,7},{9,10},{10,9},{11,... | collective-permute-start | bytes 322568 | tf_op jit(solution)/shard_map/ppermute | solution.py:240
  16.2 10.2 %collective-permute-start.3 = (bf16[105,512]{1,0:T(8,128)(2,1)S(1)}, bf16[105,512]{1,0:T(8,128)(2,1)S(1)}, u32[]{:S(2)}, u32[]{:S(2)}) collective-permute-start(bf16[105,512]{1,0:T(8,128)(2,1)S(1)} %get-tuple-element.55), channel_id=1, source_target_pairs={{0,1},{1,0},{2,3},{3,2},{4,5},{5,4},{6,7},{7,6},{8,9},{9,8},{10,11... | collective-permute-start | bytes 322568 | tf_op jit(solution)/shard_map/ppermute | solution.py:240
  27.1 10.3 %collective-permute-start.4 = (bf16[105,512]{1,0:T(8,128)(2,1)S(1)}, bf16[105,512]{1,0:T(8,128)(2,1)S(1)}, u32[]{:S(2)}, u32[]{:S(2)}) collective-permute-start(bf16[105,512]{1,0:T(8,128)(2,1)S(1)} %get-tuple-element.59), channel_id=1, source_target_pairs={{16,32},{32,16},{48,64},{64,48},{80,96},{96,80},{112,128},{128,112... | collective-permute-start | bytes 322568 | tf_op jit(solution)/shard_map/ppermute | solution.py:240
  27.8 9.9 %collective-permute-start.5 = (bf16[105,512]{1,0:T(8,128)(2,1)S(1)}, bf16[105,512]{1,0:T(8,128)(2,1)S(1)}, u32[]{:S(2)}, u32[]{:S(2)}) collective-permute-start(bf16[105,512]{1,0:T(8,128)(2,1)S(1)} %get-tuple-element.60), channel_id=1, source_target_pairs={{0,16},{16,0},{32,48},{48,32},{64,80},{80,64},{96,112},{112,96},{1... | collective-permute-start | bytes 322568 | tf_op jit(solution)/shard_map/ppermute | solution.py:240
  38.0 10.6 %collective-permute-start.6 = (bf16[105,512]{1,0:T(8,128)(2,1)S(1)}, bf16[105,512]{1,0:T(8,128)(2,1)S(1)}, u32[]{:S(2)}, u32[]{:S(2)}) collective-permute-start(bf16[105,512]{1,0:T(8,128)(2,1)S(1)} %get-tuple-element.64), channel_id=1, source_target_pairs={{1,2},{2,1},{3,4},{4,3},{5,6},{6,5},{7,8},{8,7},{9,10},{10,9},{11,... | collective-permute-start | bytes 322568 | tf_op jit(solution)/shard_map/ppermute | solution.py:240
  42.2 8.0 %collective-permute-start.7 = (bf16[105,512]{1,0:T(8,128)(2,1)S(1)}, bf16[105,512]{1,0:T(8,128)(2,1)S(1)}, u32[]{:S(2)}, u32[]{:S(2)}) collective-permute-start(bf16[105,512]{1,0:T(8,128)(2,1)S(1)} %get-tuple-element.65), channel_id=1, source_target_pairs={{0,1},{1,0},{2,3},{3,2},{4,5},{5,4},{6,7},{7,6},{8,9},{9,8},{10,11... | collective-permute-start | bytes 322568 | tf_op jit(solution)/shard_map/ppermute | solution.py:240
  51.7 3.8 %collective-permute-start.8 = (bf16[2,512,256]{2,1,0:T(8,128)(2,1)S(1)}, bf16[2,512,256]{2,1,0:T(8,128)(2,1)S(1)}, u32[]{:S(2)}, u32[]{:S(2)}) collective-permute-start(bf16[2,512,256]{2,1,0:T(8,128)(2,1)S(1)} %get-tuple-element.70), channel_id=1, source_target_pairs={{0,16},{16,0},{1,17},{17,1},{2,18},{18,2},{3,19},{19,3},{4,20},{20... | collective-permute-start | bytes 1572872 | tf_op jit(solution)/shard_map/ppermute | solution.py:366

commit v10 on v8

--- a/solution.py
+++ b/solution.py
@@ -133,19 +133,22 @@
 
 
 def prepare(field_in, stiffness_in, field, stiffness, rim_own, far, near, wide, upward, downward, sems):
+    top = DEG * SIDE * SIDE
     copies = [
-        pltpu.make_async_copy(stiffness_in, stiffness, sems.at[0]),
+        pltpu.make_async_copy(stiffness_in.at[top:], stiffness.at[top:], sems.at[0]),
         pltpu.make_async_copy(field_in, field, sems.at[1]),
+        pltpu.make_async_copy(stiffness_in.at[:top], stiffness.at[:top], sems.at[2]),
     ]
     for copy in copies:
         copy.start()
     nodes = one_hot(node_order(0, OWN), SIDE**3)
-    rim = one_hot(node_order(OWN, RIM), SIDE**3)
+    rim = one_hot(node_order(OWN, RIM) - top, SIDE * SIDE)
     copies[0].wait()
-    rim_own[...] = dot_columns(dot(rim, stiffness[...]).astype(BF16), nodes).astype(BF16)
+    rim_own[...] = dot_columns(dot(rim, stiffness[top:, :]).astype(BF16), nodes).astype(BF16)
     copies[1].wait()
     wide[...] = field[...].astype(F32)
     pack_x(dot(rim_own[...], field[...]), wide, far, near, upward, downward)
+    copies[2].wait()
 
 
 def arrange(stiffness, field, own_columns, partial, own_x, rim_x, face_x, own_y, side_y, face_y, edge_y, ordered):
@@ -261,7 +264,7 @@
             ((RIM, OWN), BF16),
             message,
             message,
-            scratch=(*staged(OWN, message_rows, FACE), pltpu.SemaphoreType.DMA((2,))),
+            scratch=(*staged(OWN, message_rows, FACE), pltpu.SemaphoreType.DMA((3,))),
             raw=(0, 1),
         )(orbitals, cell_stiffness)
         far, near = swapped(far, near, gx, length_x)

time: 117 us -> 117 us (level)
  no operation moved by 1% of the time
where the time goes in v10:
time: 117 us; the launch traced here: 116 us
  blocking collectives  58.5 us (50%)
  starting transfers between devices  37.5 us (32%)
  waiting for transfers between devices  11.3 us (10%)
  Pallas kernels  7.38 us (6%)
    all_to_all x1, blocking collectives, per_device(): terms = lax.all_to_all(terms, 'z', 0, 0, tiled=True)  31.5 us
    all_to_all x1, blocking collectives, per_device(): terms = lax.all_to_all(terms, ('half', 'gy'), 0, 0, tiled=True)  27 us
    ppermute x4, starting transfers between devices, swapped(): lax.ppermute(near, axis, pairs(0))  18.1 us
    ppermute x4, starting transfers between devices, swapped(): lax.ppermute(far, axis, pairs(1))  17.3 us
    ppermute x4, waiting for transfers between devices, swapped(): lax.ppermute(near, axis, pairs(0))  9.22 us
    pallas_call x12, Pallas kernels, run(): pl.pallas_call(kernel, out_shape=[jax.ShapeDtypeStruct(*shape) if i in re...  7.38 us
  transfers between devices with their start and end apart: 9, of which 5 were waited for; matrix products, arithmetic and copies ran while one was open for 0% of the time, Pallas kernels for 2%

profile of v10, /device:TPU:1, one launch (start us, length us, event | category | flops | bytes accessed | tf_op | source)
XLA Modules:
  0.0 115.6 jit_solution(11270635335200102875)
XLA Ops:
  0.6 1.5 %prepare.1 = (bf16[343,512]{1,0:T(8,128)(2,1)S(1)}, bf16[512,512]{1,0:T(8,128)(2,1)S(1)}, bf16[56,343]{1,0:T(8,128)(2,1)S(1)}, bf16[105,512]{1,0:T(8,128)(2,1)S(1)}, bf16[105,512]{1,0:T(8,128)(2,1)S(1)}) custom-call(bf16[343,512]{1,0:T(8,128)(2,1)} %field_in.1, bf16[512,512]{1,0:T(8,128)(2,1)} %stiffness_in.1), custom_call_target="tpu_custom_call" | custom-call | tf_op jit(solution)/shard_map/prepare/pallas_call | solution.py:64
  2.1 8.8 %collective-permute-start = (bf16[105,512]{1,0:T(8,128)(2,1)S(1)}, bf16[105,512]{1,0:T(8,128)(2,1)S(1)}, u32[]{:S(2)}, u32[]{:S(2)}) collective-permute-start(bf16[105,512]{1,0:T(8,128)(2,1)S(1)} %get-tuple-element.49), channel_id=1, source_target_pairs={{16,32},{32,16},{48,64},{64,48},{80,96},{96,80},{112,128},{128,112... | collective-permute-start | bytes 322568 | tf_op jit(solution)/shard_map/ppermute | solution.py:239
  11.0 7.9 %collective-permute-start.1 = (bf16[105,512]{1,0:T(8,128)(2,1)S(1)}, bf16[105,512]{1,0:T(8,128)(2,1)S(1)}, u32[]{:S(2)}, u32[]{:S(2)}) collective-permute-start(bf16[105,512]{1,0:T(8,128)(2,1)S(1)} %get-tuple-element.50), channel_id=1, source_target_pairs={{0,16},{16,0},{32,48},{48,32},{64,80},{80,64},{96,112},{112,96},{1... | collective-permute-start | bytes 322568 | tf_op jit(solution)/shard_map/ppermute | solution.py:239
  18.8 1.0 arrange.1
  19.8 0.0 collective-permute-done.far_in
  19.8 0.3 cross.2
  20.1 0.0 copy-start
  20.1 0.7 collective-permute-start.2
  20.8 1.9 %collective-permute-start.3 = (bf16[105,512]{1,0:T(8,128)(2,1)S(1)}, bf16[105,512]{1,0:T(8,128)(2,1)S(1)}, u32[]{:S(2)}, u32[]{:S(2)}) collective-permute-start(bf16[105,512]{1,0:T(8,128)(2,1)S(1)} %get-tuple-element.55), channel_id=1, source_target_pairs={{0,1},{1,0},{2,3},{3,2},{4,5},{5,4},{6,7},{7,6},{8,9},{9,8},{10,11... | collective-permute-start | bytes 322568 | tf_op jit(solution)/shard_map/ppermute | solution.py:239
  22.7 0.1 broadcast_in_dim.4.potential
  22.8 0.3 gather_row.2.own
  23.1 0.0 collective-permute-done.2.far_in
  23.1 4.0 %collective-permute-done.3.near_in = bf16[105,512]{1,0:T(8,128)(2,1)S(1)} collective-permute-done((bf16[105,512]{1,0:T(8,128)(2,1)S(1)}, bf16[105,512]{1,0:T(8,128)(2,1)S(1)}, u32[]{:S(2)}, u32[]{:S(2)}) %collective-permute-start.3) | collective-permute-done | bytes 107552 | tf_op jit(solution)/shard_map/ppermute | solution.py:239
  27.1 0.7 lift.1
  27.7 7.1 %collective-permute-start.4 = (bf16[105,512]{1,0:T(8,128)(2,1)S(1)}, bf16[105,512]{1,0:T(8,128)(2,1)S(1)}, u32[]{:S(2)}, u32[]{:S(2)}) collective-permute-start(bf16[105,512]{1,0:T(8,128)(2,1)S(1)} %get-tuple-element.59), channel_id=1, source_target_pairs={{16,32},{32,16},{48,64},{64,48},{80,96},{96,80},{112,128},{128,112... | collective-permute-start | bytes 322568 | tf_op jit(solution)/shard_map/ppermute | solution.py:239
  34.9 1.9 %collective-permute-start.5 = (bf16[105,512]{1,0:T(8,128)(2,1)S(1)}, bf16[105,512]{1,0:T(8,128)(2,1)S(1)}, u32[]{:S(2)}, u32[]{:S(2)}) collective-permute-start(bf16[105,512]{1,0:T(8,128)(2,1)S(1)} %get-tuple-element.60), channel_id=1, source_target_pairs={{0,16},{16,0},{32,48},{48,32},{64,80},{80,64},{96,112},{112,96},{1... | collective-permute-start | bytes 322568 | tf_op jit(solution)/shard_map/ppermute | solution.py:239
  36.8 0.7 shuffled_product.1
  37.5 0.4 collective-permute-done.4.far_in
  37.9 0.2 collective-permute-done.5.near_in
  38.1 0.2 cross.3
  38.4 0.7 collective-permute-start.6
  39.0 6.4 %collective-permute-start.7 = (bf16[105,512]{1,0:T(8,128)(2,1)S(1)}, bf16[105,512]{1,0:T(8,128)(2,1)S(1)}, u32[]{:S(2)}, u32[]{:S(2)}) collective-permute-start(bf16[105,512]{1,0:T(8,128)(2,1)S(1)} %get-tuple-element.65), channel_id=1, source_target_pairs={{0,1},{1,0},{2,3},{3,2},{4,5},{5,4},{6,7},{7,6},{8,9},{9,8},{10,11... | collective-permute-start | bytes 322568 | tf_op jit(solution)/shard_map/ppermute | solution.py:239
  45.4 0.3 gather_row.3.own
  45.7 5.0 %collective-permute-done.7.near_in = bf16[105,512]{1,0:T(8,128)(2,1)S(1)} collective-permute-done((bf16[105,512]{1,0:T(8,128)(2,1)S(1)}, bf16[105,512]{1,0:T(8,128)(2,1)S(1)}, u32[]{:S(2)}, u32[]{:S(2)}) %collective-permute-start.7) | collective-permute-done | bytes 107552 | tf_op jit(solution)/shard_map/ppermute | solution.py:239
  50.7 1.5 %filter_and_gram.1 = (bf16[343,512]{1,0:T(8,128)(2,1)}, bf16[2,512,256]{2,1,0:T(8,128)(2,1)S(1)}, bf16[2,512,256]{2,1,0:T(8,128)(2,1)S(1)}) custom-call(bf16[343,56]{1,0:T(8,128)(2,1)S(1)} %get-tuple-element.40.own_y, bf16[49,56]{1,0:T(8,128)(2,1)S(1)} %get-tuple-element.41.side_y, f32[343,512]{1,0:T(8,128)S(1)} %gather_row.3.own, ...), custom_call_target="tpu_custom_call" | custom-call | tf_op jit(solution)/shard_map/filter_and_gram/pallas_call | solution.py:64
  52.2 2.1 %collective-permute-start.8 = (bf16[2,512,256]{2,1,0:T(8,128)(2,1)S(1)}, bf16[2,512,256]{2,1,0:T(8,128)(2,1)S(1)}, u32[]{:S(2)}, u32[]{:S(2)}) collective-permute-start(bf16[2,512,256]{2,1,0:T(8,128)(2,1)S(1)} %get-tuple-element.70), channel_id=1, source_target_pairs={{0,16},{16,0},{1,17},{17,1},{2,18},{18,2},{3,19},{19,3},{4,20},{20... | collective-permute-start | bytes 1572872 | tf_op jit(solution)/shard_map/ppermute | solution.py:365
  54.3 1.7 %collective-permute-done.8.taken = bf16[2,512,256]{2,1,0:T(8,128)(2,1)S(1)} collective-permute-done((bf16[2,512,256]{2,1,0:T(8,128)(2,1)S(1)}, bf16[2,512,256]{2,1,0:T(8,128)(2,1)S(1)}, u32[]{:S(2)}, u32[]{:S(2)}) %collective-permute-start.8) | collective-permute-done | bytes 524320 | tf_op jit(solution)/shard_map/ppermute | solution.py:365
  56.1 0.1 pair_sum.1
  56.2 27.0 %all_to_all.10.terms = bf16[32,64,128]{2,1,0:T(8,128)(2,1)S(1)} all-to-all(bf16[32,64,128]{2,1,0:T(8,128)(2,1)S(1)} %bitcast.1), channel_id=1, replica_groups=mesh['z'=16,'half'=2,'core'=2,'gy'=16] {'half','gy'}, dimensions={0} | all-to-all | bytes 1048576 | tf_op jit(solution)/shard_map/all_to_all | solution.py:400
  83.2 0.2 plane_sum.1
  83.4 31.5 %all_to_all.11.terms = bf16[16,4,128]{2,1,0:T(4,128)(2,1)S(1)} all-to-all(bf16[16,4,128]{2,1,0:T(4,128)(2,1)S(1)} %plane_sum.1), channel_id=1, replica_groups=mesh['z'=16,'half'=2,'core'=2,'gy'=16] {'z'}, dimensions={0} | all-to-all | bytes 32768 | tf_op jit(solution)/shard_map/all_to_all | solution.py:402
  114.9 0.7 line_sum.1
  (3 shorter events, 0.0 us)
Async XLA Ops:
  2.1 17.7 %collective-permute-start = (bf16[105,512]{1,0:T(8,128)(2,1)S(1)}, bf16[105,512]{1,0:T(8,128)(2,1)S(1)}, u32[]{:S(2)}, u32[]{:S(2)}) collective-permute-start(bf16[105,512]{1,0:T(8,128)(2,1)S(1)} %get-tuple-element.49), channel_id=1, source_target_pairs={{16,32},{32,16},{48,64},{64,48},{80,96},{96,80},{112,128},{128,112... | collective-permute-start | bytes 322568 | tf_op jit(solution)/shard_map/ppermute | solution.py:239
  11.0 8.8 %collective-permute-start.1 = (bf16[105,512]{1,0:T(8,128)(2,1)S(1)}, bf16[105,512]{1,0:T(8,128)(2,1)S(1)}, u32[]{:S(2)}, u32[]{:S(2)}) collective-permute-start(bf16[105,512]{1,0:T(8,128)(2,1)S(1)} %get-tuple-element.50), channel_id=1, source_target_pairs={{0,16},{16,0},{32,48},{48,32},{64,80},{80,64},{96,112},{112,96},{1... | collective-permute-start | bytes 322568 | tf_op jit(solution)/shard_map/ppermute | solution.py:239
  20.1 2.6 %copy-start = (f32[343]{0:T(512)S(1)}, f32[343]{0:T(512)}, u32[]{:S(2)}) copy-start(f32[343]{0:T(512)} %param.4) | copy-start | bytes 4120
  20.1 3.0 %collective-permute-start.2 = (bf16[105,512]{1,0:T(8,128)(2,1)S(1)}, bf16[105,512]{1,0:T(8,128)(2,1)S(1)}, u32[]{:S(2)}, u32[]{:S(2)}) collective-permute-start(bf16[105,512]{1,0:T(8,128)(2,1)S(1)} %get-tuple-element.54), channel_id=1, source_target_pairs={{1,2},{2,1},{3,4},{4,3},{5,6},{6,5},{7,8},{8,7},{9,10},{10,9},{11,... | collective-permute-start | bytes 322568 | tf_op jit(solution)/shard_map/ppermute | solution.py:239
  20.8 6.3 %collective-permute-start.3 = (bf16[105,512]{1,0:T(8,128)(2,1)S(1)}, bf16[105,512]{1,0:T(8,128)(2,1)S(1)}, u32[]{:S(2)}, u32[]{:S(2)}) collective-permute-start(bf16[105,512]{1,0:T(8,128)(2,1)S(1)} %get-tuple-element.55), channel_id=1, source_target_pairs={{0,1},{1,0},{2,3},{3,2},{4,5},{5,4},{6,7},{7,6},{8,9},{9,8},{10,11... | collective-permute-start | bytes 322568 | tf_op jit(solution)/shard_map/ppermute | solution.py:239
  27.7 10.1 %collective-permute-start.4 = (bf16[105,512]{1,0:T(8,128)(2,1)S(1)}, bf16[105,512]{1,0:T(8,128)(2,1)S(1)}, u32[]{:S(2)}, u32[]{:S(2)}) collective-permute-start(bf16[105,512]{1,0:T(8,128)(2,1)S(1)} %get-tuple-element.59), channel_id=1, source_target_pairs={{16,32},{32,16},{48,64},{64,48},{80,96},{96,80},{112,128},{128,112... | collective-permute-start | bytes 322568 | tf_op jit(solution)/shard_map/ppermute | solution.py:239
  34.9 3.2 %collective-permute-start.5 = (bf16[105,512]{1,0:T(8,128)(2,1)S(1)}, bf16[105,512]{1,0:T(8,128)(2,1)S(1)}, u32[]{:S(2)}, u32[]{:S(2)}) collective-permute-start(bf16[105,512]{1,0:T(8,128)(2,1)S(1)} %get-tuple-element.60), channel_id=1, source_target_pairs={{0,16},{16,0},{32,48},{48,32},{64,80},{80,64},{96,112},{112,96},{1... | collective-permute-start | bytes 322568 | tf_op jit(solution)/shard_map/ppermute | solution.py:239
  38.4 7.4 %collective-permute-start.6 = (bf16[105,512]{1,0:T(8,128)(2,1)S(1)}, bf16[105,512]{1,0:T(8,128)(2,1)S(1)}, u32[]{:S(2)}, u32[]{:S(2)}) collective-permute-start(bf16[105,512]{1,0:T(8,128)(2,1)S(1)} %get-tuple-element.64), channel_id=1, source_target_pairs={{1,2},{2,1},{3,4},{4,3},{5,6},{6,5},{7,8},{8,7},{9,10},{10,9},{11,... | collective-permute-start | bytes 322568 | tf_op jit(solution)/shard_map/ppermute | solution.py:239
  39.0 11.7 %collective-permute-start.7 = (bf16[105,512]{1,0:T(8,128)(2,1)S(1)}, bf16[105,512]{1,0:T(8,128)(2,1)S(1)}, u32[]{:S(2)}, u32[]{:S(2)}) collective-permute-start(bf16[105,512]{1,0:T(8,128)(2,1)S(1)} %get-tuple-element.65), channel_id=1, source_target_pairs={{0,1},{1,0},{2,3},{3,2},{4,5},{5,4},{6,7},{7,6},{8,9},{9,8},{10,11... | collective-permute-start | bytes 322568 | tf_op jit(solution)/shard_map/ppermute | solution.py:239
  52.2 3.8 %collective-permute-start.8 = (bf16[2,512,256]{2,1,0:T(8,128)(2,1)S(1)}, bf16[2,512,256]{2,1,0:T(8,128)(2,1)S(1)}, u32[]{:S(2)}, u32[]{:S(2)}) collective-permute-start(bf16[2,512,256]{2,1,0:T(8,128)(2,1)S(1)} %get-tuple-element.70), channel_id=1, source_target_pairs={{0,16},{16,0},{1,17},{17,1},{2,18},{18,2},{3,19},{19,3},{4,20},{20... | collective-permute-start | bytes 1572872 | tf_op jit(solution)/shard_map/ppermute | solution.py:365
